TPU v7x, 256 devices: a whole 4x4x8 slice. The times are simulated.
256 devices in a mesh: dp: 2 (over core), order: 16 (over z_lo, y), ens: 8 (over z_hi, x).
Axes of the slice: x: 4, y: 4, z: 8 (z_hi: 2, z_lo: 4; z = z_hi * 4 + z_lo), core: 2. Of those that a mesh axis runs over, the one named last changes fastest.
Arguments:
- fourier: bfloat16 [2, 16, 320, 40960], P('dp', 'ens', 'order'), may hold values from -20 to 20
- analysis: bfloat16 [320, 320, 320], P(None, 'order'), may hold values from -0.3125 to 0.3125
- target: bfloat16 [2, 320, 40960], P('dp', 'ens', 'order'), may hold values from -6 to 6
- band_ids: int32 [320, 320], P('ens', 'order'), may hold values from 0 to 15, as said below
- partners: int32 [16, 4], replicated, may hold values from 0 to 15, as said below
- band_cotangent: float32 [2, 16], replicated, may hold values from 0.5 to 4
Outputs:
- grad_fourier: bfloat16 [2, 16, 320, 40960], P('dp', 'ens', 'order')
- grad_analysis: float32 [320, 320, 320], P(('dp', 'ens'), 'order')
- loss_bands: float32 [16], replicated
Inputs may be any that keep to these rules, and one draw needn't show every extreme that they name: band_ids[l,m] depends on l only, never falls as l grows, starts at 0 and takes every band from 0 to 15. `partners`: each row names 4 different members, none equal to the row's own member.
All inputs are finite; a program needn't handle non-finite values.
Results may differ from a plain program's by a relative error of at most 0.0085.
Values may be sent and summed in bfloat16 or wider, within the bound.
No kernel may reach another device: no remote copies, remote signals or barrier semaphores. Data moves between devices by JAX's collectives and lax.ppermute only.
A program may use at most 128 MiB of HBM per device.

v0:
```python
import jax
import jax.numpy as jnp
from jax import lax
from jax.sharding import Mesh
from jax.sharding import PartitionSpec as P

MEMBERS = 16
NLAT = 320
L = 320
C = 64
NBANDS = 16
PARTNERS = 4
ORDER = ("order_0", "order_1")
ENS = ("ens_0", "ens_1")
DP_ENS = ("dp", "ens_0", "ens_1")


HIGHEST = lax.Precision.HIGHEST
EPSILON = 1e-06
WEIGHT_RATIO = 1.0 / 64.0


def from_everyone(shard, axis):
    copies = jnp.broadcast_to(shard, (lax.axis_size(axis), *shard.shape))
    return lax.all_to_all(copies, axis, split_axis=0, concat_axis=0, tiled=True)


def of_everyone(shard, axis):
    everything = from_everyone(shard, axis)
    return jnp.sum(everything, axis=0)


def by_axis(shard, axes):
    far, near = axes
    return of_everyone(of_everyone(shard, near), far)


def over_pieces(shard, axis):
    pieces = lax.all_gather(shard, axis)
    return pieces.sum(axis=0)


def band_terms(grams, partners, cotangent):
    diagonal_part = jnp.diagonal(grams, axis1=2, axis2=3)
    squared = diagonal_part[..., :, None] + diagonal_part[..., None, :] - 2.0 * grams
    distance = jnp.sqrt(squared + EPSILON)
    member_ids = jnp.arange(MEMBERS, dtype=jnp.int32)
    counts = jnp.sum(
        (partners[:, :, None] == member_ids[None, None, :]).astype(jnp.float32), axis=1
    )
    obs_dist = distance[:, :, :MEMBERS, MEMBERS]
    pair_dist = distance[:, :, :MEMBERS, :MEMBERS]
    scores = jnp.mean(obs_dist, axis=-1) - jnp.sum(counts * pair_dist, axis=(-2, -1)) / (
        2.0 * MEMBERS * PARTNERS
    )
    scaled = cotangent * (16.0 * MEMBERS * NLAT)
    symmetric = counts + counts.T
    obs_weight = scaled[..., None] / (MEMBERS * obs_dist)
    pair_weight = scaled[..., None, None] * symmetric / (2.0 * MEMBERS * PARTNERS * pair_dist)
    identity = jnp.eye(MEMBERS, dtype=jnp.float32)
    member_part = pair_weight + identity * (obs_weight - jnp.sum(pair_weight, axis=-1))[..., None]
    mixing = jnp.concatenate([member_part, -obs_weight[..., None]], axis=-1)
    return (scores, mixing)


def body(fourier, analysis, target, band_ids, partners, band_cotangent):
    samples = fourier.shape[0]
    own_members = fourier.shape[1]
    orders = analysis.shape[1]
    width = 2 * C
    degrees_here = band_ids.shape[0]
    order_start = lax.axis_index(ORDER) * orders
    degree_start = lax.axis_index(ENS) * degrees_here
    order_index = order_start + jnp.arange(orders, dtype=jnp.int32)
    all_degrees = jnp.arange(L, dtype=jnp.int32)
    keep_all = all_degrees[:, None] >= order_index[None, :]
    local_degrees = degree_start + jnp.arange(degrees_here, dtype=jnp.int32)
    keep_here = local_degrees[:, None] >= order_index[None, :]
    rows = lax.all_to_all(fourier, ORDER, split_axis=3, concat_axis=2, tiled=True)
    items = rows.shape[1]
    grid = rows.reshape(samples, items, NLAT, orders, width)
    spec = jnp.einsum("bitmq,tml->bilmq", grid, analysis, preferred_element_type=jnp.float32)
    spec = jnp.where(keep_all[None, None, :, :, None], spec, 0.0).astype(jnp.bfloat16)
    grid_rows = rows
    spectra = spec.reshape(samples, items, L, orders * width)
    gathered = lax.all_to_all(spectra, ENS, split_axis=2, concat_axis=1, tiled=True)
    predicted = gathered.reshape(samples, MEMBERS, degrees_here, orders, width)
    observed = target.reshape(samples, degrees_here, orders, width)
    observed = jnp.where(keep_here[None, :, :, None], observed, jnp.zeros((), jnp.bfloat16))
    stacked = jnp.concatenate([predicted, observed[:, None]], axis=1)
    pair_terms = jnp.einsum(
        "bilmq,bjlmq->bijlm", stacked, stacked, preferred_element_type=jnp.float32
    )
    band_range = jnp.arange(NBANDS, dtype=jnp.int32)
    one_hot = (band_ids[:, :, None] == band_range[None, None, :]).astype(jnp.float32)
    grams = jnp.einsum("bijlm,lmk->bkij", pair_terms, one_hot, precision=HIGHEST)
    sample_start = lax.axis_index("dp") * samples
    grams = by_axis(grams, (("order_0", "order_1"), ("ens_0", "ens_1")))
    cotangent = lax.dynamic_slice_in_dim(band_cotangent, sample_start, samples, 0)
    scores, mixing = band_terms(grams, partners, cotangent)
    loss_bands = over_pieces(jnp.sum(cotangent * scores, axis=0), "dp")
    spread = jnp.einsum("lmk,bkij->blmij", one_hot, mixing, precision=HIGHEST)
    grad_spec = jnp.einsum(
        "blmij,bjlmq->bilmq", spread, stacked.astype(jnp.float32), precision=HIGHEST
    ).astype(jnp.bfloat16)
    grad_spec = grad_spec.reshape(samples, MEMBERS, degrees_here, orders * width)
    returned = lax.all_to_all(grad_spec, ENS, split_axis=1, concat_axis=2, tiled=True)
    back = returned.reshape(samples, own_members, L, orders, width)
    grid_own = grid_rows.reshape(samples, own_members, NLAT, orders, width)
    rows = grid_own
    grad_analysis = lax.psum_scatter(
        (
            jnp.einsum("bitmq,bilmq->tml", rows, back, preferred_element_type=jnp.float32)
            * WEIGHT_RATIO
        ).astype(jnp.bfloat16),
        DP_ENS,
        scatter_dimension=0,
        tiled=True,
    ).astype(jnp.float32)
    grid_grad = jnp.einsum(
        "bilmq,tml->bitmq", back, analysis, preferred_element_type=jnp.float32
    ).astype(jnp.bfloat16)
    grid_grad = grid_grad.reshape(samples, own_members, NLAT, orders * width)
    grad_fourier = lax.all_to_all(grid_grad, ORDER, split_axis=2, concat_axis=3, tiled=True)
    return (grad_fourier, grad_analysis, loss_bands)


def solution(mesh):
    torus = Mesh(
        mesh.devices.reshape(mesh.shape["dp"], 4, 4, 2, 4),
        ("dp", "order_0", "order_1", "ens_0", "ens_1"),
    )
    in_specs = (
        P("dp", ENS, ORDER, None),
        P(None, ORDER, None),
        P("dp", ENS, ORDER),
        P(ENS, ORDER),
        P(),
        P(),
    )
    out_specs = (P("dp", ENS, ORDER, None), P(DP_ENS, ORDER, None), P())
    return jax.shard_map(body, mesh=torus, in_specs=in_specs, out_specs=out_specs, check_vma=False)
```

profile of v0, /device:TPU:8, one launch (start us, length us, event | category | flops | bytes accessed | tf_op | source)
XLA Modules:
  0.0 748.4 jit_solution(11657523032341324510)
XLA Ops:
  7.2 39.3 %copy.184 = bf16[1,2,20,40960]{2,1,0,3:T(2,128)(2,1)} copy(bf16[1,2,20,40960]{3,1,2,0:T(2,128)(2,1)} %param.6) | data formatting | bytes 6553600 | tf_op args[0]
  46.4 44.7 %reshape.299 = bf16[16,2,51200]{2,1,0:T(2,128)(2,1)} reshape(bf16[40960,1,2,20]{3,2,1,0:T(2,128)(2,1)} %bitcast.135) | data formatting | bytes 6553600
  91.1 9.6 %all-to-all-start = ((bf16[16,2,51200]{2,1,0:T(2,128)(2,1)}), bf16[16,2,51200]{2,1,0:T(2,128)(2,1)S(1)}, u32[]{:S(2)}, u32[]{:S(2)}) async-start(bf16[16,2,51200]{2,1,0:T(2,128)(2,1)} %reshape.299), calls=%async_computation | async-start | bytes 6553600 | tf_op jit(solution)/shard_map/all_to_all | solution.py:79
  100.8 62.2 %all-to-all-done = bf16[16,2,51200]{2,1,0:T(2,128)(2,1)S(1)} async-done(((bf16[16,2,51200]{2,1,0:T(2,128)(2,1)}), bf16[16,2,51200]{2,1,0:T(2,128)(2,1)S(1)}, u32[]{:S(2)}, u32[]{:S(2)}) %all-to-all-start) | async-done | bytes 3276832 | tf_op jit(solution)/shard_map/all_to_all | solution.py:79
  163.0 54.7 %reshape.300 = bf16[40960,1,2,20]{3,2,1,0:T(2,128)(2,1)} reshape(bf16[16,2,51200]{2,1,0:T(2,128)(2,1)S(1)} %all-to-all-done) | data formatting | bytes 6553600
  217.8 40.4 %copy.185 = bf16[1,2,20,16,2560]{4,1,2,3,0:T(2,128)(2,1)S(1)} copy(bf16[1,2,20,16,2560]{2,1,4,3,0:T(2,128)(2,1)} %bitcast.134) | data formatting | bytes 6553600 | tf_op jit(solution)/shard_map/all_to_all | solution.py:79
  258.2 4.0 reshape.265
  262.2 6.4 fusion.1
  268.5 4.1 copy.221
  272.6 7.9 %reshape.296 = bf16[1,2,320,2560]{3,1,0,2:T(2,128)(2,1)} reshape(bf16[1,2,320,20,128]{4,3,1,2,0:T(8,128)(2,1)} %copy.221) | data formatting | bytes 6553600 | tf_op jit(solution)/shard_map/reshape | solution.py:85
  280.5 8.5 %all-to-all-start.1 = ((bf16[1,2,320,2560]{3,1,0,2:T(2,128)(2,1)}), bf16[1,2,320,2560]{3,1,0,2:T(2,128)(2,1)S(1)}, u32[]{:S(2)}, u32[]{:S(2)}) async-start(bf16[1,2,320,2560]{3,1,0,2:T(2,128)(2,1)} %reshape.296), calls=%async_computation.1 | async-start | bytes 6553600 | tf_op jit(solution)/shard_map/all_to_all | solution.py:86
  290.0 4.1 broadcast_select_fusion
  294.1 69.4 %all-to-all-done.1 = bf16[1,2,320,2560]{3,1,0,2:T(2,128)(2,1)S(1)} async-done(((bf16[1,2,320,2560]{3,1,0,2:T(2,128)(2,1)}), bf16[1,2,320,2560]{3,1,0,2:T(2,128)(2,1)S(1)}, u32[]{:S(2)}, u32[]{:S(2)}) %all-to-all-start.1) | async-done | bytes 3276832 | tf_op jit(solution)/shard_map/all_to_all | solution.py:86
  365.2 2.3 copy.244
  367.5 3.9 reshape.267
  371.4 6.0 copy.192
  377.4 5.2 fusion.9
  382.6 10.0 %copy.195 = f32[17,17,40,20]{2,1,3,0:T(8,128)} copy(f32[17,17,40,20]{0,1,3,2:T(8,128)} %fusion.9) | data formatting | bytes 1849600 | tf_op jit(solution)/shard_map/reshape.22
  392.7 7.2 convolution_bitcast_fusion.1
  401.0 2.7 reshape.301
  403.7 3.4 all-to-all-start.2
  407.2 10.6 %all-to-all-done.2 = f32[8,1,4624]{2,1,0:T(1,128)S(1)} async-done(((f32[8,1,4624]{2,1,0:T(1,128)}), f32[8,1,4624]{2,1,0:T(1,128)S(1)}, u32[]{:S(2)}, u32[]{:S(2)}) %all-to-all-start.2) | async-done | bytes 148000 | tf_op jit(solution)/shard_map/all_to_all | solution.py:25
  419.9 2.4 reshape.302
  425.2 3.8 reshape.303
  428.9 19.0 %all-to-all-start.3 = ((f32[16,1,4624]{2,1,0:T(1,128)}), f32[16,1,4624]{2,1,0:T(1,128)}, u32[]{:S(2)}, u32[]{:S(2)}) async-start(f32[16,1,4624]{2,1,0:T(1,128)} %reshape.303), calls=%async_computation.3 | async-start | bytes 606208 | tf_op jit(solution)/shard_map/all_to_all | solution.py:25
  450.4 6.5 all-to-all-done.3
  456.9 3.0 reduce.8
  459.9 3.5 reshape.304
  463.4 1.8 bitcast_reduce_fusion
  466.3 1.8 gather_fusion
  471.0 4.4 convolution_bitcast_fusion
  475.4 6.5 copy.202
  482.0 7.0 convert_bitcast_fusion.1
  489.0 2.9 copy.203
  491.9 5.3 reshape.273
  497.2 75.6 %all_to_all.73 = bf16[1,16,40,2560]{3,2,0,1:T(8,128)(2,1)S(1)} all-to-all(bf16[1,16,40,2560]{3,2,0,1:T(8,128)(2,1)S(1)} %bitcast.137), channel_id=1, replica_groups=mesh['dp'=2,'order_0'=4,'order_1'=4,'ens_0'=2,'ens_1'=4] {'ens_0','ens_1'}, dimensions={1} | all-to-all | bytes 6553600 | tf_op jit(solution)/shard_map/all_to_all | solution.py:107
  573.1 3.9 reshape.274
  576.9 5.5 convert_bitcast_fusion
  582.4 4.1 copy.224
  586.5 7.9 %reshape.298 = bf16[1,2,320,2560]{3,1,0,2:T(2,128)(2,1)} reshape(bf16[1,2,320,20,128]{4,3,1,2,0:T(8,128)(2,1)} %copy.224) | data formatting | bytes 6553600 | tf_op jit(solution)/shard_map/reshape | solution.py:123
  594.4 7.1 all-to-all-start.5
  601.5 7.6 %fusion.2 = bf16[320,20,320]{0,2,1:T(8,128)(2,1)} fusion(bf16[2,320,20,128]{3,2,1,0:T(8,128)(2,1)} %reshape.274, bf16[2,320,20,128]{3,2,0,1:T(8,128)(2,1)} %reshape.265), kind=kOutput, calls=%fused_computation.5 | convolution fusion | flops 1052672000 | bytes 10649600 | tf_op jit(solution)/shard_map/bitmq,bilmq->tml/dot_general | solution.py:113
  609.1 9.3 %copy.212 = bf16[320,20,320]{2,1,0:T(8,128)(2,1)} copy(bf16[320,20,320]{0,2,1:T(8,128)(2,1)} %fusion.2) | data formatting | bytes 8192000 | tf_op jit(solution)/shard_map/convert_element_type | solution.py:115
  619.1 1.8 all-gather
  621.4 59.1 %all-to-all-done.5 = bf16[1,2,320,2560]{3,1,0,2:T(2,128)(2,1)S(1)} async-done(((bf16[1,2,320,2560]{3,1,0,2:T(2,128)(2,1)}), bf16[1,2,320,2560]{3,1,0,2:T(2,128)(2,1)S(1)}, u32[]{:S(2)}, u32[]{:S(2)}) %all-to-all-start.5) | async-done | bytes 3276832 | tf_op jit(solution)/shard_map/all_to_all | solution.py:124
  680.5 5.0 copy.228
  685.5 53.7 %reduce-scatter.2.cloned.1.call-done = bf16[20,20,320]{2,1,0:T(8,128)(2,1)} async-done(((bf16[320,20,320]{2,1,0:T(8,128)(2,1)}), bf16[20,20,320]{2,1,0:T(8,128)(2,1)}) %reduce-scatter.2.cloned.1.call-update) | async-done | bytes 256016 | tf_op jit(solution)/shard_map/reduce_scatter | solution.py:111
  739.1 1.9 convert_element_type.57
  (47 shorter events, 16.8 us)
Async XLA Ops:
  91.1 71.9 %all-to-all-start = ((bf16[16,2,51200]{2,1,0:T(2,128)(2,1)}), bf16[16,2,51200]{2,1,0:T(2,128)(2,1)S(1)}, u32[]{:S(2)}, u32[]{:S(2)}) async-start(bf16[16,2,51200]{2,1,0:T(2,128)(2,1)} %reshape.299), calls=%async_computation | async-start | bytes 6553600 | tf_op jit(solution)/shard_map/all_to_all | solution.py:79
  280.5 8.5 %copy-start.2 = (bf16[1,40,2560]{2,1,0:T(8,128)(2,1)S(1)}, bf16[1,40,2560]{2,1,0:T(8,128)(2,1)}, u32[]{:S(2)}) copy-start(bf16[1,40,2560]{2,1,0:T(8,128)(2,1)} %param.8) | copy-start | bytes 614404
  280.5 83.0 %all-to-all-start.1 = ((bf16[1,2,320,2560]{3,1,0,2:T(2,128)(2,1)}), bf16[1,2,320,2560]{3,1,0,2:T(2,128)(2,1)S(1)}, u32[]{:S(2)}, u32[]{:S(2)}) async-start(bf16[1,2,320,2560]{3,1,0,2:T(2,128)(2,1)} %reshape.296), calls=%async_computation.1 | async-start | bytes 6553600 | tf_op jit(solution)/shard_map/all_to_all | solution.py:86
  363.5 1.7 copy-start
  371.4 6.0 copy-start.1
  382.6 10.0 %copy-start.4 = (s32[40,20]{0,1:T(8,128)S(1)}, s32[40,20]{0,1:T(8,128)}, u32[]{:S(2)}) copy-start(s32[40,20]{0,1:T(8,128)} %param.9) | copy-start | bytes 9604
  392.7 14.4 %copy-start.5 = (s32[16,4]{0,1:T(4,128)S(1)}, s32[16,4]{0,1:T(4,128)}, u32[]{:S(2)}) copy-start(s32[16,4]{0,1:T(4,128)} %param.10) | copy-start | bytes 772
  403.7 14.1 %all-to-all-start.2 = ((f32[8,1,4624]{2,1,0:T(1,128)}), f32[8,1,4624]{2,1,0:T(1,128)S(1)}, u32[]{:S(2)}, u32[]{:S(2)}) async-start(f32[8,1,4624]{2,1,0:T(1,128)} %reshape.301), calls=%async_computation.2 | async-start | bytes 303104 | tf_op jit(solution)/shard_map/all_to_all | solution.py:25
  407.2 40.8 %copy-start.3 = (f32[16,16]{0,1:T(8,128)}, f32[16,16]{0,1:T(8,128)S(1)}, u32[]{:S(2)}) copy-start(f32[16,16]{0,1:T(8,128)S(1)} %copy.193) | copy-start | bytes 3076
  419.9 29.3 %copy-start.6 = (f32[2,16]{1,0:T(2,128)S(1)}, f32[2,16]{1,0:T(2,128)}, u32[]{:S(2)}) copy-start(f32[2,16]{1,0:T(2,128)} %param.11) | copy-start | bytes 388
  428.9 27.9 %all-to-all-start.3 = ((f32[16,1,4624]{2,1,0:T(1,128)}), f32[16,1,4624]{2,1,0:T(1,128)}, u32[]{:S(2)}, u32[]{:S(2)}) async-start(f32[16,1,4624]{2,1,0:T(1,128)} %reshape.303), calls=%async_computation.3 | async-start | bytes 606208 | tf_op jit(solution)/shard_map/all_to_all | solution.py:25
  594.4 86.1 %all-to-all-start.5 = ((bf16[1,2,320,2560]{3,1,0,2:T(2,128)(2,1)}), bf16[1,2,320,2560]{3,1,0,2:T(2,128)(2,1)S(1)}, u32[]{:S(2)}, u32[]{:S(2)}) async-start(bf16[1,2,320,2560]{3,1,0,2:T(2,128)(2,1)} %reshape.298), calls=%async_computation.5 | async-start | bytes 6553600 | tf_op jit(solution)/shard_map/all_to_all | solution.py:124
  601.5 137.6 %reduce-scatter.2.cloned.1.call-start = ((), (), s32[]{:S(2)}) async-start(), calls=%async_computation.7 | async-start | bytes 6266880 | tf_op jit(solution)/shard_map/reduce_scatter | solution.py:111
  618.4 0.7 copy-start.7
Sparse Core Ops, SparseCore 0:
  618.6 120.5 reduce-scatter.1
where the time goes:
time: 757 us; the launch traced here: 748 us
  local copies, waits for them, and re-layouts  285 us (38%)
  waiting for transfers between devices  261 us (34%)
  blocking collectives  77.3 us (10%)
  starting transfers between devices  47.6 us (6%)
  matrix products  43.3 us (6%)
  other arithmetic  19 us (3%)
  between operations  14.8 us (2%)
    unnamed x25, local copies, waits for them, and re-layouts  156 us
    all_to_all x1, blocking collectives, body(): lax.all_to_all(grad_spec, ENS, split_axis=1, concat_axis=2, tiled=True)  75.6 us
    all_to_all x1, waiting for transfers between devices, body(): lax.all_to_all(spectra, ENS, split_axis=2, concat_axis=1, tiled=True)  69.4 us
    all_to_all x1, waiting for transfers between devices, body(): lax.all_to_all(fourier, ORDER, split_axis=3, concat_axis=2, tiled=True)  62.2 us
    all_to_all x1, waiting for transfers between devices, body(): lax.all_to_all(grid_grad, ORDER, split_axis=2, concat_axis=3, tiled=True)  59.1 us
    reduce_scatter x1, waiting for transfers between devices, body(): lax.psum_scatter((jnp.einsum('bitmq,bilmq->tml', rows, back, preferred_el...  53.7 us
    all_to_all x1, local copies, waits for them, and re-layouts, body(): lax.all_to_all(fourier, ORDER, split_axis=3, concat_axis=2, tiled=True)  40.4 us
    another operation x5, local copies, waits for them, and re-layouts  24.6 us
  transfers between devices with their start and end apart: 6, of which 6 were waited for; matrix products, arithmetic and copies ran while one was open for 4% of the time, Pallas kernels for 0%

commit v1 on v0

v1 whole, which is shorter than its diff:
```python
import jax
import jax.numpy as jnp
import numpy as np
from jax import lax
from jax.experimental import pallas as pl
from jax.experimental.pallas import tpu as pltpu
from jax.sharding import Mesh
from jax.sharding import PartitionSpec as P

MEMBERS = 16
NLAT = 320
L = 320
NBANDS = 16
PARTNERS = 4
JJ = MEMBERS + 1
ORDER = ("order_0", "order_1")
ENS = ("ens_0", "ens_1")
DP_ENS = ("dp", "ens_0", "ens_1")
EVERY = ORDER + ENS
EPSILON = 1e-06
WEIGHT_RATIO = 1.0 / 64.0
BF = jnp.bfloat16
F32 = jnp.float32
GROUP = 16
NGROUPS = L // GROUP
WIDE = 384
VMEM_LIMIT = 56 * 1024 * 1024


def selections():
    full = np.zeros((NLAT, 640), np.float32)
    half = np.zeros((2, NLAT, WIDE), np.float32)
    for t in range(NLAT):
        full[t, 2 * t : 2 * t + 2] = 1.0
        o, rest = divmod(t, 20)
        h, s = divmod(rest, 10)
        half[h, t, 24 * o + 2 * s : 24 * o + 2 * s + 2] = 1.0
    return full, half


FULL, HALF = selections()


def dot(a, b, ca=1, cb=0):
    return lax.dot_general(a, b, (((ca,), (cb,)), ((), ())), preferred_element_type=F32)


def iota(shape, dim):
    return lax.broadcasted_iota(jnp.int32, shape, dim)


def swap_halves(x):
    return pltpu.roll(x, 64, x.ndim - 1)


def split2(x):
    high = x.astype(BF)
    return high, (x - high.astype(F32)).astype(BF)


def split3(x):
    high = x.astype(BF)
    rest = x - high.astype(F32)
    mid = rest.astype(BF)
    return high, mid, (rest - mid.astype(F32)).astype(BF)


def pack_kernel(x_ref, o_ref):
    for p in range(4):
        for b in range(2):
            for s in range(2):
                o_ref[2 * p + b, 20 * s : 20 * s + 20] = x_ref[:, 5 * p + 3 * b + s]
        m = 5 * p + 2
        first = x_ref[0:10, m].astype(F32)
        second = x_ref[10:20, m].astype(F32)
        low = iota(first.shape, 2) < 64
        zeros = jnp.zeros((2, 2, 128), BF)
        o_ref[2 * p, 40:50] = jnp.where(low, first, swap_halves(second)).astype(BF)
        o_ref[2 * p + 1, 40:50] = jnp.where(low, swap_halves(first), second).astype(BF)
        o_ref[2 * p, 50:52] = zeros
        o_ref[2 * p + 1, 50:52] = zeros


def unpack_kernel(y_ref, x_ref):
    for p in range(4):
        for b in range(2):
            for s in range(2):
                x_ref[:, 5 * p + 3 * b + s] = y_ref[2 * p + b, 20 * s : 20 * s + 20]
        m = 5 * p + 2
        first = y_ref[2 * p, 40:50].astype(F32)
        second = y_ref[2 * p + 1, 40:50].astype(F32)
        low = iota(first.shape, 2) < 64
        x_ref[0:10, m] = jnp.where(low, first, swap_halves(second)).astype(BF)
        x_ref[10:20, m] = jnp.where(low, swap_halves(first), second).astype(BF)


def pack(x):
    return pl.pallas_call(
        pack_kernel,
        grid=(16,),
        out_shape=jax.ShapeDtypeStruct((128, 52, 2, 128), BF),
        in_specs=[pl.BlockSpec((20, 20, 2, 128), lambda o: (0, o, 0, 0))],
        out_specs=pl.BlockSpec((8, 52, 2, 128), lambda o: (o, 0, 0, 0)),
        name="pack",
    )(x)


def unpack(y):
    return pl.pallas_call(
        unpack_kernel,
        grid=(16,),
        out_shape=jax.ShapeDtypeStruct((20, 320, 2, 128), BF),
        in_specs=[pl.BlockSpec((8, 52, 2, 128), lambda o: (o, 0, 0, 0))],
        out_specs=pl.BlockSpec((20, 20, 2, 128), lambda o: (0, o, 0, 0)),
        name="unpack",
    )(y)


def target_kernel(t_ref, band_ref, o_ref):
    bands = jnp.broadcast_to(band_ref[:, 0:1].astype(F32), (40, 128))
    low = iota((40, 128), 1) < 64
    for p in range(4):
        middle = t_ref[:, 640 * p + 256 : 640 * p + 384].astype(F32)
        for b in range(2):
            start = 640 * p + WIDE * b
            o_ref[2 * p + b, :, 0:256] = t_ref[:, start : start + 256]
            part = middle if b == 0 else swap_halves(middle)
            o_ref[2 * p + b, :, 256:384] = jnp.where(low, part, bands).astype(BF)


def target_blocks(target, bands):
    return pl.pallas_call(
        target_kernel,
        out_shape=jax.ShapeDtypeStruct((8, 40, WIDE), BF),
        in_specs=[pl.BlockSpec(memory_space=pltpu.VMEM)] * 2,
        out_specs=pl.BlockSpec(memory_space=pltpu.VMEM),
        name="target_blocks",
    )(target, bands)


def own_orders(place_ref):
    ens = place_ref[1]
    pair = ens // 2
    odd = ens % 2
    first = 5 * pair + 3 * odd
    return first, first + 1, 5 * pair + 2


def fetch_orders(place_ref, analysis_ref, own_ref, sem):
    copies = [
        pltpu.make_async_copy(analysis_ref.at[m], own_ref.at[k], sem.at[k])
        for k, m in enumerate(own_orders(place_ref))
    ]
    for copy in copies:
        copy.start()
    for copy in copies:
        copy.wait()


def rows_of(rows_ref, e, start, count):
    block = rows_ref[:, e, start : start + count, :].astype(F32)
    return block.reshape(16 * count, 128).astype(BF)


def two_rows_of(rows_ref, g, start, count):
    return jnp.concatenate(
        [rows_of(rows_ref, 2 * g + k, start, count) for k in range(2)], axis=1
    )


def spectra_kernel(
    place_ref, analysis_ref, rows_ref, target_ref, full_ref, half_ref,
    stacked_ref, grams_ref, own_ref, to_full_ref, to_half_ref, terms_ref, sem,
):
    fetch_orders(place_ref, analysis_ref, own_ref, sem)
    orders = own_orders(place_ref)
    base = place_ref[0] * 20
    for slot in range(2):
        spread = dot(own_ref[slot], full_ref[...], 0, 0)
        member = iota(spread.shape, 1) % 2
        for i in range(2):
            to_full_ref[slot, i] = jnp.where(member == i, spread, 0.0).astype(BF)
    for h in range(2):
        spread = dot(own_ref[2], half_ref[h], 0, 0)
        member = iota(spread.shape, 1) % 2
        for i in range(2):
            to_half_ref[h, i] = jnp.where(member == i, spread, 0.0).astype(BF)
    degree = iota((L, 256), 0)
    low = iota((L, 128), 1) < 64

    def transform(g, carry):
        for slot in range(2):
            values = two_rows_of(rows_ref, g, 40 * slot, 40)
            keep = degree >= base + orders[slot]
            for i in range(2):
                spec = dot(to_full_ref[slot, i], values)
                spec = jnp.where(keep, spec, 0.0).astype(BF)
                for k in range(2):
                    stacked_ref[4 * g + 2 * k + i, :, 128 * slot : 128 * slot + 128] = spec[
                        :, 128 * k : 128 * k + 128
                    ]
        values = two_rows_of(rows_ref, g, 80, 24)
        keep = (degree >= base + orders[2])[:, :128] & low
        for i in range(2):
            first = dot(to_half_ref[0, i], values)
            second = dot(to_half_ref[1, i], values)
            for k in range(2):
                spec = first[:, 128 * k : 128 * k + 128] + swap_halves(
                    second[:, 128 * k : 128 * k + 128]
                )
                stacked_ref[4 * g + 2 * k + i, :, 256:384] = jnp.where(keep, spec, 0.0).astype(BF)
        return carry

    lax.fori_loop(0, 4, transform, 0)

    degree_wide = iota((L, WIDE), 0)
    lane_wide = iota((L, WIDE), 1)
    own_order = jnp.where(
        lane_wide < 128, orders[0], jnp.where(lane_wide < 256, orders[1], orders[2])
    )
    keep = (degree_wide >= base + own_order) & (lane_wide < 320)
    stacked_ref[MEMBERS] = jnp.where(keep, target_ref[...].astype(F32), 0.0).astype(BF)

    size = JJ * GROUP
    same = (iota((size, size), 0) & 15) == (iota((size, size), 1) & 15)
    gather = ((iota((size, 128), 0) >> 4) == iota((size, 128), 1)).astype(F32).astype(BF)

    def gram(g, carry):
        start = pl.multiple_of(g * GROUP, GROUP)
        block = stacked_ref[:, pl.ds(start, GROUP), :].reshape(size, WIDE)
        products = jnp.where(same, dot(block, block, 1, 1), 0.0)
        high, mid, low_part = split3(products)
        sums = dot(high, gather) + dot(mid, gather) + dot(low_part, gather)
        terms_ref[:, pl.ds(start, GROUP), :] = sums.reshape(JJ, GROUP, 128)
        return carry

    lax.fori_loop(0, NGROUPS, gram, 0)

    bands = target_ref[:, 256:384].astype(F32)
    column = jnp.broadcast_to(bands[:, 64:65], (L, 128))
    one_hot = (column == iota((L, 128), 1).astype(F32)).astype(F32).astype(BF)
    blocks = [jnp.zeros((NBANDS, 128), F32) for _ in range(3)]
    for i in range(JJ):
        parts = split3(terms_ref[i])
        total = sum(dot(one_hot, part, 0, 0) for part in parts)[:NBANDS]
        shift = JJ * (i % 7)
        blocks[i // 7] = blocks[i // 7] + (pltpu.roll(total, shift, 1) if shift else total)
    for n in range(3):
        grams_ref[NBANDS * n : NBANDS * n + NBANDS, :] = blocks[n]


def spectra(place, analysis, rows, target, full, half):
    vmem = pl.BlockSpec(memory_space=pltpu.VMEM)
    return pl.pallas_call(
        spectra_kernel,
        out_shape=[
            jax.ShapeDtypeStruct((JJ, L, WIDE), BF),
            jax.ShapeDtypeStruct((3 * NBANDS, 128), F32),
        ],
        in_specs=[
            pl.BlockSpec(memory_space=pltpu.SMEM),
            pl.BlockSpec(memory_space=pl.ANY),
            vmem, vmem, vmem, vmem,
        ],
        out_specs=[vmem, vmem],
        scratch_shapes=[
            pltpu.VMEM((3, NLAT, L), BF),
            pltpu.VMEM((2, 2, L, 640), BF),
            pltpu.VMEM((2, 2, L, WIDE), BF),
            pltpu.VMEM((JJ, L, 128), F32),
            pltpu.SemaphoreType.DMA((3,)),
        ],
        compiler_params=pltpu.CompilerParams(vmem_limit_bytes=VMEM_LIMIT),
        name="spectra",
    )(place, analysis, rows, target, full, half)


def gradient_kernel(
    place_ref, analysis_ref, rows_ref, stacked_ref, target_ref, grams_ref, counts_ref,
    symmetric_ref, cotangent_ref, full_ref, half_ref,
    back_ref, weight_ref, loss_ref,
    own_ref, from_full_ref, from_half_ref, grad_ref, full_sum_ref, half_sum_ref, sem,
):
    fetch_orders(place_ref, analysis_ref, own_ref, sem)
    grams = jnp.sum(grams_ref[...], axis=0)
    lane = iota((NBANDS, 128), 1)
    inside = lane < MEMBERS
    rows = []
    own_power = jnp.zeros((NBANDS, 128), F32)
    for i in range(JJ):
        shift = JJ * (i % 7)
        block = grams[NBANDS * (i // 7) : NBANDS * (i // 7) + NBANDS]
        block = pltpu.roll(block, 128 - shift, 1) if shift else block
        rows.append(jnp.where(lane < JJ, block, 0.0))
        own_power = own_power + jnp.where(lane == i, rows[i], 0.0)
    cotangent = cotangent_ref[...]
    scaled = cotangent * (16.0 * MEMBERS * NLAT)
    mixing = []
    score = jnp.zeros((NBANDS, 128), F32)
    for i in range(MEMBERS):
        squared = rows[i][:, i : i + 1] + own_power - 2.0 * rows[i]
        distance = jnp.sqrt(jnp.maximum(squared, 0.0) + EPSILON)
        observed = distance[:, MEMBERS : MEMBERS + 1]
        pairs = jnp.where(inside, counts_ref[i : i + 1, :] * distance, 0.0)
        score = score + observed / MEMBERS - jnp.sum(pairs, axis=1, keepdims=True) / (
            2.0 * MEMBERS * PARTNERS
        )
        observed_weight = scaled[:, :1] / (MEMBERS * observed)
        pair_weight = scaled * symmetric_ref[i : i + 1, :] / (2.0 * MEMBERS * PARTNERS * distance)
        pair_weight = jnp.where(inside, pair_weight, 0.0)
        own = observed_weight - jnp.sum(pair_weight, axis=1, keepdims=True)
        row = pair_weight + jnp.where(lane == i, own, 0.0)
        mixing.append(row + jnp.where(lane == MEMBERS, -observed_weight, 0.0))
    loss_ref[...] = score * cotangent

    size = MEMBERS * GROUP
    wide = JJ * GROUP
    widen = (iota((128, wide), 0) == (iota((128, wide), 1) >> 4)).astype(F32).astype(BF)
    mix_high, mix_low = split2(jnp.concatenate(mixing, axis=0))
    mix_high = dot(mix_high, widen).astype(BF)
    mix_low = dot(mix_low, widen).astype(BF)
    same_member = (iota((size, size), 0) >> 4) == (iota((size, size), 1) >> 4)
    band_of_column = (iota((size, size), 1) & 15).astype(F32)
    same_degree = (iota((size, wide), 0) & 15) == (iota((size, wide), 1) & 15)

    def mix(g, carry):
        start = pl.multiple_of(g * GROUP, GROUP)
        bands = target_ref[pl.ds(start, GROUP), 256:384].astype(F32)[:, 64:65]
        column = jnp.concatenate([jnp.broadcast_to(bands, (GROUP, size))] * MEMBERS, axis=0)
        pick = (same_member & (column == band_of_column)).astype(F32).astype(BF)
        block = stacked_ref[:, pl.ds(start, GROUP), :].reshape(wide, WIDE)
        high = jnp.where(same_degree, dot(pick, mix_high), 0.0).astype(BF)
        low = jnp.where(same_degree, dot(pick, mix_low), 0.0).astype(BF)
        grad = dot(high, block) + dot(low, block)
        grad_ref[:, pl.ds(start, GROUP), :] = grad.astype(BF).reshape(MEMBERS, GROUP, WIDE)
        return carry

    lax.fori_loop(0, NGROUPS, mix, 0)

    for slot in range(2):
        spread = dot(full_ref[...], own_ref[slot], 0, 0)
        member = iota(spread.shape, 0) % 2
        for i in range(2):
            from_full_ref[slot, i] = jnp.where(member == i, spread, 0.0).astype(BF)
    for h in range(2):
        spread = dot(half_ref[h], own_ref[2], 0, 0)
        member = iota(spread.shape, 0) % 2
        for i in range(2):
            from_half_ref[h, i] = jnp.where(member == i, spread, 0.0).astype(BF)
    full_sum_ref[...] = jnp.zeros_like(full_sum_ref)
    half_sum_ref[...] = jnp.zeros_like(half_sum_ref)

    def grads_of(g, i, slot):
        lanes = slice(128 * slot, 128 * slot + 128)
        return [grad_ref[4 * g + 2 * k + i, :, lanes] for k in range(2)]

    def inverse(g, carry):
        for slot in range(2):
            grads = [jnp.concatenate(grads_of(g, i, slot), axis=1) for i in range(2)]
            back = dot(from_full_ref[slot, 0], grads[0]) + dot(from_full_ref[slot, 1], grads[1])
            for k in range(2):
                part = back[:, 128 * k : 128 * k + 128].reshape(16, 40, 128)
                back_ref[:, 2 * g + k, 40 * slot : 40 * slot + 40, :] = part.astype(BF)
            values = two_rows_of(rows_ref, g, 40 * slot, 40)
            member = iota((640, L), 0) % 2
            terms = jnp.where(member == 0, dot(values, grads[0], 1, 1), dot(values, grads[1], 1, 1))
            full_sum_ref[slot] += terms
        pieces = [grads_of(g, i, 2) for i in range(2)]
        grads = [jnp.concatenate(pieces[i], axis=1) for i in range(2)]
        swapped = [
            jnp.concatenate([swap_halves(piece.astype(F32)).astype(BF) for piece in pieces[i]], axis=1)
            for i in range(2)
        ]
        first = dot(from_half_ref[0, 0], grads[0]) + dot(from_half_ref[0, 1], grads[1])
        second = dot(from_half_ref[1, 0], swapped[0]) + dot(from_half_ref[1, 1], swapped[1])
        back = first + second
        for k in range(2):
            part = back[:, 128 * k : 128 * k + 128].reshape(16, 24, 128)
            back_ref[:, 2 * g + k, 80:104, :] = part.astype(BF)
        values = two_rows_of(rows_ref, g, 80, 24)
        member = iota((WIDE, L), 0) % 2
        for h, sides in enumerate((grads, swapped)):
            half_sum_ref[h] += jnp.where(
                member == 0, dot(values, sides[0], 1, 1), dot(values, sides[1], 1, 1)
            )
        return carry

    lax.fori_loop(0, 4, inverse, 0)

    for slot in range(3):
        if slot < 2:
            parts = split2(full_sum_ref[slot])
            weight = dot(full_ref[...], parts[0]) + dot(full_ref[...], parts[1])
        else:
            weight = jnp.zeros((NLAT, L), F32)
            for h in range(2):
                parts = split2(half_sum_ref[h])
                weight = weight + dot(half_ref[h], parts[0]) + dot(half_ref[h], parts[1])
        weight = weight * WEIGHT_RATIO
        for c in range(16):
            weight_ref[c, slot] = weight[20 * c : 20 * c + 20].astype(BF)


def gradient(place, analysis, rows, stacked, target, grams, counts, symmetric, cotangent, full, half):
    vmem = pl.BlockSpec(memory_space=pltpu.VMEM)
    return pl.pallas_call(
        gradient_kernel,
        out_shape=[
            jax.ShapeDtypeStruct((16, 8, 104, 128), BF),
            jax.ShapeDtypeStruct((16, 3, 20, L), BF),
            jax.ShapeDtypeStruct((NBANDS, 128), F32),
        ],
        in_specs=[
            pl.BlockSpec(memory_space=pltpu.SMEM),
            pl.BlockSpec(memory_space=pl.ANY),
        ]
        + [vmem] * 9,
        out_specs=[vmem] * 3,
        scratch_shapes=[
            pltpu.VMEM((3, NLAT, L), BF),
            pltpu.VMEM((2, 2, 640, L), BF),
            pltpu.VMEM((2, 2, WIDE, L), BF),
            pltpu.VMEM((MEMBERS, L, WIDE), BF),
            pltpu.VMEM((2, 640, L), F32),
            pltpu.VMEM((2, WIDE, L), F32),
            pltpu.SemaphoreType.DMA((3,)),
        ],
        compiler_params=pltpu.CompilerParams(vmem_limit_bytes=VMEM_LIMIT),
        name="gradient",
    )(place, analysis, rows, stacked, target, grams, counts, symmetric, cotangent, full, half)


def finish_kernel(r_ref, o_ref):
    def both(e, slot):
        return r_ref[e, slot].astype(F32) + r_ref[8 + e, slot].astype(F32)

    for p in range(4):
        for b in range(2):
            for s in range(2):
                o_ref[:, 5 * p + 3 * b + s, :] = both(2 * p + b, s)
        o_ref[:, 5 * p + 2, :] = both(2 * p, 2) + both(2 * p + 1, 2)


def finish(received):
    return pl.pallas_call(
        finish_kernel,
        out_shape=jax.ShapeDtypeStruct((20, 20, L), F32),
        in_specs=[pl.BlockSpec(memory_space=pltpu.VMEM)],
        out_specs=pl.BlockSpec(memory_space=pltpu.VMEM),
        name="finish",
    )(received)


def exchange(x, axes):
    return lax.all_to_all(x, axes, split_axis=0, concat_axis=0, tiled=True)


def body(fourier, analysis, target, band_ids, partners, band_cotangent):
    place = jnp.stack([lax.axis_index(ORDER), lax.axis_index(ENS)]).astype(jnp.int32)
    full = jnp.asarray(FULL, BF)
    half = jnp.asarray(HALF, BF)
    by_order = jnp.transpose(analysis, (1, 0, 2))
    native = jnp.transpose(fourier[0].reshape(2, 20, 320, 128), (1, 2, 0, 3))
    blocks = target_blocks(target[0], band_ids)
    observed = exchange(blocks, ENS).reshape(L, WIDE)
    received = exchange(pack(native), EVERY)
    rows = received.reshape(128, 104, 128).reshape(16, 8, 104, 128)
    stacked, grams = spectra(place, by_order, rows, observed, full, half)
    grams = exchange(jnp.broadcast_to(grams, (16, *grams.shape)), ORDER).sum(axis=0)
    grams = exchange(jnp.broadcast_to(grams, (8, *grams.shape)), ENS)
    member_ids = jnp.arange(128, dtype=jnp.int32)
    counts = jnp.sum((partners[:, :, None] == member_ids[None, None, :]).astype(F32), axis=1)
    square = counts[:, :MEMBERS]
    symmetric = jnp.pad(square + square.T, ((0, 0), (0, 128 - MEMBERS)))
    cotangent = lax.dynamic_slice_in_dim(band_cotangent, lax.axis_index("dp"), 1, 0)[0]
    cotangent = jnp.broadcast_to(cotangent[:, None], (NBANDS, 128))
    back, weight, loss = gradient(
        place, by_order, rows, stacked, observed, grams, counts, symmetric, cotangent, full, half
    )
    loss_bands = lax.psum(loss[:, 0], "dp")
    returned = exchange(back.reshape(128, 104, 128).reshape(128, 52, 2, 128), EVERY)
    grad_analysis = finish(exchange(weight, DP_ENS))
    native_grad = unpack(returned)
    grad_fourier = jnp.transpose(native_grad, (2, 0, 1, 3)).reshape(1, 2, 20, 40960)
    return (grad_fourier, grad_analysis, loss_bands)


def solution(mesh):
    torus = Mesh(
        mesh.devices.reshape(mesh.shape["dp"], 4, 4, 2, 4),
        ("dp", "order_0", "order_1", "ens_0", "ens_1"),
    )
    in_specs = (
        P("dp", ENS, ORDER, None),
        P(None, ORDER, None),
        P("dp", ENS, ORDER),
        P(ENS, ORDER),
        P(),
        P(),
    )
    out_specs = (P("dp", ENS, ORDER, None), P(DP_ENS, ORDER, None), P())
    return jax.shard_map(body, mesh=torus, in_specs=in_specs, out_specs=out_specs, check_vma=False)
```

time: 757 us -> 354 us (0.47)
  local copies, waits for them, and re-layouts: 285 us -> 8.6 us
  waiting for transfers between devices: 261 us -> 164 us
  Pallas kernels: 0 us -> 88.5 us
  matrix products: 43.3 us -> 0 us
  blocking collectives: 77.3 us -> 41.1 us
  other arithmetic: 19 us -> 0.72 us
  between operations: 14.8 us -> 0.73 us
    unnamed x25 -> x18, local copies, waits for them, and re-layouts: 156 us -> 5.74 us
    pallas_call x0 -> x6, Pallas kernels: none -> 88.5 us  [the longest x1 33.3 us: gradient(): pl.pallas_call(gradient_kernel, out_shape=[jax.ShapeDtypeStruct((16, 8, 1...]
    reduce_scatter x1 -> x0, waiting for transfers between devices: 53.7 us -> none  [body(): lax.psum_scatter((jnp.einsum('bitmq,bilmq->tml', rows, back, preferred_el...]
    all_to_all x5 -> x0, local copies, waits for them, and re-layouts: 48.5 us -> none  [the longest x1 40.4 us: body(): lax.all_to_all(fourier, ORDER, split_axis=3, concat_axis=2, tiled=True)]
    all_to_all x5 -> x4, waiting for transfers between devices: 208 us -> 164 us  [exchange(): return lax.all_to_all(x, axes, split_axis=0, concat_axis=0, tiled=True)]
    dot_general x7 -> x0, matrix products: 43.3 us -> none  [the longest x1 7.56 us: body(): jnp.einsum('bitmq,bilmq->tml', rows, back, preferred_element_type=jnp.flo...]
    reshape x8 -> x0, local copies, waits for them, and re-layouts: 40 us -> none  [the longest x2 12 us: body(): grid_grad = grid_grad.reshape(samples, own_members, NLAT, orders * width)]
    all_to_all x1 -> x2, blocking collectives: 75.6 us -> 38.1 us  [exchange(): return lax.all_to_all(x, axes, split_axis=0, concat_axis=0, tiled=True)]
  transfers between devices with their start and end apart: 6 -> 4, of which waited for: 6 -> 4; matrix products, arithmetic and copies ran while one was open for 4% -> 0% of each run, Pallas kernels for 0% -> 4%
where the time goes in v1:
time: 354 us; the launch traced here: 352 us
  waiting for transfers between devices  164 us (46%)
  Pallas kernels  88.5 us (25%)
  starting transfers between devices  48.4 us (14%)
  blocking collectives  41.1 us (12%)
  local copies, waits for them, and re-layouts  8.6 us (2%)
    all_to_all x4, waiting for transfers between devices, exchange(): return lax.all_to_all(x, axes, split_axis=0, concat_axis=0, tiled=True)  164 us
    all_to_all x4, starting transfers between devices, exchange(): return lax.all_to_all(x, axes, split_axis=0, concat_axis=0, tiled=True)  48.4 us
    all_to_all x2, blocking collectives, exchange(): return lax.all_to_all(x, axes, split_axis=0, concat_axis=0, tiled=True)  38.1 us
    pallas_call x1, Pallas kernels, gradient(): pl.pallas_call(gradient_kernel, out_shape=[jax.ShapeDtypeStruct((16, 8, 1...  33.3 us
    pallas_call x1, Pallas kernels, spectra(): pl.pallas_call(spectra_kernel, out_shape=[jax.ShapeDtypeStruct((JJ, L, WI...  28.9 us
    pallas_call x1, Pallas kernels, unpack(): pl.pallas_call(unpack_kernel, grid=(16,), out_shape=jax.ShapeDtypeStruct(...  11.4 us
    pallas_call x1, Pallas kernels, pack(): pl.pallas_call(pack_kernel, grid=(16,), out_shape=jax.ShapeDtypeStruct((1...  10.9 us
  transfers between devices with their start and end apart: 4, of which 4 were waited for; matrix products, arithmetic and copies ran while one was open for 0% of the time, Pallas kernels for 4%

profile of v1, /device:TPU:8, one launch (start us, length us, event | category | flops | bytes accessed | tf_op | source)
XLA Modules:
  0.0 352.4 jit_solution(2695287387169335884)
XLA Ops:
  0.6 0.0 copy-start
  0.6 1.4 copy.19.band_ref
  2.0 1.7 target_blocks.1
  3.8 10.9 %all-to-all-start.1 = ((bf16[8,40,384]{2,1,0:T(8,128)(2,1)}), bf16[8,40,384]{2,1,0:T(8,128)(2,1)S(1)}, u32[]{:S(2)}, u32[]{:S(2)}) async-start(bf16[8,40,384]{2,1,0:T(8,128)(2,1)} %target_blocks.1), calls=%async_computation.1 | async-start | bytes 491520 | tf_op jit(solution)/shard_map/all_to_all | solution.py:455
  14.7 10.9 %pack.1 = bf16[128,52,2,128]{3,2,1,0:T(2,128)(2,1)} custom-call(bf16[20,320,2,128]{3,2,1,0:T(2,128)(2,1)} %bitcast.23), custom_call_target="tpu_custom_call" | custom-call | tf_op jit(solution)/shard_map/pack/pallas_call | solution.py:98
  25.6 0.2 all-to-all-done.1
  25.7 0.0 copy-start.3
  25.7 0.7 copy-done.3
  26.4 13.9 %all-to-all-start = ((bf16[128,52,2,128]{3,2,1,0:T(2,128)(2,1)}), bf16[128,52,2,128]{3,2,1,0:T(2,128)(2,1)S(1)}, u32[]{:S(2)}, u32[]{:S(2)}) async-start(bf16[128,52,2,128]{3,2,1,0:T(2,128)(2,1)} %pack.1), calls=%async_computation | async-start | bytes 6815744 | tf_op jit(solution)/shard_map/all_to_all | solution.py:455
  40.3 0.6 pad_add_fusion.place_ref
  40.9 79.0 %all-to-all-done = bf16[128,52,2,128]{3,2,1,0:T(2,128)(2,1)S(1)} async-done(((bf16[128,52,2,128]{3,2,1,0:T(2,128)(2,1)}), bf16[128,52,2,128]{3,2,1,0:T(2,128)(2,1)S(1)}, u32[]{:S(2)}, u32[]{:S(2)}) %all-to-all-start) | async-done | bytes 3407904 | tf_op jit(solution)/shard_map/all_to_all | solution.py:455
  120.0 0.0 copy-start.1
  120.0 1.8 copy-done.1
  121.8 0.0 copy-start.7
  121.8 28.9 %spectra.1 = (bf16[17,320,384]{2,1,0:T(8,128)(2,1)}, f32[48,128]{1,0:T(8,128)}) custom-call(s32[2]{0:T(128)} %pad_add_fusion.place_ref, bf16[20,320,320]{2,1,0:T(8,128)(2,1)} %bitcast.20, bf16[16,8,104,128]{3,2,1,0:T(8,128)(2,1)} %bitcast.18, bf16[320,384]{1,0:T(8,128)(2,1)} %bitcast.25, bf16[320,640]{1,0:T(8,128)(2,1)} %constant.33.clone.full_ref, ...), custom_call_target="tpu_custom_call" | custom-call | tf_op jit(solution)/shard_map/spectra/pallas_call | solution.py:254
  150.7 0.8 broadcast_in_dim.15
  151.5 15.2 %all_to_all.30 = f32[16,48,128]{2,1,0:T(8,128)S(1)} all-to-all(f32[16,48,128]{2,1,0:T(8,128)S(1)} %broadcast_in_dim.15), channel_id=1, replica_groups=mesh['dp'=2,'order_0'=4,'order_1'=4,'ens_0'=2,'ens_1'=4] {'order_0','ord..., dimensions={0} | all-to-all | bytes 786432 | tf_op jit(solution)/shard_map/all_to_all | solution.py:455
  166.7 0.7 broadcast_in_dim.16
  167.4 6.6 %all-to-all-start.3 = ((f32[8,48,128]{2,1,0:T(8,128)}), f32[8,48,128]{2,1,0:T(8,128)S(1)}, u32[]{:S(2)}, u32[]{:S(2)}) async-start(f32[8,48,128]{2,1,0:T(8,128)} %broadcast_in_dim.16), calls=%async_computation.3 | async-start | bytes 393216 | tf_op jit(solution)/shard_map/all_to_all | solution.py:455
  174.0 0.0 copy-done.7
  174.0 0.1 convert_reduce_fusion.counts_ref
  174.1 0.0 copy-start.5
  174.1 0.1 copy.22
  174.1 0.6 pad.4.symmetric_ref
  174.7 0.0 copy-done
  174.8 10.2 %all-to-all-done.3.grams_ref = f32[8,48,128]{2,1,0:T(8,128)S(1)} async-done(((f32[8,48,128]{2,1,0:T(8,128)}), f32[8,48,128]{2,1,0:T(8,128)S(1)}, u32[]{:S(2)}, u32[]{:S(2)}) %all-to-all-start.3) | async-done | bytes 196640 | tf_op jit(solution)/shard_map/all_to_all | solution.py:455
  184.9 0.0 copy-start.4
  184.9 0.7 broadcast_in_dim.18.cotangent_ref
  185.6 0.0 copy-done.5
  185.6 0.0 copy-done.4
  185.6 33.3 %gradient.1 = (bf16[16,8,104,128]{3,2,1,0:T(8,128)(2,1)}, bf16[16,3,20,320]{3,2,1,0:T(8,128)(2,1)}, f32[16,128]{1,0:T(8,128)}) custom-call(s32[2]{0:T(128)} %pad_add_fusion.place_ref, bf16[20,320,320]{2,1,0:T(8,128)(2,1)} %bitcast.21, bf16[16,8,104,128]{3,2,1,0:T(8,128)(2,1)} %bitcast.19, bf16[17,320,384]{2,1,0:T(8,128)(2,1)} %get-tuple-element.8.stacked_ref, ...), custom_call_target="tpu_custom_call" | custom-call | tf_op jit(solution)/shard_map/gradient/pallas_call | solution.py:406
  218.9 23.0 %all_to_all.31.r_ref = bf16[16,3,20,320]{3,2,1,0:T(8,128)(2,1)} all-to-all(bf16[16,3,20,320]{3,2,1,0:T(8,128)(2,1)} %get-tuple-element.11), channel_id=1, replica_groups=mesh['dp'=2,'order_0'=4,'order_1'=4,'ens_0'=2,'ens_1'=4] {'dp','ens_0','..., dimensions={0} | all-to-all | bytes 1228800 | tf_op jit(solution)/shard_map/all_to_all | solution.py:455
  241.9 0.0 copy-start.6
  241.9 17.0 %all-to-all-start.4 = ((bf16[128,52,2,128]{3,2,1,0:T(2,128)(2,1)}), bf16[128,52,2,128]{3,2,1,0:T(2,128)(2,1)S(1)}, u32[]{:S(2)}, u32[]{:S(2)}) async-start(bf16[128,52,2,128]{3,2,1,0:T(2,128)(2,1)} %bitcast.22), calls=%async_computation.4 | async-start | bytes 6815744 | tf_op jit(solution)/shard_map/all_to_all | solution.py:455
  258.9 0.0 copy-done.6
  258.9 0.1 slice_reduce_fusion
  259.0 3.0 psum.7
  262.0 2.3 finish.1
  264.3 75.0 %all-to-all-done.4.y_ref = bf16[128,52,2,128]{3,2,1,0:T(2,128)(2,1)S(1)} async-done(((bf16[128,52,2,128]{3,2,1,0:T(2,128)(2,1)}), bf16[128,52,2,128]{3,2,1,0:T(2,128)(2,1)S(1)}, u32[]{:S(2)}, u32[]{:S(2)}) %all-to-all-start.4) | async-done | bytes 3407904 | tf_op jit(solution)/shard_map/all_to_all | solution.py:455
  339.3 0.0 copy-start.2
  339.3 1.7 copy-done.2
  341.0 11.4 %unpack.1 = bf16[20,320,2,128]{3,2,1,0:T(2,128)(2,1)} custom-call(bf16[128,52,2,128]{3,2,1,0:T(2,128)(2,1)} %copy-done.2), custom_call_target="tpu_custom_call" | custom-call | tf_op jit(solution)/shard_map/unpack/pallas_call | solution.py:109
  (3 shorter events, 0.0 us)
Async XLA Ops:
  0.6 174.1 %copy-start = (f32[2,16]{1,0:T(2,128)S(1)}, f32[2,16]{1,0:T(2,128)}, u32[]{:S(2)}) copy-start(f32[2,16]{1,0:T(2,128)} %param.13) | copy-start | bytes 388
  3.8 22.0 %all-to-all-start.1 = ((bf16[8,40,384]{2,1,0:T(8,128)(2,1)}), bf16[8,40,384]{2,1,0:T(8,128)(2,1)S(1)}, u32[]{:S(2)}, u32[]{:S(2)}) async-start(bf16[8,40,384]{2,1,0:T(8,128)(2,1)} %target_blocks.1), calls=%async_computation.1 | async-start | bytes 491520 | tf_op jit(solution)/shard_map/all_to_all | solution.py:455
  25.7 0.7 copy-start.3
  26.4 93.5 %all-to-all-start = ((bf16[128,52,2,128]{3,2,1,0:T(2,128)(2,1)}), bf16[128,52,2,128]{3,2,1,0:T(2,128)(2,1)S(1)}, u32[]{:S(2)}, u32[]{:S(2)}) async-start(bf16[128,52,2,128]{3,2,1,0:T(2,128)(2,1)} %pack.1), calls=%async_computation | async-start | bytes 6815744 | tf_op jit(solution)/shard_map/all_to_all | solution.py:455
  120.0 1.8 copy-start.1
  121.8 52.2 %copy-start.7 = (s32[16,4]{0,1:T(4,128)S(1)}, s32[16,4]{0,1:T(4,128)}, u32[]{:S(2)}) copy-start(s32[16,4]{0,1:T(4,128)} %param.12) | copy-start | bytes 772
  167.4 17.5 %all-to-all-start.3 = ((f32[8,48,128]{2,1,0:T(8,128)}), f32[8,48,128]{2,1,0:T(8,128)S(1)}, u32[]{:S(2)}, u32[]{:S(2)}) async-start(f32[8,48,128]{2,1,0:T(8,128)} %broadcast_in_dim.16), calls=%async_computation.3 | async-start | bytes 393216 | tf_op jit(solution)/shard_map/all_to_all | solution.py:455
  174.1 11.5 %copy-start.5 = (f32[16,128]{1,0:T(8,128)}, f32[16,128]{1,0:T(8,128)S(1)}, u32[]{:S(2)}) copy-start(f32[16,128]{1,0:T(8,128)S(1)} %convert_reduce_fusion.counts_ref) | copy-start | bytes 24580
  184.9 0.7 copy-start.4
  241.9 17.0 %copy-start.6 = (f32[16,128]{1,0:T(8,128)S(1)}, f32[16,128]{1,0:T(8,128)}, u32[]{:S(2)}) copy-start(f32[16,128]{1,0:T(8,128)} %get-tuple-element.12) | copy-start | bytes 24580
  241.9 97.4 %all-to-all-start.4 = ((bf16[128,52,2,128]{3,2,1,0:T(2,128)(2,1)}), bf16[128,52,2,128]{3,2,1,0:T(2,128)(2,1)S(1)}, u32[]{:S(2)}, u32[]{:S(2)}) async-start(bf16[128,52,2,128]{3,2,1,0:T(2,128)(2,1)} %bitcast.22), calls=%async_computation.4 | async-start | bytes 6815744 | tf_op jit(solution)/shard_map/all_to_all | solution.py:455
  339.3 1.7 copy-start.2

commit v2 on v1

v2 whole, which is shorter than its diff:
```python
import functools

import jax
import jax.numpy as jnp
import numpy as np
from jax import lax
from jax.experimental import pallas as pl
from jax.experimental.pallas import tpu as pltpu
from jax.sharding import Mesh
from jax.sharding import PartitionSpec as P

MEMBERS = 16
NLAT = 320
L = 320
NBANDS = 16
PARTNERS = 4
JJ = MEMBERS + 1
ORDER = ("order_0", "order_1")
ENS = ("ens_0", "ens_1")
DP_ENS = ("dp", "ens_0", "ens_1")
EVERY = ORDER + ENS
EPSILON = 1e-06
WEIGHT_RATIO = 1.0 / 64.0
BF = jnp.bfloat16
F32 = jnp.float32
GROUP = 16
NGROUPS = L // GROUP
WIDE = 384
VMEM_LIMIT = 48 * 1024 * 1024
VMEM = pl.BlockSpec(memory_space=pltpu.VMEM)
SMEM = pl.BlockSpec(memory_space=pltpu.SMEM)
ANY = pl.BlockSpec(memory_space=pl.ANY)


def selections():
    full = np.zeros((NLAT, 640), np.float32)
    half = np.zeros((2, NLAT, WIDE), np.float32)
    for t in range(NLAT):
        full[t, 2 * t : 2 * t + 2] = 1.0
        o, rest = divmod(t, 20)
        h, s = divmod(rest, 10)
        half[h, t, 24 * o + 2 * s : 24 * o + 2 * s + 2] = 1.0
    return full, half


def orderings():
    whole = np.zeros((320, 320), np.float32)
    half = np.zeros((2, 96, 160), np.float32)
    for t in range(20):
        h, s = divmod(t, 10)
        for i in range(2):
            for e in range(8):
                whole[40 * e + 2 * t + i, 16 * t + 2 * e + i] = 1.0
            for p in range(4):
                half[h, 24 * p + 2 * s + i, 8 * t + 2 * p + i] = 1.0
    return whole, half


FULL, HALF = selections()
WHOLE_ORDER, HALF_ORDER = orderings()


def dot(a, b, ca=1, cb=0):
    return lax.dot_general(a, b, (((ca,), (cb,)), ((), ())), preferred_element_type=F32)


def iota(shape, dim):
    return lax.broadcasted_iota(jnp.int32, shape, dim)


def swap_halves(x):
    return pltpu.roll(x, 64, x.ndim - 1)


def split2(x):
    high = x.astype(BF)
    return high, (x - high.astype(F32)).astype(BF)


def split3(x):
    high = x.astype(BF)
    rest = x - high.astype(F32)
    mid = rest.astype(BF)
    return high, mid, (rest - mid.astype(F32)).astype(BF)


def pack_kernel(x_ref, whole_ref, half_ref, o_ref):
    def columns(start, count):
        parts = [x_ref[:, 40 * k + start : 40 * k + start + count, :] for k in range(2)]
        parts = [part.astype(F32).reshape(20 * count, 128).astype(BF) for part in parts]
        return jnp.concatenate(parts, axis=1)

    for slot in range(2):
        moved = halves(dot(whole_ref[...], columns(16 * slot, 16)))
        for k in range(2):
            o_ref[k, :, 40 * slot : 40 * slot + 40, :] = moved[k].reshape(8, 40, 128).astype(BF)
    values = columns(32, 8)
    first = halves(dot(half_ref[0], values))
    second = halves(dot(half_ref[1], values))
    low = iota((96, 128), 1) < 64
    for k in range(2):
        real = jnp.where(low, first[k], swap_halves(second[k])).astype(BF)
        imaginary = jnp.where(low, swap_halves(first[k]), second[k]).astype(BF)
        for p in range(4):
            o_ref[k, 2 * p, 80:104, :] = real[24 * p : 24 * p + 24]
            o_ref[k, 2 * p + 1, 80:104, :] = imaginary[24 * p : 24 * p + 24]


def unpack_kernel(y_ref, whole_ref, half_ref, x_ref):
    for slot in range(2):
        parts = [y_ref[k, :, 40 * slot : 40 * slot + 40, :].astype(F32) for k in range(2)]
        parts = [part.reshape(320, 128).astype(BF) for part in parts]
        moved = halves(dot(whole_ref[...], jnp.concatenate(parts, axis=1)))
        for k in range(2):
            start = 40 * k + 16 * slot
            x_ref[:, start : start + 16, :] = moved[k].reshape(20, 16, 128).astype(BF)
    low = iota((96, 128), 1) < 64
    firsts, seconds = [], []
    for k in range(2):
        real, imaginary = [
            jnp.concatenate([y_ref[k, 2 * p + r, 80:104, :].astype(F32) for p in range(4)], axis=0)
            for r in range(2)
        ]
        firsts.append(jnp.where(low, real, swap_halves(imaginary)).astype(BF))
        seconds.append(jnp.where(low, swap_halves(real), imaginary).astype(BF))
    moved = halves(
        dot(half_ref[0], jnp.concatenate(firsts, axis=1))
        + dot(half_ref[1], jnp.concatenate(seconds, axis=1))
    )
    for k in range(2):
        x_ref[:, 40 * k + 32 : 40 * k + 40, :] = moved[k].reshape(20, 8, 128).astype(BF)


NATIVE = pl.BlockSpec((20, 80, 128), lambda o: (0, o, 0))
PACKED = pl.BlockSpec((2, 8, 104, 128), lambda o: (o, 0, 0, 0))


def constant(shape):
    return pl.BlockSpec(shape, lambda o: (0,) * len(shape))


def pack(x):
    return pl.pallas_call(
        pack_kernel,
        grid=(8,),
        out_shape=jax.ShapeDtypeStruct((16, 8, 104, 128), BF),
        in_specs=[NATIVE, constant((320, 320)), constant((2, 96, 160))],
        out_specs=PACKED,
        name="pack",
    )(x, jnp.asarray(WHOLE_ORDER, BF), jnp.asarray(HALF_ORDER, BF))


def unpack(y):
    return pl.pallas_call(
        unpack_kernel,
        grid=(8,),
        out_shape=jax.ShapeDtypeStruct((20, 640, 128), BF),
        in_specs=[PACKED, constant((320, 320)), constant((2, 160, 96))],
        out_specs=NATIVE,
        name="unpack",
    )(y, jnp.asarray(WHOLE_ORDER.T, BF), jnp.asarray(HALF_ORDER.transpose(0, 2, 1), BF))


def target_kernel(place_ref, t_ref, band_ref, *o_refs):
    bands = jnp.broadcast_to(band_ref[:, 0:1].astype(F32), (40, 128))
    low = iota((40, 128), 1) < 64
    for k in range(8):
        e = jnp.bitwise_xor(place_ref[1], k)

        def lanes(start):
            return t_ref[:, pl.ds(pl.multiple_of(start, 128), 128)]

        middle = lanes(2048 + 128 * (e // 2)).astype(F32)
        o_refs[k][:, 0:128] = lanes(128 * e)
        o_refs[k][:, 128:256] = lanes(1024 + 128 * e)
        odd = jnp.broadcast_to(e % 2, (40, 128)) == 1
        part = jnp.where(odd, swap_halves(middle), middle)
        o_refs[k][:, 256:384] = jnp.where(low, part, bands).astype(BF)


def target_blocks(place, target, bands):
    return pl.pallas_call(
        target_kernel,
        out_shape=[jax.ShapeDtypeStruct((40, WIDE), BF)] * 8,
        in_specs=[SMEM, VMEM, VMEM],
        out_specs=[VMEM] * 8,
        name="target_blocks",
    )(place, target, bands)


def own_orders(place_ref):
    ens = place_ref[1]
    return ens, 8 + ens, 16 + ens // 2


def fetches(place_ref, analysis_ref, own_ref, sem):
    return [
        pltpu.make_async_copy(analysis_ref.at[m], own_ref.at[k], sem.at[k])
        for k, m in enumerate(own_orders(place_ref))
    ]


def halves(x):
    return [x[:, 128 * k : 128 * k + 128] for k in range(2)]


STARTS = (0, 40, 80)
COUNTS = (40, 40, 24)


def two_rows_of(rows_ref, g, slot):
    start, count = STARTS[slot], COUNTS[slot]
    parts = [
        rows_ref[:, 2 * g + k, start : start + count, :]
        .astype(F32)
        .reshape(16 * count, 128)
        .astype(BF)
        for k in range(2)
    ]
    return jnp.concatenate(parts, axis=1)


def band_column(target_ref, start, count):
    return target_ref[pl.ds(start, count), 256:384].astype(F32)[:, 64:65]


def spectra_kernel(place_ref, analysis_ref, rows_ref, full_ref, half_ref, *refs):
    target_refs = refs[:8]
    stacked_ref, target_ref, grams_ref = refs[8:11]
    own_ref, to_full_ref, to_half_ref, terms_ref, order_ref, sem = refs[11:]
    copies = fetches(place_ref, analysis_ref, own_ref, sem)
    for copy in copies:
        copy.start()
    for k in range(8):
        order_ref[jnp.bitwise_xor(place_ref[1], k)] = target_refs[k][...].astype(F32)
    target_ref[...] = order_ref[...].reshape(L, WIDE).astype(BF)
    for copy in copies:
        copy.wait()
    base = place_ref[0] * 20
    orders = [base + m for m in own_orders(place_ref)]
    for n in range(4):
        if n < 2:
            spread = dot(own_ref[n], full_ref[...], 0, 0)
        else:
            spread = dot(own_ref[2], half_ref[n - 2], 0, 0)
        member = iota(spread.shape, 1) % 2
        for i in range(2):
            part = jnp.where(member == i, spread, 0.0).astype(BF)
            if n < 2:
                to_full_ref[n, i] = part
            else:
                to_half_ref[n - 2, i] = part
    degree = iota((L, 128), 0)
    low = iota((L, 128), 1) < 64
    keeps = [degree >= orders[0], degree >= orders[1], (degree >= orders[2]) & low]

    def transform(g, carry):
        for slot in range(3):
            values = two_rows_of(rows_ref, g, slot)
            for i in range(2):
                if slot < 2:
                    parts = halves(dot(to_full_ref[slot, i], values))
                else:
                    parts = halves(dot(to_half_ref[0, i], values))
                    other = halves(dot(to_half_ref[1, i], values))
                    parts = [parts[k] + swap_halves(other[k]) for k in range(2)]
                for k in range(2):
                    stacked_ref[4 * g + 2 * k + i, :, 128 * slot : 128 * slot + 128] = jnp.where(
                        keeps[slot], parts[k], 0.0
                    ).astype(BF)
        return carry

    lax.fori_loop(0, 4, transform, 0)
    for slot in range(3):
        lanes = slice(128 * slot, 128 * slot + 128)
        observed = jnp.where(keeps[slot], target_ref[:, lanes].astype(F32), 0.0)
        stacked_ref[MEMBERS, :, lanes] = observed.astype(BF)

    size = MEMBERS * GROUP
    same = (iota((size, size), 0) & 15) == (iota((size, size), 1) & 15)
    gather = ((iota((size, 128), 0) >> 4) == iota((size, 128), 1)).astype(F32).astype(BF)
    at_observed = iota((size, 128), 1) == MEMBERS

    def gram(g, carry):
        start = pl.multiple_of(g * GROUP, GROUP)
        block = stacked_ref[0:MEMBERS, pl.ds(start, GROUP), :].reshape(size, WIDE)
        own = stacked_ref[MEMBERS, pl.ds(start, GROUP), :].astype(F32)
        products = jnp.where(same, dot(block, block, 1, 1), 0.0)
        high, mid, low_part = split3(products)
        sums = dot(high, gather) + dot(mid, gather) + dot(low_part, gather)
        beside = jnp.concatenate([own] * MEMBERS, axis=0) * block.astype(F32)
        sums = jnp.where(at_observed, jnp.sum(beside, axis=1, keepdims=True), sums)
        last = jnp.sum(own * own, axis=1, keepdims=True)
        pieces = [sums[GROUP * i : GROUP * i + GROUP] for i in range(MEMBERS)]
        pieces.append(jnp.where(at_observed[:GROUP], last, 0.0))
        for n in range(3):
            total = pieces[7 * n]
            for i in range(7 * n + 1, min(7 * n + 7, JJ)):
                total = total + pltpu.roll(pieces[i], JJ * (i % 7), 1)
            terms_ref[n, pl.ds(start, GROUP), :] = total
        return carry

    lax.fori_loop(0, NGROUPS, gram, 0, unroll=4)

    column = jnp.broadcast_to(band_column(target_ref, 0, L), (L, 128))
    one_hot = (column == iota((L, 128), 1).astype(F32)).astype(F32).astype(BF)
    for n in range(3):
        total = sum(dot(one_hot, part, 0, 0) for part in split3(terms_ref[n]))
        grams_ref[NBANDS * n : NBANDS * n + NBANDS] = total[:NBANDS]


def spectra(place, analysis, rows, targets, full, half):
    return pl.pallas_call(
        spectra_kernel,
        out_shape=[
            jax.ShapeDtypeStruct((JJ, L, WIDE), BF),
            jax.ShapeDtypeStruct((L, WIDE), BF),
            jax.ShapeDtypeStruct((3 * NBANDS, 128), F32),
        ],
        in_specs=[SMEM, ANY] + [VMEM] * 11,
        out_specs=[VMEM] * 3,
        scratch_shapes=[
            pltpu.VMEM((3, NLAT, L), BF),
            pltpu.VMEM((2, 2, L, 640), BF),
            pltpu.VMEM((2, 2, L, WIDE), BF),
            pltpu.VMEM((3, L, 128), F32),
            pltpu.VMEM((8, 40, WIDE), F32),
            pltpu.SemaphoreType.DMA((3,)),
        ],
        compiler_params=pltpu.CompilerParams(vmem_limit_bytes=VMEM_LIMIT),
        cost_estimate=pl.CostEstimate(
            flops=10_000_000_000, bytes_accessed=12_000_000, transcendentals=0
        ),
        name="spectra",
    )(place, analysis, rows, full, half, *targets)


def gradient_kernel(
    place_ref, analysis_ref, stacked_ref, target_ref, grams_ref, counts_ref,
    symmetric_ref, cotangent_ref, full_ref, half_ref,
    back_ref, grad_ref, loss_ref,
    own_ref, from_full_ref, from_half_ref, sem,
):
    copies = fetches(place_ref, analysis_ref, own_ref, sem)
    for copy in copies:
        copy.start()
    grams = jnp.sum(grams_ref[...], axis=0)
    lane = iota((NBANDS, 128), 1)
    inside = lane < MEMBERS
    rows = []
    own_power = jnp.zeros((NBANDS, 128), F32)
    for i in range(JJ):
        shift = JJ * (i % 7)
        block = grams[NBANDS * (i // 7) : NBANDS * (i // 7) + NBANDS]
        block = pltpu.roll(block, 128 - shift, 1) if shift else block
        rows.append(jnp.where(lane < JJ, block, 0.0))
        own_power = own_power + jnp.where(lane == i, rows[i], 0.0)
    cotangent = cotangent_ref[...]
    scaled = cotangent * (16.0 * MEMBERS * NLAT)
    mixing = []
    score = jnp.zeros((NBANDS, 128), F32)
    beside = jnp.zeros((NBANDS, 128), F32)
    for i in range(MEMBERS):
        squared = rows[i][:, i : i + 1] + own_power - 2.0 * rows[i]
        distance = jnp.sqrt(jnp.maximum(squared, 0.0) + EPSILON)
        observed = distance[:, MEMBERS : MEMBERS + 1]
        pairs = jnp.where(inside, counts_ref[i : i + 1, :] * distance, 0.0)
        score = score + observed / MEMBERS - jnp.sum(pairs, axis=1, keepdims=True) / (
            2.0 * MEMBERS * PARTNERS
        )
        observed_weight = scaled[:, :1] / (MEMBERS * observed)
        pair_weight = scaled * symmetric_ref[i : i + 1, :] / (2.0 * MEMBERS * PARTNERS * distance)
        pair_weight = jnp.where(inside, pair_weight, 0.0)
        own = observed_weight - jnp.sum(pair_weight, axis=1, keepdims=True)
        mixing.append(pair_weight + jnp.where(lane == i, own, 0.0))
        beside = beside + jnp.where(lane == i, -observed_weight, 0.0)
    loss_ref[...] = score * cotangent

    size = MEMBERS * GROUP
    widen = (iota((128, size), 0) == (iota((128, size), 1) >> 4)).astype(F32).astype(BF)
    mix_high, mix_low = split2(jnp.concatenate(mixing, axis=0))
    mix_high = dot(mix_high, widen).astype(BF)
    mix_low = dot(mix_low, widen).astype(BF)
    beside = jnp.concatenate([beside, jnp.zeros((128 - NBANDS, 128), F32)], axis=0)
    beside_high, beside_low = split2(beside)
    same_member = (iota((size, size), 0) >> 4) == (iota((size, size), 1) >> 4)
    band_of_column = (iota((size, size), 1) & 15).astype(F32)
    same_degree = (iota((size, size), 0) & 15) == (iota((size, size), 1) & 15)
    band_of_lane = iota((GROUP, 128), 1).astype(F32)

    def mix(g, carry):
        start = pl.multiple_of(g * GROUP, GROUP)
        bands = band_column(target_ref, start, GROUP)
        column = jnp.concatenate([jnp.broadcast_to(bands, (GROUP, size))] * MEMBERS, axis=0)
        pick = (same_member & (column == band_of_column)).astype(F32).astype(BF)
        high = jnp.where(same_degree, dot(pick, mix_high), 0.0).astype(BF)
        low = jnp.where(same_degree, dot(pick, mix_low), 0.0).astype(BF)
        one_hot = (jnp.broadcast_to(bands, (GROUP, 128)) == band_of_lane).astype(F32).astype(BF)
        weights = dot(one_hot, beside_high) + dot(one_hot, beside_low)
        weights = jnp.concatenate(
            [jnp.broadcast_to(weights[:, i : i + 1], (GROUP, 128)) for i in range(MEMBERS)], axis=0
        )
        block = stacked_ref[0:MEMBERS, pl.ds(start, GROUP), :].reshape(size, WIDE)
        own = stacked_ref[MEMBERS, pl.ds(start, GROUP), :].astype(F32)
        grad = dot(high, block) + dot(low, block)
        for slot in range(3):
            lanes = slice(128 * slot, 128 * slot + 128)
            part = grad[:, lanes] + weights * jnp.concatenate([own[:, lanes]] * MEMBERS, axis=0)
            grad_ref[:, pl.ds(start, GROUP), lanes] = part.astype(BF).reshape(MEMBERS, GROUP, 128)
        return carry

    lax.fori_loop(0, NGROUPS, mix, 0, unroll=2)
    for copy in copies:
        copy.wait()
    for n in range(4):
        choose = full_ref[...] if n < 2 else half_ref[n - 2]
        spread = dot(choose, own_ref[min(n, 2)], 0, 0)
        member = iota(spread.shape, 0) % 2
        for i in range(2):
            part = jnp.where(member == i, spread, 0.0).astype(BF)
            if n < 2:
                from_full_ref[n, i] = part
            else:
                from_half_ref[n - 2, i] = part

    def inverse(g, carry):
        for slot in range(3):
            grads = [jnp.concatenate(grads_of(grad_ref, g, i, slot), axis=1) for i in range(2)]
            from_ref = from_full_ref.at[slot] if slot < 2 else from_half_ref.at[0]
            parts = halves(dot(from_ref[0], grads[0]) + dot(from_ref[1], grads[1]))
            if slot == 2:
                from_ref = from_half_ref.at[1]
                other = halves(dot(from_ref[0], grads[0]) + dot(from_ref[1], grads[1]))
                parts = [parts[k] + swap_halves(other[k]) for k in range(2)]
            start, count = STARTS[slot], COUNTS[slot]
            for k in range(2):
                part = parts[k].reshape(16, count, 128).astype(BF)
                back_ref[:, 2 * g + k, start : start + count, :] = part
        return carry

    lax.fori_loop(0, 4, inverse, 0)


def grads_of(grad_ref, g, i, slot):
    lanes = slice(128 * slot, 128 * slot + 128)
    return [grad_ref[4 * g + 2 * k + i, :, lanes] for k in range(2)]


def gradient(place, analysis, stacked, target, grams, counts, symmetric, cotangent, full, half):
    return pl.pallas_call(
        gradient_kernel,
        out_shape=[
            jax.ShapeDtypeStruct((16, 8, 104, 128), BF),
            jax.ShapeDtypeStruct((MEMBERS, L, WIDE), BF),
            jax.ShapeDtypeStruct((NBANDS, 128), F32),
        ],
        in_specs=[SMEM, ANY] + [VMEM] * 8,
        out_specs=[VMEM] * 3,
        scratch_shapes=[
            pltpu.VMEM((3, NLAT, L), BF),
            pltpu.VMEM((2, 2, 640, L), BF),
            pltpu.VMEM((2, 2, WIDE, L), BF),
            pltpu.SemaphoreType.DMA((3,)),
        ],
        compiler_params=pltpu.CompilerParams(vmem_limit_bytes=VMEM_LIMIT),
        cost_estimate=pl.CostEstimate(
            flops=10_000_000_000, bytes_accessed=12_000_000, transcendentals=0
        ),
        name="gradient",
    )(place, analysis, stacked, target, grams, counts, symmetric, cotangent, full, half)


def weight_kernel(
    place_ref, rows_ref, grad_ref, full_ref, half_ref, weight_ref, full_sum_ref, half_sum_ref
):
    full_sum_ref[...] = jnp.zeros_like(full_sum_ref)
    half_sum_ref[...] = jnp.zeros_like(half_sum_ref)

    def step(g, carry):
        for slot in range(3):
            values = two_rows_of(rows_ref, g, slot)
            member = iota((values.shape[0], L), 0) % 2
            sides = [[grads_of(grad_ref, g, i, slot) for i in range(2)]]
            if slot == 2:
                sides.append(
                    [[swap_halves(x.astype(F32)).astype(BF) for x in pair] for pair in sides[0]]
                )
            for h, side in enumerate(sides):
                grads = [jnp.concatenate(side[i], axis=1) for i in range(2)]
                terms = jnp.where(
                    member == 0, dot(values, grads[0], 1, 1), dot(values, grads[1], 1, 1)
                )
                if slot < 2:
                    full_sum_ref[slot] += terms
                else:
                    half_sum_ref[h] += terms
        return carry

    lax.fori_loop(0, 4, step, 0)
    for slot in range(3):
        if slot < 2:
            parts = split2(full_sum_ref[slot])
            weight = dot(full_ref[...], parts[0]) + dot(full_ref[...], parts[1])
        else:
            weight = jnp.zeros((NLAT, L), F32)
            for h in range(2):
                parts = split2(half_sum_ref[h])
                weight = weight + dot(half_ref[h], parts[0]) + dot(half_ref[h], parts[1])
        weight = weight * WEIGHT_RATIO
        for c in range(16):
            other = jnp.bitwise_xor(place_ref[2], c // 8)
            step_to = jnp.bitwise_xor(place_ref[1], c % 8)
            weight_ref[other, step_to, slot] = weight[20 * c : 20 * c + 20].astype(BF)


def weights(place, rows, grads, full, half):
    return pl.pallas_call(
        weight_kernel,
        out_shape=jax.ShapeDtypeStruct((2, 8, 3, 20, L), BF),
        in_specs=[SMEM] + [VMEM] * 4,
        out_specs=VMEM,
        scratch_shapes=[
            pltpu.VMEM((2, 640, L), F32),
            pltpu.VMEM((2, WIDE, L), F32),
        ],
        compiler_params=pltpu.CompilerParams(vmem_limit_bytes=VMEM_LIMIT),
        cost_estimate=pl.CostEstimate(
            flops=5_000_000_000, bytes_accessed=8_000_000, transcendentals=0
        ),
        name="weights",
    )(place, rows, grads, full, half)


def finish_kernel(place_ref, *refs):
    *r_refs, o_ref, order_ref = refs
    for k in range(8):
        order_ref[jnp.bitwise_xor(place_ref[1], k)] = r_refs[k][...]
    for e in range(8):
        o_ref[:, e, :] = order_ref[e, 0].astype(F32)
        o_ref[:, 8 + e, :] = order_ref[e, 1].astype(F32)
    for p in range(4):
        o_ref[:, 16 + p, :] = order_ref[2 * p, 2].astype(F32) + order_ref[2 * p + 1, 2].astype(F32)


def finish(place, received):
    return pl.pallas_call(
        finish_kernel,
        out_shape=jax.ShapeDtypeStruct((20, 20, L), F32),
        in_specs=[SMEM] + [VMEM] * 8,
        out_specs=VMEM,
        scratch_shapes=[pltpu.VMEM((8, 3, 20, L), BF)],
        name="finish",
    )(place, *received)


def exchange(x, axes):
    return lax.all_to_all(x, axes, split_axis=0, concat_axis=0, tiled=True)


def swap(blocks):
    return [blocks[0]] + [
        lax.ppermute(blocks[k], ENS, [(e, e ^ k) for e in range(8)]) for k in range(1, 8)
    ]


def travel(x):
    moved = exchange(x.reshape(128, 52, 2, 128), EVERY)
    return moved.reshape(16, 8, 104, 128)


def body(fourier, analysis, target, band_ids, partners, band_cotangent):
    place = jnp.stack([lax.axis_index(ORDER), lax.axis_index(ENS), lax.axis_index("dp")])
    place = place.astype(jnp.int32)
    full = jnp.asarray(FULL, BF)
    half = jnp.asarray(HALF, BF)
    by_order = jnp.transpose(analysis, (1, 0, 2))
    native = jnp.transpose(fourier[0].reshape(2, 20, 320, 128), (1, 2, 0, 3)).reshape(20, 640, 128)
    packed = pack(native)
    target_in, packed = lax.optimization_barrier((target[0], packed))
    rows = travel(packed)
    targets = swap(target_blocks(place, target_in, band_ids))
    stacked, observed, grams = spectra(place, by_order, rows, targets, full, half)
    grams = exchange(jnp.broadcast_to(grams, (16, *grams.shape)), ORDER).sum(axis=0)
    grams = exchange(jnp.broadcast_to(grams, (8, *grams.shape)), ENS)
    member_ids = jnp.arange(128, dtype=jnp.int32)
    counts = jnp.sum((partners[:, :, None] == member_ids[None, None, :]).astype(F32), axis=1)
    square = counts[:, :MEMBERS]
    symmetric = jnp.pad(square + square.T, ((0, 0), (0, 128 - MEMBERS)))
    cotangent = lax.dynamic_slice_in_dim(band_cotangent, lax.axis_index("dp"), 1, 0)[0]
    cotangent = jnp.broadcast_to(cotangent[:, None], (NBANDS, 128))
    back, grads, loss = gradient(
        place, by_order, stacked, observed, grams, counts, symmetric, cotangent, full, half
    )
    returned = travel(back)
    weight = weights(place, rows, grads, full, half)
    beside = lax.ppermute(weight[1], "dp", [(0, 1), (1, 0)])
    weight = (weight[0].astype(F32) + beside.astype(F32)).astype(BF)
    grad_analysis = finish(place, swap([weight[k] for k in range(8)]))
    loss_bands = lax.psum(loss[:, 0], "dp")
    native_grad = unpack(returned).reshape(20, 320, 2, 128)
    grad_fourier = jnp.transpose(native_grad, (2, 0, 1, 3)).reshape(1, 2, 20, 40960)
    return (grad_fourier, grad_analysis, loss_bands)


def solution(mesh):
    torus = Mesh(
        mesh.devices.reshape(mesh.shape["dp"], 4, 4, 2, 4),
        ("dp", "order_0", "order_1", "ens_0", "ens_1"),
    )
    in_specs = (
        P("dp", ENS, ORDER, None),
        P(None, ORDER, None),
        P("dp", ENS, ORDER),
        P(ENS, ORDER),
        P(),
        P(),
    )
    out_specs = (P("dp", ENS, ORDER, None), P(DP_ENS, ORDER, None), P())
    return jax.shard_map(body, mesh=torus, in_specs=in_specs, out_specs=out_specs, check_vma=False)
```

time: 354 us -> 301 us (0.85)
  waiting for transfers between devices: 164 us -> 122 us
  Pallas kernels: 88.5 us -> 65.2 us
  blocking collectives: 41.1 us -> 21.8 us
  starting transfers between devices: 48.4 us -> 65.6 us
  local copies, waits for them, and re-layouts: 8.6 us -> 19.3 us
    all_to_all x4 -> x3, waiting for transfers between devices: 164 us -> 10.9 us  [exchange(): return lax.all_to_all(x, axes, split_axis=0, concat_axis=0, tiled=True)]
    ppermute x0 -> x15, waiting for transfers between devices: none -> 111 us  [the longest x14 109 us: swap(): lax.ppermute(blocks[k], ENS, [(e, e ^ k) for e in range(8)])]
    ppermute x0 -> x15, starting transfers between devices: none -> 37.6 us  [the longest x14 37.5 us: swap(): lax.ppermute(blocks[k], ENS, [(e, e ^ k) for e in range(8)])]
    all_to_all x4 -> x3, starting transfers between devices: 48.4 us -> 28 us  [exchange(): return lax.all_to_all(x, axes, split_axis=0, concat_axis=0, tiled=True)]
    all_to_all x2 -> x1, blocking collectives: 38.1 us -> 18.9 us  [exchange(): return lax.all_to_all(x, axes, split_axis=0, concat_axis=0, tiled=True)]
    pallas_call x1, Pallas kernels: 33.3 us -> 19 us  [gradient(): pl.pallas_call(gradient_kernel, out_shape=[jax.ShapeDtypeStruct((16, 8, 1...]
    unnamed x18 -> x62, local copies, waits for them, and re-layouts: 5.74 us -> 17.7 us
    pallas_call x1, Pallas kernels: 28.9 us -> 17.4 us  [spectra(): pl.pallas_call(spectra_kernel, out_shape=[jax.ShapeDtypeStruct((JJ, L, WI...]
  transfers between devices with their start and end apart: 4 -> 18, of which waited for: 4 -> 10; matrix products, arithmetic and copies ran while one was open for 0% -> 1% of each run, Pallas kernels for 4% -> 5%
where the time goes in v2:
time: 301 us; the launch traced here: 296 us
  waiting for transfers between devices  122 us (41%)
  starting transfers between devices  65.6 us (22%)
  Pallas kernels  65.2 us (22%)
  blocking collectives  21.8 us (7%)
  local copies, waits for them, and re-layouts  19.3 us (6%)
    ppermute x14, waiting for transfers between devices, swap(): lax.ppermute(blocks[k], ENS, [(e, e ^ k) for e in range(8)])  109 us
    ppermute x14, starting transfers between devices, swap(): lax.ppermute(blocks[k], ENS, [(e, e ^ k) for e in range(8)])  37.5 us
    all_to_all x3, starting transfers between devices, exchange(): return lax.all_to_all(x, axes, split_axis=0, concat_axis=0, tiled=True)  28 us
    pallas_call x1, Pallas kernels, gradient(): pl.pallas_call(gradient_kernel, out_shape=[jax.ShapeDtypeStruct((16, 8, 1...  19 us
    all_to_all x1, blocking collectives, exchange(): return lax.all_to_all(x, axes, split_axis=0, concat_axis=0, tiled=True)  18.9 us
    unnamed x62, local copies, waits for them, and re-layouts  17.7 us
    pallas_call x1, Pallas kernels, spectra(): pl.pallas_call(spectra_kernel, out_shape=[jax.ShapeDtypeStruct((JJ, L, WI...  17.4 us
    all_to_all x3, waiting for transfers between devices, exchange(): return lax.all_to_all(x, axes, split_axis=0, concat_axis=0, tiled=True)  10.9 us
  transfers between devices with their start and end apart: 18, of which 10 were waited for; matrix products, arithmetic and copies ran while one was open for 1% of the time, Pallas kernels for 5%

profile of v2, /device:TPU:8, one launch (start us, length us, event | category | flops | bytes accessed | tf_op | source)
XLA Modules:
  0.0 296.3 jit_solution(113452029460182966)
XLA Ops:
  0.6 7.9 %pack.1 = bf16[16,8,104,128]{3,2,1,0:T(8,128)(2,1)} custom-call(bf16[20,640,128]{2,1,0:T(8,128)(2,1)} %bitcast.52, bf16[320,320]{1,0:T(8,128)(2,1)} %constant.43.clone.whole_ref, bf16[2,96,160]{2,1,0:T(8,128)(2,1)} %constant.44.clone.half_ref), custom_call_target="tpu_custom_call" | custom-call | tf_op jit(solution)/shard_map/pack/pallas_call | solution.py:143
  8.5 15.5 %all-to-all-start = ((bf16[128,52,2,128]{3,2,1,0:T(2,128)(2,1)}), bf16[128,52,2,128]{3,2,1,0:T(2,128)(2,1)S(1)}, u32[]{:S(2)}, u32[]{:S(2)}) async-start(bf16[128,52,2,128]{3,2,1,0:T(2,128)(2,1)} %bitcast.51), calls=%async_computation | async-start | bytes 6815744 | tf_op jit(solution)/shard_map/all_to_all | solution.py:557
  24.0 0.7 copy.28.band_ref
  24.7 0.6 pad_add_fusion.place_ref
  25.3 1.7 target_blocks.1
  27.0 1.5 collective-permute-start
  28.5 2.7 collective-permute-start.1
  31.8 5.4 %collective-permute-start.3 = (bf16[40,384]{1,0:T(8,128)(2,1)}, bf16[40,384]{1,0:T(8,128)(2,1)S(1)}, u32[]{:S(2)}, u32[]{:S(2)}) collective-permute-start(bf16[40,384]{1,0:T(8,128)(2,1)} %get-tuple-element.25), channel_id=1, source_target_pairs={{0,4},{1,5},{2,6},{3,7},{4,0},{5,1},{6,2},{7,3},{8,12},{9,13},{10,... | collective-permute-start | bytes 92168 | tf_op jit(solution)/shard_map/ppermute | solution.py:562
  37.4 8.7 %collective-permute-start.5 = (bf16[40,384]{1,0:T(8,128)(2,1)}, bf16[40,384]{1,0:T(8,128)(2,1)S(1)}, u32[]{:S(2)}, u32[]{:S(2)}) collective-permute-start(bf16[40,384]{1,0:T(8,128)(2,1)} %get-tuple-element.27), channel_id=1, source_target_pairs={{0,6},{1,7},{2,4},{3,5},{4,2},{5,3},{6,0},{7,1},{8,14},{9,15},{10,... | collective-permute-start | bytes 92168 | tf_op jit(solution)/shard_map/ppermute | solution.py:562
  46.7 55.9 %collective-permute-done.3.refs_4_ = bf16[40,384]{1,0:T(8,128)(2,1)S(1)} collective-permute-done((bf16[40,384]{1,0:T(8,128)(2,1)}, bf16[40,384]{1,0:T(8,128)(2,1)S(1)}, u32[]{:S(2)}, u32[]{:S(2)}) %collective-permute-start.3) | collective-permute-done | bytes 30752 | tf_op jit(solution)/shard_map/ppermute | solution.py:562
  103.5 0.6 copy-done.7
  104.1 2.5 collective-permute-done.5.refs_6_
  107.9 0.6 copy-done.2
  108.5 0.8 copy-done.4
  109.3 0.8 copy-done.6
  110.0 0.8 copy-done.8
  110.8 0.8 copy-done.10
  111.5 0.8 copy-done.12
  112.3 1.0 copy-done.13
  113.3 1.0 copy-done.16
  114.3 17.4 %spectra.1 = (bf16[17,320,384]{2,1,0:T(8,128)(2,1)}, bf16[320,384]{1,0:T(8,128)(2,1)S(1)}, f32[48,128]{1,0:T(8,128)S(1)}) custom-call(s32[3]{0:T(128)S(1)} %copy-done.2, bf16[20,320,320]{2,1,0:T(8,128)(2,1)} %bitcast.55, bf16[16,8,104,128]{3,2,1,0:T(8,128)(2,1)S(1)} %bitcast.47, bf16[320,640]{1,0:T(8,128)(2,1)S(1)} %copy-done.16, ...), custom_call_target="tpu_custom_call" | custom-call | flops 10000000000 | bytes 12000000 | tf_op jit(solution)/shard_map/spectra/pallas_call | solution.py:313
  131.7 0.6 copy-done.19
  132.4 18.9 %all_to_all.20 = f32[16,48,128]{2,1,0:T(8,128)} all-to-all(f32[16,48,128]{2,1,0:T(8,128)S(1)} %broadcast_in_dim.15), channel_id=1, replica_groups=mesh['dp'=2,'order_0'=4,'order_1'=4,'ens_0'=2,'ens_1'=4] {'order_0','ord..., dimensions={0} | all-to-all | bytes 786432 | tf_op jit(solution)/shard_map/all_to_all | solution.py:557
  151.2 1.0 reduce_sum.18
  152.3 0.7 broadcast_in_dim.16
  153.0 4.6 %all-to-all-start.2 = ((f32[8,48,128]{2,1,0:T(8,128)}), f32[8,48,128]{2,1,0:T(8,128)}, u32[]{:S(2)}, u32[]{:S(2)}) async-start(f32[8,48,128]{2,1,0:T(8,128)} %broadcast_in_dim.16), calls=%async_computation.2 | async-start | bytes 393216 | tf_op jit(solution)/shard_map/all_to_all | solution.py:557
  157.7 10.9 %all-to-all-done.2.grams_ref = f32[8,48,128]{2,1,0:T(8,128)} async-done(((f32[8,48,128]{2,1,0:T(8,128)}), f32[8,48,128]{2,1,0:T(8,128)}, u32[]{:S(2)}, u32[]{:S(2)}) %all-to-all-start.2) | async-done | bytes 196640 | tf_op jit(solution)/shard_map/all_to_all | solution.py:557
  168.7 1.0 copy-done.14
  169.7 1.0 copy-done.17
  170.7 0.9 copy-done.20
  171.6 19.0 %gradient.1 = (bf16[16,8,104,128]{3,2,1,0:T(8,128)(2,1)S(1)}, bf16[16,320,384]{2,1,0:T(8,128)(2,1)}, f32[16,128]{1,0:T(8,128)S(1)}) custom-call(s32[3]{0:T(128)S(1)} %copy-done.3, bf16[20,320,320]{2,1,0:T(8,128)(2,1)} %bitcast.56, bf16[17,320,384]{2,1,0:T(8,128)(2,1)} %get-tuple-element.29.stacked_ref, bf16[320,384]{1,0:T(8,128)(2,1)S(1)} %copy-done.20, ...), custom_call_target="tpu_custom_call" | custom-call | flops 10000000000 | bytes 12000000 | tf_op jit(solution)/shard_map/gradient/pallas_call | solution.py:450
  190.7 1.8 copy-done.1
  192.4 8.0 %all-to-all-start.3 = ((bf16[128,52,2,128]{3,2,1,0:T(2,128)(2,1)}), bf16[128,52,2,128]{3,2,1,0:T(2,128)(2,1)}, u32[]{:S(2)}, u32[]{:S(2)}) async-start(bf16[128,52,2,128]{3,2,1,0:T(2,128)(2,1)} %bitcast.49), calls=%async_computation.3 | async-start | bytes 6815744 | tf_op jit(solution)/shard_map/all_to_all | solution.py:557
  200.4 1.0 copy-done.15
  201.4 1.0 copy-done.18
  202.4 9.6 %weights.1 = bf16[2,8,3,20,320]{4,3,2,1,0:T(8,128)(2,1)S(1)} custom-call(s32[3]{0:T(128)S(1)} %copy-done.3, bf16[16,8,104,128]{3,2,1,0:T(8,128)(2,1)S(1)} %bitcast.48, bf16[16,320,384]{2,1,0:T(8,128)(2,1)} %get-tuple-element.33.grad_ref, bf16[320,640]{1,0:T(8,128)(2,1)S(1)} %copy-done.18, bf16[2,320,384]{2,1,0:T(8,128)(2,1)S(1)} %copy-done.15), custom_call_target="tpu_custom_call" | custom-call | flops 5000000000 | bytes 8000000 | tf_op jit(solution)/shard_map/weights/pallas_call | solution.py:517
  212.2 1.8 collective-permute-done.7
  214.1 0.7 slice_bitcast_fusion.2
  214.8 7.5 %collective-permute-start.14 = (bf16[3,20,320]{2,1,0:T(8,128)(2,1)S(1)}, bf16[3,20,320]{2,1,0:T(8,128)(2,1)S(1)}, u32[]{:S(2)}, u32[]{:S(2)}) collective-permute-start(bf16[3,20,320]{2,1,0:T(8,128)(2,1)S(1)} %get-tuple-element.35), channel_id=1, source_target_pairs={{0,7},{1,6},{2,5},{3,4},{4,3},{5,2},{6,1},{7,0},{8,15},{9,14},{10,... | collective-permute-start | bytes 115208 | tf_op jit(solution)/shard_map/ppermute | solution.py:562
  222.3 0.8 collective-permute-start.13
  223.1 5.4 %collective-permute-start.12 = (bf16[3,20,320]{2,1,0:T(8,128)(2,1)S(1)}, bf16[3,20,320]{2,1,0:T(8,128)(2,1)S(1)}, u32[]{:S(2)}, u32[]{:S(2)}) collective-permute-start(bf16[3,20,320]{2,1,0:T(8,128)(2,1)S(1)} %get-tuple-element.37), channel_id=1, source_target_pairs={{0,5},{1,4},{2,7},{3,6},{4,1},{5,0},{6,3},{7,2},{8,13},{9,12},{10,... | collective-permute-start | bytes 115208 | tf_op jit(solution)/shard_map/ppermute | solution.py:562
  229.0 2.7 collective-permute-start.10
  231.7 48.1 %collective-permute-done.14.refs_7_ = bf16[3,20,320]{2,1,0:T(8,128)(2,1)S(1)} collective-permute-done((bf16[3,20,320]{2,1,0:T(8,128)(2,1)S(1)}, bf16[3,20,320]{2,1,0:T(8,128)(2,1)S(1)}, u32[]{:S(2)}, u32[]{:S(2)}) %collective-permute-start.14) | collective-permute-done | bytes 38432 | tf_op jit(solution)/shard_map/ppermute | solution.py:562
  279.9 0.9 collective-permute-start.9
  280.8 1.1 collective-permute-done.13.refs_6_
  282.0 3.0 %psum.7 = f32[16]{0:T(128)} all-reduce(f32[16]{0:T(128)S(1)} %slice_reduce_fusion), channel_id=1, replica_groups=mesh['dp'=2,'order_0'=4,'order_1'=4,'ens_0'=2,'ens_1'=4] {'dp'}, use_global_device_ids=true, to_apply=%region_2.3 | all-reduce | flops 16 | bytes 128 | tf_op jit(solution)/shard_map/psum | solution.py:599
  286.6 2.1 finish.1
  288.8 7.5 %unpack.1 = bf16[20,640,128]{2,1,0:T(8,128)(2,1)} custom-call(bf16[16,8,104,128]{3,2,1,0:T(8,128)(2,1)} %bitcast.13.y_ref, bf16[320,320]{1,0:T(8,128)(2,1)} %constant.45.clone.whole_ref, bf16[2,160,96]{2,1,0:T(8,128)(2,1)} %constant.46.clone.half_ref), custom_call_target="tpu_custom_call" | custom-call | tf_op jit(solution)/shard_map/unpack/pallas_call | solution.py:154
  (72 shorter events, 6.4 us)
Async XLA Ops:
  0.6 157.1 %copy-start = (f32[2,16]{1,0:T(2,128)S(1)}, f32[2,16]{1,0:T(2,128)}, u32[]{:S(2)}) copy-start(f32[2,16]{1,0:T(2,128)} %param.17) | copy-start | bytes 388
  8.5 15.5 %copy-start.28 = (s32[40,20]{0,1:T(8,128)S(1)}, s32[40,20]{0,1:T(8,128)}, u32[]{:S(2)}) copy-start(s32[40,20]{0,1:T(8,128)} %param.15) | copy-start | bytes 9604
  8.5 99.4 %all-to-all-start = ((bf16[128,52,2,128]{3,2,1,0:T(2,128)(2,1)}), bf16[128,52,2,128]{3,2,1,0:T(2,128)(2,1)S(1)}, u32[]{:S(2)}, u32[]{:S(2)}) async-start(bf16[128,52,2,128]{3,2,1,0:T(2,128)(2,1)} %bitcast.51), calls=%async_computation | async-start | bytes 6815744 | tf_op jit(solution)/shard_map/all_to_all | solution.py:557
  27.0 10.4 %collective-permute-start = (bf16[40,384]{1,0:T(8,128)(2,1)}, bf16[40,384]{1,0:T(8,128)(2,1)S(1)}, u32[]{:S(2)}, u32[]{:S(2)}) collective-permute-start(bf16[40,384]{1,0:T(8,128)(2,1)} %get-tuple-element.22), channel_id=1, source_target_pairs={{0,1},{1,0},{2,3},{3,2},{4,5},{5,4},{6,7},{7,6},{8,9},{9,8},{10,11... | collective-permute-start | bytes 92168 | tf_op jit(solution)/shard_map/ppermute | solution.py:562
  28.5 17.6 %collective-permute-start.1 = (bf16[40,384]{1,0:T(8,128)(2,1)}, bf16[40,384]{1,0:T(8,128)(2,1)S(1)}, u32[]{:S(2)}, u32[]{:S(2)}) collective-permute-start(bf16[40,384]{1,0:T(8,128)(2,1)} %get-tuple-element.23), channel_id=1, source_target_pairs={{0,2},{1,3},{2,0},{3,1},{4,6},{5,7},{6,4},{7,5},{8,10},{9,11},{10,... | collective-permute-start | bytes 92168 | tf_op jit(solution)/shard_map/ppermute | solution.py:562
  31.2 15.4 %collective-permute-start.2 = (bf16[40,384]{1,0:T(8,128)(2,1)}, bf16[40,384]{1,0:T(8,128)(2,1)S(1)}, u32[]{:S(2)}, u32[]{:S(2)}) collective-permute-start(bf16[40,384]{1,0:T(8,128)(2,1)} %get-tuple-element.24), channel_id=1, source_target_pairs={{0,3},{1,2},{2,1},{3,0},{4,7},{5,6},{6,5},{7,4},{8,11},{9,10},{10,... | collective-permute-start | bytes 92168 | tf_op jit(solution)/shard_map/ppermute | solution.py:562
  31.8 70.8 %collective-permute-start.3 = (bf16[40,384]{1,0:T(8,128)(2,1)}, bf16[40,384]{1,0:T(8,128)(2,1)S(1)}, u32[]{:S(2)}, u32[]{:S(2)}) collective-permute-start(bf16[40,384]{1,0:T(8,128)(2,1)} %get-tuple-element.25), channel_id=1, source_target_pairs={{0,4},{1,5},{2,6},{3,7},{4,0},{5,1},{6,2},{7,3},{8,12},{9,13},{10,... | collective-permute-start | bytes 92168 | tf_op jit(solution)/shard_map/ppermute | solution.py:562
  37.1 66.3 %collective-permute-start.4 = (bf16[40,384]{1,0:T(8,128)(2,1)}, bf16[40,384]{1,0:T(8,128)(2,1)S(1)}, u32[]{:S(2)}, u32[]{:S(2)}) collective-permute-start(bf16[40,384]{1,0:T(8,128)(2,1)} %get-tuple-element.26), channel_id=1, source_target_pairs={{0,5},{1,4},{2,7},{3,6},{4,1},{5,0},{6,3},{7,2},{8,13},{9,12},{10,... | collective-permute-start | bytes 92168 | tf_op jit(solution)/shard_map/ppermute | solution.py:562
  37.4 69.2 %collective-permute-start.5 = (bf16[40,384]{1,0:T(8,128)(2,1)}, bf16[40,384]{1,0:T(8,128)(2,1)S(1)}, u32[]{:S(2)}, u32[]{:S(2)}) collective-permute-start(bf16[40,384]{1,0:T(8,128)(2,1)} %get-tuple-element.27), channel_id=1, source_target_pairs={{0,6},{1,7},{2,4},{3,5},{4,2},{5,3},{6,0},{7,1},{8,14},{9,15},{10,... | collective-permute-start | bytes 92168 | tf_op jit(solution)/shard_map/ppermute | solution.py:562
  46.1 61.1 %collective-permute-start.6 = (bf16[40,384]{1,0:T(8,128)(2,1)}, bf16[40,384]{1,0:T(8,128)(2,1)S(1)}, u32[]{:S(2)}, u32[]{:S(2)}) collective-permute-start(bf16[40,384]{1,0:T(8,128)(2,1)} %get-tuple-element.28), channel_id=1, source_target_pairs={{0,7},{1,6},{2,5},{3,4},{4,3},{5,2},{6,1},{7,0},{8,15},{9,14},{10,... | collective-permute-start | bytes 92168 | tf_op jit(solution)/shard_map/ppermute | solution.py:562
  102.6 0.6 copy-start.5
  103.5 0.6 copy-start.7
  106.6 0.6 copy-start.9
  107.2 0.6 copy-start.11
  107.9 0.6 copy-start.2
  108.5 0.8 copy-start.4
  109.3 0.8 copy-start.6
  110.0 0.8 copy-start.8
  110.8 0.8 copy-start.10
  111.5 0.8 copy-start.12
  112.3 1.0 copy-start.13
  113.3 1.0 copy-start.16
  114.3 43.2 %copy-start.29 = (s32[16,4]{0,1:T(4,128)S(1)}, s32[16,4]{0,1:T(4,128)}, u32[]{:S(2)}) copy-start(s32[16,4]{0,1:T(4,128)} %param.16) | copy-start | bytes 772
  114.3 54.4 %copy-start.3 = (s32[3]{0:T(128)S(1)}, s32[3]{0:T(128)}, u32[]{:S(2)}) copy-start(s32[3]{0:T(128)} %pad_add_fusion.place_ref) | copy-start | bytes 40
  131.7 0.7 copy-start.19
  153.0 15.6 %all-to-all-start.2 = ((f32[8,48,128]{2,1,0:T(8,128)}), f32[8,48,128]{2,1,0:T(8,128)}, u32[]{:S(2)}, u32[]{:S(2)}) async-start(f32[8,48,128]{2,1,0:T(8,128)} %broadcast_in_dim.16), calls=%async_computation.2 | async-start | bytes 393216 | tf_op jit(solution)/shard_map/all_to_all | solution.py:557
  168.7 1.0 copy-start.14
  169.7 1.0 copy-start.17
  170.7 0.9 copy-start.20
  190.7 1.8 copy-start.1
  192.4 96.4 %all-to-all-start.3 = ((bf16[128,52,2,128]{3,2,1,0:T(2,128)(2,1)}), bf16[128,52,2,128]{3,2,1,0:T(2,128)(2,1)}, u32[]{:S(2)}, u32[]{:S(2)}) async-start(bf16[128,52,2,128]{3,2,1,0:T(2,128)(2,1)} %bitcast.49), calls=%async_computation.3 | async-start | bytes 6815744 | tf_op jit(solution)/shard_map/all_to_all | solution.py:557
  200.4 1.0 copy-start.15
  201.4 1.0 copy-start.18
  212.1 1.9 collective-permute-start.7
  214.8 65.1 %collective-permute-start.14 = (bf16[3,20,320]{2,1,0:T(8,128)(2,1)S(1)}, bf16[3,20,320]{2,1,0:T(8,128)(2,1)S(1)}, u32[]{:S(2)}, u32[]{:S(2)}) collective-permute-start(bf16[3,20,320]{2,1,0:T(8,128)(2,1)S(1)} %get-tuple-element.35), channel_id=1, source_target_pairs={{0,7},{1,6},{2,5},{3,4},{4,3},{5,2},{6,1},{7,0},{8,15},{9,14},{10,... | collective-permute-start | bytes 115208 | tf_op jit(solution)/shard_map/ppermute | solution.py:562
  222.3 59.6 %collective-permute-start.13 = (bf16[3,20,320]{2,1,0:T(8,128)(2,1)S(1)}, bf16[3,20,320]{2,1,0:T(8,128)(2,1)S(1)}, u32[]{:S(2)}, u32[]{:S(2)}) collective-permute-start(bf16[3,20,320]{2,1,0:T(8,128)(2,1)S(1)} %get-tuple-element.36), channel_id=1, source_target_pairs={{0,6},{1,7},{2,4},{3,5},{4,2},{5,3},{6,0},{7,1},{8,14},{9,15},{10,... | collective-permute-start | bytes 115208 | tf_op jit(solution)/shard_map/ppermute | solution.py:562
  223.1 61.8 %collective-permute-start.12 = (bf16[3,20,320]{2,1,0:T(8,128)(2,1)S(1)}, bf16[3,20,320]{2,1,0:T(8,128)(2,1)S(1)}, u32[]{:S(2)}, u32[]{:S(2)}) collective-permute-start(bf16[3,20,320]{2,1,0:T(8,128)(2,1)S(1)} %get-tuple-element.37), channel_id=1, source_target_pairs={{0,5},{1,4},{2,7},{3,6},{4,1},{5,0},{6,3},{7,2},{8,13},{9,12},{10,... | collective-permute-start | bytes 115208 | tf_op jit(solution)/shard_map/ppermute | solution.py:562
  228.5 56.5 %collective-permute-start.11 = (bf16[3,20,320]{2,1,0:T(8,128)(2,1)S(1)}, bf16[3,20,320]{2,1,0:T(8,128)(2,1)S(1)}, u32[]{:S(2)}, u32[]{:S(2)}) collective-permute-start(bf16[3,20,320]{2,1,0:T(8,128)(2,1)S(1)} %get-tuple-element.38), channel_id=1, source_target_pairs={{0,4},{1,5},{2,6},{3,7},{4,0},{5,1},{6,2},{7,3},{8,12},{9,13},{10,... | collective-permute-start | bytes 115208 | tf_op jit(solution)/shard_map/ppermute | solution.py:562
  229.0 55.9 %collective-permute-start.10 = (bf16[3,20,320]{2,1,0:T(8,128)(2,1)S(1)}, bf16[3,20,320]{2,1,0:T(8,128)(2,1)S(1)}, u32[]{:S(2)}, u32[]{:S(2)}) collective-permute-start(bf16[3,20,320]{2,1,0:T(8,128)(2,1)S(1)} %get-tuple-element.39), channel_id=1, source_target_pairs={{0,3},{1,2},{2,1},{3,0},{4,7},{5,6},{6,5},{7,4},{8,11},{9,10},{10,... | collective-permute-start | bytes 115208 | tf_op jit(solution)/shard_map/ppermute | solution.py:562
  279.9 6.2 %copy-start.21 = (bf16[3,20,320]{2,1,0:T(8,128)(2,1)}, bf16[3,20,320]{2,1,0:T(8,128)(2,1)S(1)}, u32[]{:S(2)}) copy-start(bf16[3,20,320]{2,1,0:T(8,128)(2,1)S(1)} %collective-permute-done.14.refs_7_) | copy-start | bytes 115204
  279.9 5.7 %collective-permute-start.9 = (bf16[3,20,320]{2,1,0:T(8,128)(2,1)S(1)}, bf16[3,20,320]{2,1,0:T(8,128)(2,1)S(1)}, u32[]{:S(2)}, u32[]{:S(2)}) collective-permute-start(bf16[3,20,320]{2,1,0:T(8,128)(2,1)S(1)} %get-tuple-element.40), channel_id=1, source_target_pairs={{0,2},{1,3},{2,0},{3,1},{4,6},{5,7},{6,4},{7,5},{8,10},{9,11},{10,... | collective-permute-start | bytes 115208 | tf_op jit(solution)/shard_map/ppermute | solution.py:562
  281.9 4.2 %copy-start.22 = (bf16[3,20,320]{2,1,0:T(8,128)(2,1)}, bf16[3,20,320]{2,1,0:T(8,128)(2,1)S(1)}, u32[]{:S(2)}) copy-start(bf16[3,20,320]{2,1,0:T(8,128)(2,1)S(1)} %collective-permute-done.13.refs_6_) | copy-start | bytes 115204
  281.9 4.2 %collective-permute-start.8 = (bf16[3,20,320]{2,1,0:T(8,128)(2,1)S(1)}, bf16[3,20,320]{2,1,0:T(8,128)(2,1)S(1)}, u32[]{:S(2)}, u32[]{:S(2)}) collective-permute-start(bf16[3,20,320]{2,1,0:T(8,128)(2,1)S(1)} %get-tuple-element.41), channel_id=1, source_target_pairs={{0,1},{1,0},{2,3},{3,2},{4,5},{5,4},{6,7},{7,6},{8,9},{9,8},{10,11... | collective-permute-start | bytes 115208 | tf_op jit(solution)/shard_map/ppermute | solution.py:562
  285.0 1.1 copy-start.23
  285.0 1.1 copy-start.24
  285.0 1.1 copy-start.25
  285.5 0.6 copy-start.26
  286.0 0.6 copy-start.27

commit v3 on v2

--- a/solution.py
+++ b/solution.py
@@ -26,10 +26,10 @@
 GROUP = 16
 NGROUPS = L // GROUP
 WIDE = 384
-VMEM_LIMIT = 48 * 1024 * 1024
+MIB = 1024 * 1024
 VMEM = pl.BlockSpec(memory_space=pltpu.VMEM)
 SMEM = pl.BlockSpec(memory_space=pltpu.SMEM)
-ANY = pl.BlockSpec(memory_space=pl.ANY)
+HBM = pl.BlockSpec(memory_space=pltpu.HBM)
 
 
 def selections():
@@ -161,7 +161,8 @@
     )(y, jnp.asarray(WHOLE_ORDER.T, BF), jnp.asarray(HALF_ORDER.transpose(0, 2, 1), BF))
 
 
-def target_kernel(place_ref, t_ref, band_ref, *o_refs):
+def target_kernel(place_ref, t_ref, band_ref, *refs):
+    *o_refs, held_ref, sem = refs
     bands = jnp.broadcast_to(band_ref[:, 0:1].astype(F32), (40, 128))
     low = iota((40, 128), 1) < 64
     for k in range(8):
@@ -171,11 +172,16 @@
             return t_ref[:, pl.ds(pl.multiple_of(start, 128), 128)]
 
         middle = lanes(2048 + 128 * (e // 2)).astype(F32)
-        o_refs[k][:, 0:128] = lanes(128 * e)
-        o_refs[k][:, 128:256] = lanes(1024 + 128 * e)
+        held_ref[k, :, 0:128] = lanes(128 * e)
+        held_ref[k, :, 128:256] = lanes(1024 + 128 * e)
         odd = jnp.broadcast_to(e % 2, (40, 128)) == 1
         part = jnp.where(odd, swap_halves(middle), middle)
-        o_refs[k][:, 256:384] = jnp.where(low, part, bands).astype(BF)
+        held_ref[k, :, 256:384] = jnp.where(low, part, bands).astype(BF)
+    copies = [pltpu.make_async_copy(held_ref.at[k], o_refs[k], sem.at[k]) for k in range(8)]
+    for copy in copies:
+        copy.start()
+    for copy in copies:
+        copy.wait()
 
 
 def target_blocks(place, target, bands):
@@ -183,7 +189,9 @@
         target_kernel,
         out_shape=[jax.ShapeDtypeStruct((40, WIDE), BF)] * 8,
         in_specs=[SMEM, VMEM, VMEM],
-        out_specs=[VMEM] * 8,
+        out_specs=[HBM] * 8,
+        scratch_shapes=[pltpu.VMEM((8, 40, WIDE), BF), pltpu.SemaphoreType.DMA((8,))],
+        compiler_params=pltpu.CompilerParams(vmem_limit_bytes=63 * MIB),
         name="target_blocks",
     )(place, target, bands)
 
@@ -224,37 +232,134 @@
     return target_ref[pl.ds(start, count), 256:384].astype(F32)[:, 64:65]
 
 
-def spectra_kernel(place_ref, analysis_ref, rows_ref, full_ref, half_ref, *refs):
-    target_refs = refs[:8]
-    stacked_ref, target_ref, grams_ref = refs[8:11]
-    own_ref, to_full_ref, to_half_ref, terms_ref, order_ref, sem = refs[11:]
+def prepare_kernel(
+    place_ref, analysis_ref, full_ref, half_ref, other_row_ref, other_column_ref,
+    to_full_ref, to_half_ref, from_full_ref, from_half_ref, select_ref, to_mixing_ref, own_ref, sem,
+):
     copies = fetches(place_ref, analysis_ref, own_ref, sem)
     for copy in copies:
         copy.start()
+    def is_at(a, b):
+        n = (a >= 7).astype(jnp.int32) + (a >= 14).astype(jnp.int32)
+        return (iota((WIDE, 128), 0) == 128 * n + JJ * (a - 7 * n) + b).astype(F32)
+
+    lane = iota((WIDE, 128), 1)
+    who = lane & 15
+    other = jnp.broadcast_to(other_row_ref[0:1, :], (WIDE, 128))
+    select = is_at(who, who) + is_at(other, other) - 2.0 * is_at(who, other)
+    select_ref[...] = jnp.where(lane < 80, select, 0.0).astype(BF)
+    row, j = iota((128, 128), 0), iota((128, 128), 1)
+    who, other = row & 15, other_column_ref[...]
+    pair = (row >= 16) & (row < 80)
+    for i in range(MEMBERS):
+        own = (j == i).astype(F32)
+        value = jnp.where(pair & (who == i), (other == j).astype(F32) - own, 0.0)
+        value = value + jnp.where(pair & (other == i), (who == j).astype(F32) - own, 0.0)
+        value = value + jnp.where((row < 16) & (who == i), own, 0.0)
+        to_mixing_ref[:, 128 * i : 128 * i + 128] = value.astype(BF)
+    for copy in copies:
+        copy.wait()
+    for n in range(4):
+        choose = full_ref[...] if n < 2 else half_ref[n - 2]
+        own = own_ref[min(n, 2)]
+        to_ref = to_full_ref.at[n] if n < 2 else to_half_ref.at[n - 2]
+        from_ref = from_full_ref.at[n] if n < 2 else from_half_ref.at[n - 2]
+        spread = dot(own, choose, 0, 0)
+        member = iota(spread.shape, 1) % 2
+        for i in range(2):
+            to_ref[i] = jnp.where(member == i, spread, 0.0).astype(BF)
+        spread = dot(choose, own, 0, 0)
+        member = iota(spread.shape, 0) % 2
+        for i in range(2):
+            from_ref[i] = jnp.where(member == i, spread, 0.0).astype(BF)
+
+
+def prepare(place, analysis, full, half, partners):
+    other = jnp.concatenate(
+        [jnp.full((16,), MEMBERS, jnp.int32), partners.T.reshape(64), jnp.zeros((48,), jnp.int32)]
+    )
+    return pl.pallas_call(
+        prepare_kernel,
+        out_shape=[
+            jax.ShapeDtypeStruct((2, 2, L, 640), BF),
+            jax.ShapeDtypeStruct((2, 2, L, WIDE), BF),
+            jax.ShapeDtypeStruct((2, 2, 640, L), BF),
+            jax.ShapeDtypeStruct((2, 2, WIDE, L), BF),
+            jax.ShapeDtypeStruct((WIDE, 128), BF),
+            jax.ShapeDtypeStruct((128, MEMBERS * 128), BF),
+        ],
+        in_specs=[SMEM, HBM, VMEM, VMEM, VMEM, VMEM],
+        out_specs=[VMEM] * 6,
+        scratch_shapes=[pltpu.VMEM((3, NLAT, L), BF), pltpu.SemaphoreType.DMA((3,))],
+        compiler_params=pltpu.CompilerParams(vmem_limit_bytes=63 * MIB),
+        name="prepare",
+    )(
+        place, analysis, full, half,
+        jnp.broadcast_to(other[None], (8, 128)), jnp.broadcast_to(other[:, None], (128, 128)),
+    )
+
+
+def compact(x):
+    top, rest = x[:8], x[8:]
+    lane = iota((8, 128), 1)
+    first = jnp.where(lane < 80, top, pltpu.roll(rest, 80, 1))
+    left = pltpu.roll(rest, 80, 1)
+    lane = iota((1, 128), 1)
+    tails = []
+    for n in range(2):
+        tail = jnp.zeros((1, 128), F32)
+        for r in range(4):
+            row = pltpu.roll(left[4 * n + r : 4 * n + r + 1], 32 * r, 1)
+            tail = jnp.where((lane >= 32 * r) & (lane < 32 * r + 32), row, tail)
+        tails.append(tail)
+    return jnp.concatenate([first] + tails, axis=0)
+
+
+def expand(x):
+    first = x[:8]
+    lane = iota((8, 128), 1)
+    top = jnp.where(lane < 80, first, 0.0)
+    rows = []
+    for n in range(2):
+        for r in range(4):
+            rows.append(pltpu.roll(x[8 + n : 9 + n], (48 - 32 * r) % 128, 1))
+    rest = jnp.where(lane < 48, pltpu.roll(first, 48, 1), jnp.concatenate(rows, axis=0))
+    return jnp.concatenate([top, jnp.where(lane < 80, rest, 0.0)], axis=0)
+
+
+def spectra_kernel(place_ref, rows_hbm, to_full_hbm, to_half_hbm, select_hbm, *refs):
+    target_refs = refs[:8]
+    stacked_hbm, target_hbm, sums_hbm = refs[8:11]
+    to_full_ref, to_half_ref, select_ref, stacked_ref, target_ref, sums_ref = refs[11:17]
+    rows_ref, terms_ref, order_ref, in_sem, rows_sem, target_sem, out_sem = refs[17:]
+
+    def load_rows(g):
+        where = pl.ds(2 * g, 2)
+        return pltpu.make_async_copy(rows_hbm.at[:, where], rows_ref.at[:, where], rows_sem.at[g])
+
+    load_rows(0).start()
+    loads = [pltpu.make_async_copy(to_full_hbm, to_full_ref, in_sem.at[0])]
+    loads.append(pltpu.make_async_copy(to_half_hbm, to_half_ref, in_sem.at[1]))
+    loads.append(pltpu.make_async_copy(select_hbm, select_ref, in_sem.at[2]))
     for k in range(8):
-        order_ref[jnp.bitwise_xor(place_ref[1], k)] = target_refs[k][...].astype(F32)
-    target_ref[...] = order_ref[...].reshape(L, WIDE).astype(BF)
-    for copy in copies:
+        there = order_ref.at[jnp.bitwise_xor(place_ref[1], k)]
+        loads.append(pltpu.make_async_copy(target_refs[k], there, target_sem.at[k]))
+    for copy in loads[:2]:
+        copy.start()
+    for g in range(1, 4):
+        load_rows(g).start()
+    for copy in loads[2:]:
+        copy.start()
+    for copy in loads[:2]:
         copy.wait()
     base = place_ref[0] * 20
     orders = [base + m for m in own_orders(place_ref)]
-    for n in range(4):
-        if n < 2:
-            spread = dot(own_ref[n], full_ref[...], 0, 0)
-        else:
-            spread = dot(own_ref[2], half_ref[n - 2], 0, 0)
-        member = iota(spread.shape, 1) % 2
-        for i in range(2):
-            part = jnp.where(member == i, spread, 0.0).astype(BF)
-            if n < 2:
-                to_full_ref[n, i] = part
-            else:
-                to_half_ref[n - 2, i] = part
     degree = iota((L, 128), 0)
     low = iota((L, 128), 1) < 64
     keeps = [degree >= orders[0], degree >= orders[1], (degree >= orders[2]) & low]
 
     def transform(g, carry):
+        load_rows(g).wait()
         for slot in range(3):
             values = two_rows_of(rows_ref, g, slot)
             for i in range(2):
@@ -268,13 +373,26 @@
                     stacked_ref[4 * g + 2 * k + i, :, 128 * slot : 128 * slot + 128] = jnp.where(
                         keeps[slot], parts[k], 0.0
                     ).astype(BF)
+        store(g).start()
         return carry
 
+    def store(g):
+        where = pl.ds(4 * g, 4)
+        return pltpu.make_async_copy(stacked_ref.at[where], stacked_hbm.at[where], out_sem.at[g])
+
     lax.fori_loop(0, 4, transform, 0)
+    for copy in loads[2:]:
+        copy.wait()
+    target_ref[...] = order_ref[...].astype(F32).reshape(L, WIDE).astype(BF)
+    stores = [pltpu.make_async_copy(target_ref, target_hbm, out_sem.at[4])]
     for slot in range(3):
         lanes = slice(128 * slot, 128 * slot + 128)
         observed = jnp.where(keeps[slot], target_ref[:, lanes].astype(F32), 0.0)
         stacked_ref[MEMBERS, :, lanes] = observed.astype(BF)
+    last = stacked_hbm.at[MEMBERS]
+    stores.append(pltpu.make_async_copy(stacked_ref.at[MEMBERS], last, out_sem.at[5]))
+    for copy in stores:
+        copy.start()
 
     size = MEMBERS * GROUP
     same = (iota((size, size), 0) & 15) == (iota((size, size), 1) & 15)
@@ -304,77 +422,89 @@
 
     column = jnp.broadcast_to(band_column(target_ref, 0, L), (L, 128))
     one_hot = (column == iota((L, 128), 1).astype(F32)).astype(F32).astype(BF)
+    squares = jnp.zeros((NBANDS, 128), F32)
     for n in range(3):
-        total = sum(dot(one_hot, part, 0, 0) for part in split3(terms_ref[n]))
-        grams_ref[NBANDS * n : NBANDS * n + NBANDS] = total[:NBANDS]
-
-
-def spectra(place, analysis, rows, targets, full, half):
+        total = sum(dot(one_hot, part, 0, 0) for part in split3(terms_ref[n]))[:NBANDS]
+        for part in split3(total):
+            squares = squares + dot(part, select_ref[128 * n : 128 * n + 128, :])
+    sums = compact(squares)
+    sums = jnp.concatenate([sums] * 4, axis=0)
+    sums_ref[...] = jnp.broadcast_to(sums[None], (32, 40, 128))
+    stores.append(pltpu.make_async_copy(sums_ref, sums_hbm, out_sem.at[6]))
+    stores[2].start()
+    for copy in stores:
+        copy.wait()
+    for g in range(4):
+        store(g).wait()
+
+
+def spectra(place, rows, to_full, to_half, select, targets):
     return pl.pallas_call(
         spectra_kernel,
         out_shape=[
             jax.ShapeDtypeStruct((JJ, L, WIDE), BF),
             jax.ShapeDtypeStruct((L, WIDE), BF),
-            jax.ShapeDtypeStruct((3 * NBANDS, 128), F32),
+            jax.ShapeDtypeStruct((32, 40, 128), F32),
         ],
-        in_specs=[SMEM, ANY] + [VMEM] * 11,
-        out_specs=[VMEM] * 3,
+        in_specs=[SMEM] + [HBM] * 12,
+        out_specs=[HBM] * 3,
         scratch_shapes=[
-            pltpu.VMEM((3, NLAT, L), BF),
             pltpu.VMEM((2, 2, L, 640), BF),
             pltpu.VMEM((2, 2, L, WIDE), BF),
+            pltpu.VMEM((WIDE, 128), BF),
+            pltpu.VMEM((JJ, L, WIDE), BF),
+            pltpu.VMEM((L, WIDE), BF),
+            pltpu.VMEM((32, 40, 128), F32),
+            pltpu.VMEM((16, 8, 104, 128), BF),
             pltpu.VMEM((3, L, 128), F32),
-            pltpu.VMEM((8, 40, WIDE), F32),
+            pltpu.VMEM((8, 40, WIDE), BF),
             pltpu.SemaphoreType.DMA((3,)),
+            pltpu.SemaphoreType.DMA((4,)),
+            pltpu.SemaphoreType.DMA((8,)),
+            pltpu.SemaphoreType.DMA((7,)),
         ],
-        compiler_params=pltpu.CompilerParams(vmem_limit_bytes=VMEM_LIMIT),
+        compiler_params=pltpu.CompilerParams(vmem_limit_bytes=60 * MIB),
         cost_estimate=pl.CostEstimate(
             flops=10_000_000_000, bytes_accessed=12_000_000, transcendentals=0
         ),
         name="spectra",
-    )(place, analysis, rows, full, half, *targets)
+    )(place, rows, to_full, to_half, select, *targets)
 
 
 def gradient_kernel(
-    place_ref, analysis_ref, stacked_ref, target_ref, grams_ref, counts_ref,
-    symmetric_ref, cotangent_ref, full_ref, half_ref,
-    back_ref, grad_ref, loss_ref,
-    own_ref, from_full_ref, from_half_ref, sem,
+    stacked_hbm, target_hbm, sums_ref, cotangent_ref, share_ref, to_mixing_hbm,
+    from_full_hbm, from_half_hbm,
+    back_ref, grad_hbm, loss_ref,
+    stacked_ref, target_ref, to_mixing_ref, from_full_ref, from_half_ref, grad_ref,
+    held_ref, in_sem, sem,
 ):
-    copies = fetches(place_ref, analysis_ref, own_ref, sem)
-    for copy in copies:
+    loads = [
+        pltpu.make_async_copy(there, here, in_sem.at[n])
+        for n, (there, here) in enumerate(
+            (
+                (to_mixing_hbm, to_mixing_ref),
+                (target_hbm, target_ref),
+                (stacked_hbm, stacked_ref),
+                (from_full_hbm, from_full_ref),
+                (from_half_hbm, from_half_ref),
+            )
+        )
+    ]
+    for copy in loads:
         copy.start()
-    grams = jnp.sum(grams_ref[...], axis=0)
+    sums = jnp.sum(sums_ref[...], axis=0)
+    sums = sum(sums[10 * n : 10 * n + 10] for n in range(4))
     lane = iota((NBANDS, 128), 1)
-    inside = lane < MEMBERS
-    rows = []
-    own_power = jnp.zeros((NBANDS, 128), F32)
-    for i in range(JJ):
-        shift = JJ * (i % 7)
-        block = grams[NBANDS * (i // 7) : NBANDS * (i // 7) + NBANDS]
-        block = pltpu.roll(block, 128 - shift, 1) if shift else block
-        rows.append(jnp.where(lane < JJ, block, 0.0))
-        own_power = own_power + jnp.where(lane == i, rows[i], 0.0)
+    distance = jnp.sqrt(jnp.maximum(expand(sums), 0.0) + EPSILON)
     cotangent = cotangent_ref[...]
-    scaled = cotangent * (16.0 * MEMBERS * NLAT)
-    mixing = []
-    score = jnp.zeros((NBANDS, 128), F32)
-    beside = jnp.zeros((NBANDS, 128), F32)
-    for i in range(MEMBERS):
-        squared = rows[i][:, i : i + 1] + own_power - 2.0 * rows[i]
-        distance = jnp.sqrt(jnp.maximum(squared, 0.0) + EPSILON)
-        observed = distance[:, MEMBERS : MEMBERS + 1]
-        pairs = jnp.where(inside, counts_ref[i : i + 1, :] * distance, 0.0)
-        score = score + observed / MEMBERS - jnp.sum(pairs, axis=1, keepdims=True) / (
-            2.0 * MEMBERS * PARTNERS
-        )
-        observed_weight = scaled[:, :1] / (MEMBERS * observed)
-        pair_weight = scaled * symmetric_ref[i : i + 1, :] / (2.0 * MEMBERS * PARTNERS * distance)
-        pair_weight = jnp.where(inside, pair_weight, 0.0)
-        own = observed_weight - jnp.sum(pair_weight, axis=1, keepdims=True)
-        mixing.append(pair_weight + jnp.where(lane == i, own, 0.0))
-        beside = beside + jnp.where(lane == i, -observed_weight, 0.0)
+    share = share_ref[0:1, :]
+    score = jnp.sum(distance * share, axis=1, keepdims=True)
     loss_ref[...] = score * cotangent
+    weight = cotangent * (16.0 * MEMBERS * NLAT) * jnp.abs(share) / distance
+    beside = jnp.where(lane < MEMBERS, -weight, 0.0)
+    loads[0].wait()
+    mixing = sum(dot(part, to_mixing_ref[...]) for part in split3(weight))
+    mixing = [mixing[:, 128 * i : 128 * i + 128] for i in range(MEMBERS)]
 
     size = MEMBERS * GROUP
     widen = (iota((128, size), 0) == (iota((128, size), 1) >> 4)).astype(F32).astype(BF)
@@ -409,20 +539,13 @@
             grad_ref[:, pl.ds(start, GROUP), lanes] = part.astype(BF).reshape(MEMBERS, GROUP, 128)
         return carry
 
+    loads[1].wait()
+    loads[2].wait()
     lax.fori_loop(0, NGROUPS, mix, 0, unroll=2)
-    for copy in copies:
-        copy.wait()
-    for n in range(4):
-        choose = full_ref[...] if n < 2 else half_ref[n - 2]
-        spread = dot(choose, own_ref[min(n, 2)], 0, 0)
-        member = iota(spread.shape, 0) % 2
-        for i in range(2):
-            part = jnp.where(member == i, spread, 0.0).astype(BF)
-            if n < 2:
-                from_full_ref[n, i] = part
-            else:
-                from_half_ref[n - 2, i] = part
-
+    kept = pltpu.make_async_copy(grad_ref, grad_hbm, sem.at[4])
+    kept.start()
+    loads[3].wait()
+    loads[4].wait()
     def inverse(g, carry):
         for slot in range(3):
             grads = [jnp.concatenate(grads_of(grad_ref, g, i, slot), axis=1) for i in range(2)]
@@ -435,10 +558,18 @@
             start, count = STARTS[slot], COUNTS[slot]
             for k in range(2):
                 part = parts[k].reshape(16, count, 128).astype(BF)
-                back_ref[:, 2 * g + k, start : start + count, :] = part
+                held_ref[:, 2 * g + k, start : start + count, :] = part
+        send(g).start()
         return carry
 
+    def send(g):
+        where = pl.ds(2 * g, 2)
+        return pltpu.make_async_copy(held_ref.at[:, where], back_ref.at[:, where], sem.at[g])
+
     lax.fori_loop(0, 4, inverse, 0)
+    for g in range(4):
+        send(g).wait()
+    kept.wait()
 
 
 def grads_of(grad_ref, g, i, slot):
@@ -446,7 +577,7 @@
     return [grad_ref[4 * g + 2 * k + i, :, lanes] for k in range(2)]
 
 
-def gradient(place, analysis, stacked, target, grams, counts, symmetric, cotangent, full, half):
+def gradient(stacked, target, sums, cotangent, share, to_mixing, from_full, from_half):
     return pl.pallas_call(
         gradient_kernel,
         out_shape=[
@@ -454,20 +585,25 @@
             jax.ShapeDtypeStruct((MEMBERS, L, WIDE), BF),
             jax.ShapeDtypeStruct((NBANDS, 128), F32),
         ],
-        in_specs=[SMEM, ANY] + [VMEM] * 8,
-        out_specs=[VMEM] * 3,
+        in_specs=[HBM, HBM, VMEM, VMEM, VMEM, HBM, HBM, HBM],
+        out_specs=[HBM, HBM, VMEM],
         scratch_shapes=[
-            pltpu.VMEM((3, NLAT, L), BF),
+            pltpu.VMEM((JJ, L, WIDE), BF),
+            pltpu.VMEM((L, WIDE), BF),
+            pltpu.VMEM((128, MEMBERS * 128), BF),
             pltpu.VMEM((2, 2, 640, L), BF),
             pltpu.VMEM((2, 2, WIDE, L), BF),
-            pltpu.SemaphoreType.DMA((3,)),
+            pltpu.VMEM((MEMBERS, L, WIDE), BF),
+            pltpu.VMEM((16, 8, 104, 128), BF),
+            pltpu.SemaphoreType.DMA((5,)),
+            pltpu.SemaphoreType.DMA((5,)),
         ],
-        compiler_params=pltpu.CompilerParams(vmem_limit_bytes=VMEM_LIMIT),
+        compiler_params=pltpu.CompilerParams(vmem_limit_bytes=63 * MIB),
         cost_estimate=pl.CostEstimate(
             flops=10_000_000_000, bytes_accessed=12_000_000, transcendentals=0
         ),
         name="gradient",
-    )(place, analysis, stacked, target, grams, counts, symmetric, cotangent, full, half)
+    )(stacked, target, sums, cotangent, share, to_mixing, from_full, from_half)
 
 
 def weight_kernel(
@@ -523,7 +659,7 @@
             pltpu.VMEM((2, 640, L), F32),
             pltpu.VMEM((2, WIDE, L), F32),
         ],
-        compiler_params=pltpu.CompilerParams(vmem_limit_bytes=VMEM_LIMIT),
+        compiler_params=pltpu.CompilerParams(vmem_limit_bytes=63 * MIB),
         cost_estimate=pl.CostEstimate(
             flops=5_000_000_000, bytes_accessed=8_000_000, transcendentals=0
         ),
@@ -576,27 +712,31 @@
     by_order = jnp.transpose(analysis, (1, 0, 2))
     native = jnp.transpose(fourier[0].reshape(2, 20, 320, 128), (1, 2, 0, 3)).reshape(20, 640, 128)
     packed = pack(native)
-    target_in, packed = lax.optimization_barrier((target[0], packed))
+    target_in, partners, full, place, packed = lax.optimization_barrier(
+        (target[0], partners, full, place, packed)
+    )
     rows = travel(packed)
     targets = swap(target_blocks(place, target_in, band_ids))
-    stacked, observed, grams = spectra(place, by_order, rows, targets, full, half)
-    grams = exchange(jnp.broadcast_to(grams, (16, *grams.shape)), ORDER).sum(axis=0)
-    grams = exchange(jnp.broadcast_to(grams, (8, *grams.shape)), ENS)
-    member_ids = jnp.arange(128, dtype=jnp.int32)
-    counts = jnp.sum((partners[:, :, None] == member_ids[None, None, :]).astype(F32), axis=1)
-    square = counts[:, :MEMBERS]
-    symmetric = jnp.pad(square + square.T, ((0, 0), (0, 128 - MEMBERS)))
+    to_full, to_half, from_full, from_half, select, to_mixing = prepare(
+        place, by_order, full, half, partners
+    )
     cotangent = lax.dynamic_slice_in_dim(band_cotangent, lax.axis_index("dp"), 1, 0)[0]
     cotangent = jnp.broadcast_to(cotangent[:, None], (NBANDS, 128))
+    share = np.zeros((8, 128), np.float32)
+    share[:, :16] = 1.0 / MEMBERS
+    share[:, 16:80] = -1.0 / (2.0 * MEMBERS * PARTNERS)
+    stacked, observed, sums = spectra(place, rows, to_full, to_half, select, targets)
+    sums = exchange(sums.reshape(128, 5, 2, 128), EVERY).reshape(32, 40, 128)
     back, grads, loss = gradient(
-        place, by_order, stacked, observed, grams, counts, symmetric, cotangent, full, half
+        stacked, observed, sums, cotangent, jnp.asarray(share), to_mixing, from_full, from_half
     )
     returned = travel(back)
+    loss = loss[:, 0]
+    loss_bands = loss + lax.ppermute(loss, "dp", [(0, 1), (1, 0)])
     weight = weights(place, rows, grads, full, half)
     beside = lax.ppermute(weight[1], "dp", [(0, 1), (1, 0)])
     weight = (weight[0].astype(F32) + beside.astype(F32)).astype(BF)
     grad_analysis = finish(place, swap([weight[k] for k in range(8)]))
-    loss_bands = lax.psum(loss[:, 0], "dp")
     native_grad = unpack(returned).reshape(20, 320, 2, 128)
     grad_fourier = jnp.transpose(native_grad, (2, 0, 1, 3)).reshape(1, 2, 20, 40960)
     return (grad_fourier, grad_analysis, loss_bands)

time: 301 us -> 286 us (0.950)
  blocking collectives: 21.8 us -> 0 us
  local copies, waits for them, and re-layouts: 19.3 us -> 5.41 us
  Pallas kernels: 65.2 us -> 74.1 us
  starting transfers between devices: 65.6 us -> 72 us
  waiting for transfers between devices: 122 us -> 128 us
    all_to_all x1 -> x0, blocking collectives: 18.9 us -> none  [exchange(): return lax.all_to_all(x, axes, split_axis=0, concat_axis=0, tiled=True)]
    unnamed x62 -> x39, local copies, waits for them, and re-layouts: 17.7 us -> 1.43 us
    all_to_all x3, waiting for transfers between devices: 10.9 us -> 23.2 us  [exchange(): return lax.all_to_all(x, axes, split_axis=0, concat_axis=0, tiled=True)]
    pallas_call x0 -> x1, Pallas kernels: none -> 6.98 us  [prepare(): pl.pallas_call(prepare_kernel, out_shape=[jax.ShapeDtypeStruct((2, 2, L,...]
    ppermute x14, waiting for transfers between devices: 109 us -> 103 us  [swap(): lax.ppermute(blocks[k], ENS, [(e, e ^ k) for e in range(8)])]
    all_to_all x3, starting transfers between devices: 28 us -> 33.3 us  [exchange(): return lax.all_to_all(x, axes, split_axis=0, concat_axis=0, tiled=True)]
  transfers between devices with their start and end apart: 18 -> 19, of which waited for: 10 -> 10; matrix products, arithmetic and copies ran while one was open for 1% -> 2% of each run, Pallas kernels for 5% -> 8%
where the time goes in v3:
time: 286 us; the launch traced here: 282 us
  waiting for transfers between devices  128 us (45%)
  Pallas kernels  74.1 us (26%)
  starting transfers between devices  72 us (25%)
  local copies, waits for them, and re-layouts  5.41 us (2%)
    ppermute x14, waiting for transfers between devices, swap(): lax.ppermute(blocks[k], ENS, [(e, e ^ k) for e in range(8)])  103 us
    ppermute x14, starting transfers between devices, swap(): lax.ppermute(blocks[k], ENS, [(e, e ^ k) for e in range(8)])  38.5 us
    all_to_all x3, starting transfers between devices, exchange(): return lax.all_to_all(x, axes, split_axis=0, concat_axis=0, tiled=True)  33.3 us
    all_to_all x3, waiting for transfers between devices, exchange(): return lax.all_to_all(x, axes, split_axis=0, concat_axis=0, tiled=True)  23.2 us
    pallas_call x1, Pallas kernels, gradient(): pl.pallas_call(gradient_kernel, out_shape=[jax.ShapeDtypeStruct((16, 8, 1...  18.4 us
    pallas_call x1, Pallas kernels, spectra(): pl.pallas_call(spectra_kernel, out_shape=[jax.ShapeDtypeStruct((JJ, L, WI...  17.8 us
    pallas_call x1, Pallas kernels, weights(): pl.pallas_call(weight_kernel, out_shape=jax.ShapeDtypeStruct((2, 8, 3, 20...  11.6 us
    pallas_call x1, Pallas kernels, pack(): pl.pallas_call(pack_kernel, grid=(8,), out_shape=jax.ShapeDtypeStruct((16...  7.81 us
  transfers between devices with their start and end apart: 19, of which 10 were waited for; matrix products, arithmetic and copies ran while one was open for 2% of the time, Pallas kernels for 8%

profile of v3, /device:TPU:8, one launch (start us, length us, event | category | flops | bytes accessed | tf_op | source)
XLA Modules:
  0.0 282.3 jit_solution(2801095388918154516)
XLA Ops:
  0.7 0.6 pad_add_fusion.place_ref
  1.3 7.8 %pack.1 = bf16[16,8,104,128]{3,2,1,0:T(8,128)(2,1)} custom-call(bf16[20,640,128]{2,1,0:T(8,128)(2,1)} %bitcast.50, bf16[320,320]{1,0:T(8,128)(2,1)} %constant.45.clone.whole_ref, bf16[2,96,160]{2,1,0:T(8,128)(2,1)} %constant.46.clone.half_ref), custom_call_target="tpu_custom_call" | custom-call | tf_op jit(solution)/shard_map/pack/pallas_call | solution.py:143
  9.1 15.9 %all-to-all-start = ((bf16[128,52,2,128]{3,2,1,0:T(2,128)(2,1)}), bf16[128,52,2,128]{3,2,1,0:T(2,128)(2,1)}, u32[]{:S(2)}, u32[]{:S(2)}) async-start(bf16[128,52,2,128]{3,2,1,0:T(2,128)(2,1)} %bitcast.47), calls=%async_computation | async-start | bytes 6815744 | tf_op jit(solution)/shard_map/all_to_all | solution.py:693
  25.0 0.7 copy.20.band_ref
  25.7 1.8 target_blocks.1
  27.5 1.6 collective-permute-start
  29.1 2.7 collective-permute-start.1
  31.8 0.6 collective-permute-start.2
  32.3 5.4 %collective-permute-start.3 = (bf16[40,384]{1,0:T(8,128)(2,1)}, bf16[40,384]{1,0:T(8,128)(2,1)S(1)}, u32[]{:S(2)}, u32[]{:S(2)}) collective-permute-start(bf16[40,384]{1,0:T(8,128)(2,1)} %get-tuple-element.40), channel_id=1, source_target_pairs={{0,4},{1,5},{2,6},{3,7},{4,0},{5,1},{6,2},{7,3},{8,12},{9,13},{10,... | collective-permute-start | bytes 92168 | tf_op jit(solution)/shard_map/ppermute | solution.py:698
  37.7 0.2 collective-permute-start.4
  38.0 8.8 %collective-permute-start.5 = (bf16[40,384]{1,0:T(8,128)(2,1)}, bf16[40,384]{1,0:T(8,128)(2,1)S(1)}, u32[]{:S(2)}, u32[]{:S(2)}) collective-permute-start(bf16[40,384]{1,0:T(8,128)(2,1)} %get-tuple-element.42), channel_id=1, source_target_pairs={{0,6},{1,7},{2,4},{3,5},{4,2},{5,3},{6,0},{7,1},{8,14},{9,15},{10,... | collective-permute-start | bytes 92168 | tf_op jit(solution)/shard_map/ppermute | solution.py:698
  46.8 0.6 collective-permute-start.6
  47.4 0.6 broadcast_in_dim.11.other_row_ref
  48.0 0.7 broadcast_in_dim.24.other_column_ref
  48.7 7.0 %prepare.1 = (bf16[2,2,320,640]{3,2,1,0:T(8,128)(2,1)}, bf16[2,2,320,384]{3,2,1,0:T(8,128)(2,1)}, bf16[2,2,640,320]{3,2,1,0:T(8,128)(2,1)}, bf16[2,2,384,320]{3,...) custom-call(s32[3]{0:T(128)} %pad_add_fusion.place_ref, bf16[20,320,320]{2,1,0:T(8,128)(2,1)} %bitcast.48, ...), custom_call_target="tpu_custom_call" | custom-call | tf_op jit(solution)/shard_map/prepare/pallas_call | solution.py:281
  55.8 47.5 %collective-permute-done.3.refs_4_ = bf16[40,384]{1,0:T(8,128)(2,1)S(1)} collective-permute-done((bf16[40,384]{1,0:T(8,128)(2,1)}, bf16[40,384]{1,0:T(8,128)(2,1)S(1)}, u32[]{:S(2)}, u32[]{:S(2)}) %collective-permute-start.3) | collective-permute-done | bytes 30752 | tf_op jit(solution)/shard_map/ppermute | solution.py:698
  103.2 0.9 collective-permute-done.4.refs_5_
  104.1 3.1 %collective-permute-done.5.refs_6_ = bf16[40,384]{1,0:T(8,128)(2,1)S(1)} collective-permute-done((bf16[40,384]{1,0:T(8,128)(2,1)}, bf16[40,384]{1,0:T(8,128)(2,1)S(1)}, u32[]{:S(2)}, u32[]{:S(2)}) %collective-permute-start.5) | collective-permute-done | bytes 30752 | tf_op jit(solution)/shard_map/ppermute | solution.py:698
  107.2 1.4 all-to-all-done
  108.6 17.8 %spectra.1 = (bf16[17,320,384]{2,1,0:T(8,128)(2,1)}, bf16[320,384]{1,0:T(8,128)(2,1)}, f32[32,40,128]{2,1,0:T(8,128)}) custom-call(s32[3]{0:T(128)} %pad_add_fusion.place_ref, bf16[16,8,104,128]{3,2,1,0:T(8,128)(2,1)} %bitcast.8.rows_hbm.rows_ref, bf16[2,2,320,640]{3,2,1,0:T(8,128)(2,1)} %get-tuple-element.32.to_full_hbm, ...), custom_call_target="tpu_custom_call" | custom-call | flops 10000000000 | bytes 12000000 | tf_op jit(solution)/shard_map/spectra/pallas_call | solution.py:442
  126.5 9.8 %all-to-all-start.1 = ((f32[128,5,2,128]{3,2,1,0:T(2,128)}), f32[128,5,2,128]{3,2,1,0:T(2,128)S(1)}, u32[]{:S(2)}, u32[]{:S(2)}) async-start(f32[128,5,2,128]{3,2,1,0:T(2,128)} %bitcast.53), calls=%async_computation.1 | async-start | bytes 1310720 | tf_op jit(solution)/shard_map/all_to_all | solution.py:693
  136.3 21.8 %all-to-all-done.1 = f32[128,5,2,128]{3,2,1,0:T(2,128)S(1)} async-done(((f32[128,5,2,128]{3,2,1,0:T(2,128)}), f32[128,5,2,128]{3,2,1,0:T(2,128)S(1)}, u32[]{:S(2)}, u32[]{:S(2)}) %all-to-all-start.1) | async-done | bytes 655392 | tf_op jit(solution)/shard_map/all_to_all | solution.py:693
  158.1 0.7 broadcast_in_dim.26.cotangent_ref
  158.8 0.1 copy-done.1
  158.9 18.4 %gradient.1 = (bf16[16,8,104,128]{3,2,1,0:T(8,128)(2,1)}, bf16[16,320,384]{2,1,0:T(8,128)(2,1)}, f32[16,128]{1,0:T(8,128)}) custom-call(bf16[17,320,384]{2,1,0:T(8,128)(2,1)} %get-tuple-element.44.stacked_hbm, bf16[320,384]{1,0:T(8,128)(2,1)} %get-tuple-element.45.target_hbm, f32[32,40,128]{2,1,0:T(8,128)} %bitcast.52, ...), custom_call_target="tpu_custom_call" | custom-call | flops 10000000000 | bytes 12000000 | tf_op jit(solution)/shard_map/gradient/pallas_call | solution.py:581
  177.3 7.7 %all-to-all-start.2 = ((bf16[128,52,2,128]{3,2,1,0:T(2,128)(2,1)}), bf16[128,52,2,128]{3,2,1,0:T(2,128)(2,1)}, u32[]{:S(2)}, u32[]{:S(2)}) async-start(bf16[128,52,2,128]{3,2,1,0:T(2,128)(2,1)} %bitcast.49), calls=%async_computation.2 | async-start | bytes 6815744 | tf_op jit(solution)/shard_map/all_to_all | solution.py:693
  185.0 11.6 %weights.1 = bf16[2,8,3,20,320]{4,3,2,1,0:T(8,128)(2,1)} custom-call(s32[3]{0:T(128)} %pad_add_fusion.place_ref, bf16[16,8,104,128]{3,2,1,0:T(8,128)(2,1)} %bitcast.8.rows_hbm.rows_ref, bf16[16,320,384]{2,1,0:T(8,128)(2,1)} %get-tuple-element.51.grad_ref, bf16[320,640]{1,0:T(8,128)(2,1)} %constant.43.clone.full_ref, bf16[2,320,384]{2,1,0:T(8,128)(2,1)} %constant.44.clone.half_ref), custom_call_target="tpu_custom_call" | custom-call | flops 5000000000 | bytes 8000000 | tf_op jit(solution)/shard_map/weights/pallas_call | solution.py:653
  196.6 1.1 slice_bitcast_fusion
  197.7 0.1 collective-permute-start.7
  197.8 1.8 collective-permute-done.7
  199.5 1.1 fusion
  200.7 0.7 slice_bitcast_fusion.2
  201.3 7.5 %collective-permute-start.14 = (bf16[3,20,320]{2,1,0:T(8,128)(2,1)S(1)}, bf16[3,20,320]{2,1,0:T(8,128)(2,1)S(1)}, u32[]{:S(2)}, u32[]{:S(2)}) collective-permute-start(bf16[3,20,320]{2,1,0:T(8,128)(2,1)S(1)} %get-tuple-element.53), channel_id=1, source_target_pairs={{0,7},{1,6},{2,5},{3,4},{4,3},{5,2},{6,1},{7,0},{8,15},{9,14},{10,... | collective-permute-start | bytes 115208 | tf_op jit(solution)/shard_map/ppermute | solution.py:698
  208.8 0.9 collective-permute-start.13
  209.7 0.1 slice_reduce_fusion
  209.9 5.5 %collective-permute-start.12 = (bf16[3,20,320]{2,1,0:T(8,128)(2,1)S(1)}, bf16[3,20,320]{2,1,0:T(8,128)(2,1)S(1)}, u32[]{:S(2)}, u32[]{:S(2)}) collective-permute-start(bf16[3,20,320]{2,1,0:T(8,128)(2,1)S(1)} %get-tuple-element.55), channel_id=1, source_target_pairs={{0,5},{1,4},{2,7},{3,6},{4,1},{5,0},{6,3},{7,2},{8,13},{9,12},{10,... | collective-permute-start | bytes 115208 | tf_op jit(solution)/shard_map/ppermute | solution.py:698
  215.4 0.6 collective-permute-start.11
  215.9 2.7 collective-permute-start.10
  218.6 46.7 %collective-permute-done.14.refs_7_ = bf16[3,20,320]{2,1,0:T(8,128)(2,1)S(1)} collective-permute-done((bf16[3,20,320]{2,1,0:T(8,128)(2,1)S(1)}, bf16[3,20,320]{2,1,0:T(8,128)(2,1)S(1)}, u32[]{:S(2)}, u32[]{:S(2)}) %collective-permute-start.14) | collective-permute-done | bytes 38432 | tf_op jit(solution)/shard_map/ppermute | solution.py:698
  265.3 1.4 collective-permute-start.9
  266.7 1.2 collective-permute-done.13.refs_6_
  267.9 0.3 collective-permute-start.8
  268.2 0.5 add.19
  268.7 2.2 collective-permute-done.9.refs_2_
  270.9 1.1 collective-permute-done.8.refs_1_
  272.1 0.6 copy-done.8
  272.6 2.1 finish.1
  274.8 7.5 %unpack.1 = bf16[20,640,128]{2,1,0:T(8,128)(2,1)} custom-call(bf16[16,8,104,128]{3,2,1,0:T(8,128)(2,1)} %bitcast.15.y_ref, bf16[320,320]{1,0:T(8,128)(2,1)} %constant.48.clone.whole_ref, bf16[2,160,96]{2,1,0:T(8,128)(2,1)} %constant.49.clone.half_ref), custom_call_target="tpu_custom_call" | custom-call | tf_op jit(solution)/shard_map/unpack/pallas_call | solution.py:154
  (51 shorter events, 0.4 us)
Async XLA Ops:
  0.6 135.6 %copy-start = (f32[2,16]{1,0:T(2,128)S(1)}, f32[2,16]{1,0:T(2,128)}, u32[]{:S(2)}) copy-start(f32[2,16]{1,0:T(2,128)} %param.18) | copy-start | bytes 388
  9.1 15.9 %copy-start.9 = (s32[40,20]{0,1:T(8,128)S(1)}, s32[40,20]{0,1:T(8,128)}, u32[]{:S(2)}) copy-start(s32[40,20]{0,1:T(8,128)} %param.16) | copy-start | bytes 9604
  9.1 28.8 %copy-start.11 = (s32[16,4]{0,1:T(4,128)S(1)}, s32[16,4]{0,1:T(4,128)}, u32[]{:S(2)}) copy-start(s32[16,4]{0,1:T(4,128)} %param.17) | copy-start | bytes 772
  9.1 99.4 %all-to-all-start = ((bf16[128,52,2,128]{3,2,1,0:T(2,128)(2,1)}), bf16[128,52,2,128]{3,2,1,0:T(2,128)(2,1)}, u32[]{:S(2)}, u32[]{:S(2)}) async-start(bf16[128,52,2,128]{3,2,1,0:T(2,128)(2,1)} %bitcast.47), calls=%async_computation | async-start | bytes 6815744 | tf_op jit(solution)/shard_map/all_to_all | solution.py:693
  27.5 10.5 %collective-permute-start = (bf16[40,384]{1,0:T(8,128)(2,1)}, bf16[40,384]{1,0:T(8,128)(2,1)S(1)}, u32[]{:S(2)}, u32[]{:S(2)}) collective-permute-start(bf16[40,384]{1,0:T(8,128)(2,1)} %get-tuple-element.37), channel_id=1, source_target_pairs={{0,1},{1,0},{2,3},{3,2},{4,5},{5,4},{6,7},{7,6},{8,9},{9,8},{10,11... | collective-permute-start | bytes 92168 | tf_op jit(solution)/shard_map/ppermute | solution.py:698
  29.1 17.7 %collective-permute-start.1 = (bf16[40,384]{1,0:T(8,128)(2,1)}, bf16[40,384]{1,0:T(8,128)(2,1)S(1)}, u32[]{:S(2)}, u32[]{:S(2)}) collective-permute-start(bf16[40,384]{1,0:T(8,128)(2,1)} %get-tuple-element.38), channel_id=1, source_target_pairs={{0,2},{1,3},{2,0},{3,1},{4,6},{5,7},{6,4},{7,5},{8,10},{9,11},{10,... | collective-permute-start | bytes 92168 | tf_op jit(solution)/shard_map/ppermute | solution.py:698
  31.8 24.0 %collective-permute-start.2 = (bf16[40,384]{1,0:T(8,128)(2,1)}, bf16[40,384]{1,0:T(8,128)(2,1)S(1)}, u32[]{:S(2)}, u32[]{:S(2)}) collective-permute-start(bf16[40,384]{1,0:T(8,128)(2,1)} %get-tuple-element.39), channel_id=1, source_target_pairs={{0,3},{1,2},{2,1},{3,0},{4,7},{5,6},{6,5},{7,4},{8,11},{9,10},{10,... | collective-permute-start | bytes 92168 | tf_op jit(solution)/shard_map/ppermute | solution.py:698
  32.3 70.9 %collective-permute-start.3 = (bf16[40,384]{1,0:T(8,128)(2,1)}, bf16[40,384]{1,0:T(8,128)(2,1)S(1)}, u32[]{:S(2)}, u32[]{:S(2)}) collective-permute-start(bf16[40,384]{1,0:T(8,128)(2,1)} %get-tuple-element.40), channel_id=1, source_target_pairs={{0,4},{1,5},{2,6},{3,7},{4,0},{5,1},{6,2},{7,3},{8,12},{9,13},{10,... | collective-permute-start | bytes 92168 | tf_op jit(solution)/shard_map/ppermute | solution.py:698
  37.7 66.4 %collective-permute-start.4 = (bf16[40,384]{1,0:T(8,128)(2,1)}, bf16[40,384]{1,0:T(8,128)(2,1)S(1)}, u32[]{:S(2)}, u32[]{:S(2)}) collective-permute-start(bf16[40,384]{1,0:T(8,128)(2,1)} %get-tuple-element.41), channel_id=1, source_target_pairs={{0,5},{1,4},{2,7},{3,6},{4,1},{5,0},{6,3},{7,2},{8,13},{9,12},{10,... | collective-permute-start | bytes 92168 | tf_op jit(solution)/shard_map/ppermute | solution.py:698
  38.0 70.5 %copy-start.12 = (bf16[40,384]{1,0:T(8,128)(2,1)}, bf16[40,384]{1,0:T(8,128)(2,1)S(1)}, u32[]{:S(2)}) copy-start(bf16[40,384]{1,0:T(8,128)(2,1)S(1)} %collective-permute-done.refs_1_) | copy-start | bytes 92164
  38.0 69.1 %collective-permute-start.5 = (bf16[40,384]{1,0:T(8,128)(2,1)}, bf16[40,384]{1,0:T(8,128)(2,1)S(1)}, u32[]{:S(2)}, u32[]{:S(2)}) collective-permute-start(bf16[40,384]{1,0:T(8,128)(2,1)} %get-tuple-element.42), channel_id=1, source_target_pairs={{0,6},{1,7},{2,4},{3,5},{4,2},{5,3},{6,0},{7,1},{8,14},{9,15},{10,... | collective-permute-start | bytes 92168 | tf_op jit(solution)/shard_map/ppermute | solution.py:698
  46.8 61.8 %copy-start.13 = (bf16[40,384]{1,0:T(8,128)(2,1)}, bf16[40,384]{1,0:T(8,128)(2,1)S(1)}, u32[]{:S(2)}) copy-start(bf16[40,384]{1,0:T(8,128)(2,1)S(1)} %collective-permute-done.1.refs_2_) | copy-start | bytes 92164
  46.8 60.4 %collective-permute-start.6 = (bf16[40,384]{1,0:T(8,128)(2,1)}, bf16[40,384]{1,0:T(8,128)(2,1)S(1)}, u32[]{:S(2)}, u32[]{:S(2)}) collective-permute-start(bf16[40,384]{1,0:T(8,128)(2,1)} %get-tuple-element.43), channel_id=1, source_target_pairs={{0,7},{1,6},{2,5},{3,4},{4,3},{5,2},{6,1},{7,0},{8,15},{9,14},{10,... | collective-permute-start | bytes 92168 | tf_op jit(solution)/shard_map/ppermute | solution.py:698
  55.7 52.8 %copy-start.14 = (bf16[40,384]{1,0:T(8,128)(2,1)}, bf16[40,384]{1,0:T(8,128)(2,1)S(1)}, u32[]{:S(2)}) copy-start(bf16[40,384]{1,0:T(8,128)(2,1)S(1)} %collective-permute-done.2.refs_3_) | copy-start | bytes 92164
  103.2 5.4 %copy-start.15 = (bf16[40,384]{1,0:T(8,128)(2,1)}, bf16[40,384]{1,0:T(8,128)(2,1)S(1)}, u32[]{:S(2)}) copy-start(bf16[40,384]{1,0:T(8,128)(2,1)S(1)} %collective-permute-done.3.refs_4_) | copy-start | bytes 92164
  104.1 4.5 %copy-start.16 = (bf16[40,384]{1,0:T(8,128)(2,1)}, bf16[40,384]{1,0:T(8,128)(2,1)S(1)}, u32[]{:S(2)}) copy-start(bf16[40,384]{1,0:T(8,128)(2,1)S(1)} %collective-permute-done.4.refs_5_) | copy-start | bytes 92164
  107.2 1.4 copy-start.17
  107.2 1.4 copy-start.18
  126.5 31.6 %all-to-all-start.1 = ((f32[128,5,2,128]{3,2,1,0:T(2,128)}), f32[128,5,2,128]{3,2,1,0:T(2,128)S(1)}, u32[]{:S(2)}, u32[]{:S(2)}) async-start(f32[128,5,2,128]{3,2,1,0:T(2,128)} %bitcast.53), calls=%async_computation.1 | async-start | bytes 1310720 | tf_op jit(solution)/shard_map/all_to_all | solution.py:693
  158.1 0.8 copy-start.1
  177.3 97.5 %all-to-all-start.2 = ((bf16[128,52,2,128]{3,2,1,0:T(2,128)(2,1)}), bf16[128,52,2,128]{3,2,1,0:T(2,128)(2,1)}, u32[]{:S(2)}, u32[]{:S(2)}) async-start(bf16[128,52,2,128]{3,2,1,0:T(2,128)(2,1)} %bitcast.49), calls=%async_computation.2 | async-start | bytes 6815744 | tf_op jit(solution)/shard_map/all_to_all | solution.py:693
  185.0 24.7 %copy-start.10 = (f32[16,128]{1,0:T(8,128)S(1)}, f32[16,128]{1,0:T(8,128)}, u32[]{:S(2)}) copy-start(f32[16,128]{1,0:T(8,128)} %get-tuple-element.52) | copy-start | bytes 24580
  197.7 1.9 collective-permute-start.7
  201.3 63.9 %collective-permute-start.14 = (bf16[3,20,320]{2,1,0:T(8,128)(2,1)S(1)}, bf16[3,20,320]{2,1,0:T(8,128)(2,1)S(1)}, u32[]{:S(2)}, u32[]{:S(2)}) collective-permute-start(bf16[3,20,320]{2,1,0:T(8,128)(2,1)S(1)} %get-tuple-element.53), channel_id=1, source_target_pairs={{0,7},{1,6},{2,5},{3,4},{4,3},{5,2},{6,1},{7,0},{8,15},{9,14},{10,... | collective-permute-start | bytes 115208 | tf_op jit(solution)/shard_map/ppermute | solution.py:698
  208.8 59.0 %collective-permute-start.13 = (bf16[3,20,320]{2,1,0:T(8,128)(2,1)S(1)}, bf16[3,20,320]{2,1,0:T(8,128)(2,1)S(1)}, u32[]{:S(2)}, u32[]{:S(2)}) collective-permute-start(bf16[3,20,320]{2,1,0:T(8,128)(2,1)S(1)} %get-tuple-element.54), channel_id=1, source_target_pairs={{0,6},{1,7},{2,4},{3,5},{4,2},{5,3},{6,0},{7,1},{8,14},{9,15},{10,... | collective-permute-start | bytes 115208 | tf_op jit(solution)/shard_map/ppermute | solution.py:698
  209.8 6.1 %collective-permute-start.15 = (f32[16]{0:T(128)S(1)}, f32[16]{0:T(128)S(1)}, u32[]{:S(2)}, u32[]{:S(2)}) collective-permute-start(f32[16]{0:T(128)S(1)} %slice_reduce_fusion), channel_id=1, source_target_pairs={{0,128},{128,0},{1,129},{129,1},{2,130},{130,2},{3,131},{131,3},{4... | collective-permute-start | bytes 200 | tf_op jit(solution)/shard_map/ppermute | solution.py:735
  209.9 58.8 %collective-permute-start.12 = (bf16[3,20,320]{2,1,0:T(8,128)(2,1)S(1)}, bf16[3,20,320]{2,1,0:T(8,128)(2,1)S(1)}, u32[]{:S(2)}, u32[]{:S(2)}) collective-permute-start(bf16[3,20,320]{2,1,0:T(8,128)(2,1)S(1)} %get-tuple-element.55), channel_id=1, source_target_pairs={{0,5},{1,4},{2,7},{3,6},{4,1},{5,0},{6,3},{7,2},{8,13},{9,12},{10,... | collective-permute-start | bytes 115208 | tf_op jit(solution)/shard_map/ppermute | solution.py:698
  215.4 53.3 %collective-permute-start.11 = (bf16[3,20,320]{2,1,0:T(8,128)(2,1)S(1)}, bf16[3,20,320]{2,1,0:T(8,128)(2,1)S(1)}, u32[]{:S(2)}, u32[]{:S(2)}) collective-permute-start(bf16[3,20,320]{2,1,0:T(8,128)(2,1)S(1)} %get-tuple-element.56), channel_id=1, source_target_pairs={{0,4},{1,5},{2,6},{3,7},{4,0},{5,1},{6,2},{7,3},{8,12},{9,13},{10,... | collective-permute-start | bytes 115208 | tf_op jit(solution)/shard_map/ppermute | solution.py:698
  215.9 52.8 %collective-permute-start.10 = (bf16[3,20,320]{2,1,0:T(8,128)(2,1)S(1)}, bf16[3,20,320]{2,1,0:T(8,128)(2,1)S(1)}, u32[]{:S(2)}, u32[]{:S(2)}) collective-permute-start(bf16[3,20,320]{2,1,0:T(8,128)(2,1)S(1)} %get-tuple-element.57), channel_id=1, source_target_pairs={{0,3},{1,2},{2,1},{3,0},{4,7},{5,6},{6,5},{7,4},{8,11},{9,10},{10,... | collective-permute-start | bytes 115208 | tf_op jit(solution)/shard_map/ppermute | solution.py:698
  265.3 6.8 %copy-start.2 = (bf16[3,20,320]{2,1,0:T(8,128)(2,1)}, bf16[3,20,320]{2,1,0:T(8,128)(2,1)S(1)}, u32[]{:S(2)}) copy-start(bf16[3,20,320]{2,1,0:T(8,128)(2,1)S(1)} %collective-permute-done.14.refs_7_) | copy-start | bytes 115204
  265.3 5.7 %collective-permute-start.9 = (bf16[3,20,320]{2,1,0:T(8,128)(2,1)S(1)}, bf16[3,20,320]{2,1,0:T(8,128)(2,1)S(1)}, u32[]{:S(2)}, u32[]{:S(2)}) collective-permute-start(bf16[3,20,320]{2,1,0:T(8,128)(2,1)S(1)} %get-tuple-element.58), channel_id=1, source_target_pairs={{0,2},{1,3},{2,0},{3,1},{4,6},{5,7},{6,4},{7,5},{8,10},{9,11},{10,... | collective-permute-start | bytes 115208 | tf_op jit(solution)/shard_map/ppermute | solution.py:698
  267.9 4.2 %copy-start.3 = (bf16[3,20,320]{2,1,0:T(8,128)(2,1)}, bf16[3,20,320]{2,1,0:T(8,128)(2,1)S(1)}, u32[]{:S(2)}) copy-start(bf16[3,20,320]{2,1,0:T(8,128)(2,1)S(1)} %collective-permute-done.13.refs_6_) | copy-start | bytes 115204
  267.9 4.2 %collective-permute-start.8 = (bf16[3,20,320]{2,1,0:T(8,128)(2,1)S(1)}, bf16[3,20,320]{2,1,0:T(8,128)(2,1)S(1)}, u32[]{:S(2)}, u32[]{:S(2)}) collective-permute-start(bf16[3,20,320]{2,1,0:T(8,128)(2,1)S(1)} %get-tuple-element.59), channel_id=1, source_target_pairs={{0,1},{1,0},{2,3},{3,2},{4,5},{5,4},{6,7},{7,6},{8,9},{9,8},{10,11... | collective-permute-start | bytes 115208 | tf_op jit(solution)/shard_map/ppermute | solution.py:698
  268.7 3.3 %copy-start.4 = (bf16[3,20,320]{2,1,0:T(8,128)(2,1)}, bf16[3,20,320]{2,1,0:T(8,128)(2,1)S(1)}, u32[]{:S(2)}) copy-start(bf16[3,20,320]{2,1,0:T(8,128)(2,1)S(1)} %collective-permute-done.12.refs_5_) | copy-start | bytes 115204
  268.7 3.3 %copy-start.5 = (bf16[3,20,320]{2,1,0:T(8,128)(2,1)}, bf16[3,20,320]{2,1,0:T(8,128)(2,1)S(1)}, u32[]{:S(2)}) copy-start(bf16[3,20,320]{2,1,0:T(8,128)(2,1)S(1)} %collective-permute-done.11.refs_4_) | copy-start | bytes 115204
  268.7 3.3 %copy-start.6 = (bf16[3,20,320]{2,1,0:T(8,128)(2,1)}, bf16[3,20,320]{2,1,0:T(8,128)(2,1)S(1)}, u32[]{:S(2)}) copy-start(bf16[3,20,320]{2,1,0:T(8,128)(2,1)S(1)} %collective-permute-done.10.refs_3_) | copy-start | bytes 115204
  270.9 1.1 copy-start.7
  272.0 0.6 copy-start.8

commit v4 on v3

--- a/solution.py
+++ b/solution.py
@@ -233,21 +233,12 @@
 
 
 def prepare_kernel(
-    place_ref, analysis_ref, full_ref, half_ref, other_row_ref, other_column_ref,
-    to_full_ref, to_half_ref, from_full_ref, from_half_ref, select_ref, to_mixing_ref, own_ref, sem,
+    place_ref, analysis_ref, full_ref, half_ref, other_column_ref,
+    to_full_ref, to_half_ref, from_full_ref, from_half_ref, to_mixing_ref, own_ref, sem,
 ):
     copies = fetches(place_ref, analysis_ref, own_ref, sem)
     for copy in copies:
         copy.start()
-    def is_at(a, b):
-        n = (a >= 7).astype(jnp.int32) + (a >= 14).astype(jnp.int32)
-        return (iota((WIDE, 128), 0) == 128 * n + JJ * (a - 7 * n) + b).astype(F32)
-
-    lane = iota((WIDE, 128), 1)
-    who = lane & 15
-    other = jnp.broadcast_to(other_row_ref[0:1, :], (WIDE, 128))
-    select = is_at(who, who) + is_at(other, other) - 2.0 * is_at(who, other)
-    select_ref[...] = jnp.where(lane < 80, select, 0.0).astype(BF)
     row, j = iota((128, 128), 0), iota((128, 128), 1)
     who, other = row & 15, other_column_ref[...]
     pair = (row >= 16) & (row < 80)
@@ -274,10 +265,7 @@
             from_ref[i] = jnp.where(member == i, spread, 0.0).astype(BF)
 
 
-def prepare(place, analysis, full, half, partners):
-    other = jnp.concatenate(
-        [jnp.full((16,), MEMBERS, jnp.int32), partners.T.reshape(64), jnp.zeros((48,), jnp.int32)]
-    )
+def prepare(place, analysis, full, half, other):
     return pl.pallas_call(
         prepare_kernel,
         out_shape=[
@@ -285,18 +273,35 @@
             jax.ShapeDtypeStruct((2, 2, L, WIDE), BF),
             jax.ShapeDtypeStruct((2, 2, 640, L), BF),
             jax.ShapeDtypeStruct((2, 2, WIDE, L), BF),
-            jax.ShapeDtypeStruct((WIDE, 128), BF),
             jax.ShapeDtypeStruct((128, MEMBERS * 128), BF),
         ],
-        in_specs=[SMEM, HBM, VMEM, VMEM, VMEM, VMEM],
-        out_specs=[VMEM] * 6,
+        in_specs=[SMEM, HBM, VMEM, VMEM, VMEM],
+        out_specs=[VMEM] * 5,
         scratch_shapes=[pltpu.VMEM((3, NLAT, L), BF), pltpu.SemaphoreType.DMA((3,))],
         compiler_params=pltpu.CompilerParams(vmem_limit_bytes=63 * MIB),
         name="prepare",
-    )(
-        place, analysis, full, half,
-        jnp.broadcast_to(other[None], (8, 128)), jnp.broadcast_to(other[:, None], (128, 128)),
-    )
+    )(place, analysis, full, half, other)
+
+
+def block_mask(size, kind, lanes=None):
+    shape = (size, lanes or size)
+    row, lane = iota(shape, 0), iota(shape, 1)
+    same = (row >> 4) == (lane >> 4) if kind == "block" else (row & 15) == (lane & 15)
+    return same.astype(F32).astype(BF)
+
+
+def pick_bands(bands, mask):
+    shape = (GROUP, 128)
+    one_hot = jnp.broadcast_to(bands, shape) == (iota(shape, 1) & 15).astype(F32)
+    tile = jnp.concatenate([one_hot.astype(F32).astype(BF)] * MEMBERS, axis=0)
+    return jnp.concatenate([tile, tile], axis=1) * mask
+
+
+def fold(x):
+    x = x[:, :128] + x[:, 128:]
+    for shift in (64, 32, 16):
+        x = x + pltpu.roll(x, shift, 1)
+    return x
 
 
 def compact(x):
@@ -327,11 +332,11 @@
     return jnp.concatenate([top, jnp.where(lane < 80, rest, 0.0)], axis=0)
 
 
-def spectra_kernel(place_ref, rows_hbm, to_full_hbm, to_half_hbm, select_hbm, *refs):
+def spectra_kernel(place_ref, rows_hbm, to_full_hbm, to_half_hbm, other_ref, *refs):
     target_refs = refs[:8]
     stacked_hbm, target_hbm, sums_hbm = refs[8:11]
-    to_full_ref, to_half_ref, select_ref, stacked_ref, target_ref, sums_ref = refs[11:17]
-    rows_ref, terms_ref, order_ref, in_sem, rows_sem, target_sem, out_sem = refs[17:]
+    to_full_ref, to_half_ref, stacked_ref, target_ref, sums_ref = refs[11:16]
+    rows_ref, mask_ref, order_ref, in_sem, rows_sem, target_sem, out_sem = refs[16:]
 
     def load_rows(g):
         where = pl.ds(2 * g, 2)
@@ -340,7 +345,6 @@
     load_rows(0).start()
     loads = [pltpu.make_async_copy(to_full_hbm, to_full_ref, in_sem.at[0])]
     loads.append(pltpu.make_async_copy(to_half_hbm, to_half_ref, in_sem.at[1]))
-    loads.append(pltpu.make_async_copy(select_hbm, select_ref, in_sem.at[2]))
     for k in range(8):
         there = order_ref.at[jnp.bitwise_xor(place_ref[1], k)]
         loads.append(pltpu.make_async_copy(target_refs[k], there, target_sem.at[k]))
@@ -350,6 +354,7 @@
         load_rows(g).start()
     for copy in loads[2:]:
         copy.start()
+    mask_ref[...] = block_mask(256, "block")
     for copy in loads[:2]:
         copy.wait()
     base = place_ref[0] * 20
@@ -395,38 +400,48 @@
         copy.start()
 
     size = MEMBERS * GROUP
-    same = (iota((size, size), 0) & 15) == (iota((size, size), 1) & 15)
-    gather = ((iota((size, 128), 0) >> 4) == iota((size, 128), 1)).astype(F32).astype(BF)
-    at_observed = iota((size, 128), 1) == MEMBERS
+    same = (iota((JJ * GROUP, size), 0) & 15) == (iota((JJ * GROUP, size), 1) & 15)
+    empty = jnp.zeros((32 - JJ, size), F32)
 
     def gram(g, carry):
+        totals, last = carry
         start = pl.multiple_of(g * GROUP, GROUP)
-        block = stacked_ref[0:MEMBERS, pl.ds(start, GROUP), :].reshape(size, WIDE)
-        own = stacked_ref[MEMBERS, pl.ds(start, GROUP), :].astype(F32)
-        products = jnp.where(same, dot(block, block, 1, 1), 0.0)
-        high, mid, low_part = split3(products)
-        sums = dot(high, gather) + dot(mid, gather) + dot(low_part, gather)
-        beside = jnp.concatenate([own] * MEMBERS, axis=0) * block.astype(F32)
-        sums = jnp.where(at_observed, jnp.sum(beside, axis=1, keepdims=True), sums)
-        last = jnp.sum(own * own, axis=1, keepdims=True)
-        pieces = [sums[GROUP * i : GROUP * i + GROUP] for i in range(MEMBERS)]
-        pieces.append(jnp.where(at_observed[:GROUP], last, 0.0))
-        for n in range(3):
-            total = pieces[7 * n]
-            for i in range(7 * n + 1, min(7 * n + 7, JJ)):
-                total = total + pltpu.roll(pieces[i], JJ * (i % 7), 1)
-            terms_ref[n, pl.ds(start, GROUP), :] = total
-        return carry
-
-    lax.fori_loop(0, NGROUPS, gram, 0, unroll=4)
-
-    column = jnp.broadcast_to(band_column(target_ref, 0, L), (L, 128))
-    one_hot = (column == iota((L, 128), 1).astype(F32)).astype(F32).astype(BF)
-    squares = jnp.zeros((NBANDS, 128), F32)
-    for n in range(3):
-        total = sum(dot(one_hot, part, 0, 0) for part in split3(terms_ref[n]))[:NBANDS]
-        for part in split3(total):
-            squares = squares + dot(part, select_ref[128 * n : 128 * n + 128, :])
+        block = stacked_ref[:, pl.ds(start, GROUP), :].reshape(JJ * GROUP, WIDE)
+        products = jnp.where(same, dot(block, block[:size], 1, 1), 0.0)
+        products = jnp.sum(products.reshape(JJ, GROUP, size), axis=1)
+        parts = split3(jnp.concatenate([products, empty], axis=0))
+        bands = band_column(target_ref, start, GROUP)
+        moved = dot(jnp.concatenate(parts, axis=0), pick_bands(bands, mask_ref[...]))
+        totals = totals + (moved[:32] + moved[32:64] + moved[64:])
+        own = block[size:].astype(F32)
+        power = jnp.sum(own * own, axis=1, keepdims=True)
+        lane = (iota((GROUP, 128), 1) & 15).astype(F32)
+        power = jnp.where(jnp.broadcast_to(bands, (GROUP, 128)) == lane, power, 0.0)
+        return totals, last + jnp.sum(power, axis=0, keepdims=True)
+
+    start = (jnp.zeros((32, size), F32), jnp.zeros((1, 128), F32))
+    totals, last = lax.fori_loop(0, NGROUPS, gram, start, unroll=2)
+
+    grams = totals[:MEMBERS]
+    member = iota((MEMBERS, size), 1) >> 4
+    diagonal = jnp.where(iota((MEMBERS, size), 0) == member, grams, 0.0)
+    powers = jnp.sum(diagonal, axis=0, keepdims=True)
+    own_power = fold(diagonal)
+    squares = jnp.concatenate([own_power, own_power], axis=1) + powers - 2.0 * grams
+    beside = powers + jnp.concatenate([last, last], axis=1) - 2.0 * totals[MEMBERS : MEMBERS + 1]
+    beside = jnp.broadcast_to(beside, (MEMBERS, size))
+    chosen = fold(jnp.where(iota((MEMBERS, size), 0) == member, beside, 0.0))
+    kind = iota((MEMBERS, 128), 1) >> 4
+    wanted = jnp.where(kind == 0, chosen, 0.0)
+    for p in range(PARTNERS):
+        other = other_ref[GROUP * (p + 1) : GROUP * (p + 2), :]
+        other = jnp.concatenate([other, other], axis=1)
+        chosen = fold(jnp.where(member == other, squares, 0.0))
+        wanted = wanted + jnp.where(kind == p + 1, chosen, 0.0)
+    wanted = jnp.concatenate([wanted, jnp.zeros((112, 128), F32)], axis=0).T
+    squares = wanted[:NBANDS]
+    for c in range(1, PARTNERS + 1):
+        squares = squares + pltpu.roll(wanted[16 * c : 16 * c + 16], 16 * c, 1)
     sums = compact(squares)
     sums = jnp.concatenate([sums] * 4, axis=0)
     sums_ref[...] = jnp.broadcast_to(sums[None], (32, 40, 128))
@@ -438,7 +453,7 @@
         store(g).wait()
 
 
-def spectra(place, rows, to_full, to_half, select, targets):
+def spectra(place, rows, to_full, to_half, other, targets):
     return pl.pallas_call(
         spectra_kernel,
         out_shape=[
@@ -446,19 +461,18 @@
             jax.ShapeDtypeStruct((L, WIDE), BF),
             jax.ShapeDtypeStruct((32, 40, 128), F32),
         ],
-        in_specs=[SMEM] + [HBM] * 12,
+        in_specs=[SMEM] + [HBM] * 3 + [VMEM] + [HBM] * 8,
         out_specs=[HBM] * 3,
         scratch_shapes=[
             pltpu.VMEM((2, 2, L, 640), BF),
             pltpu.VMEM((2, 2, L, WIDE), BF),
-            pltpu.VMEM((WIDE, 128), BF),
             pltpu.VMEM((JJ, L, WIDE), BF),
             pltpu.VMEM((L, WIDE), BF),
             pltpu.VMEM((32, 40, 128), F32),
             pltpu.VMEM((16, 8, 104, 128), BF),
-            pltpu.VMEM((3, L, 128), F32),
+            pltpu.VMEM((256, 256), BF),
             pltpu.VMEM((8, 40, WIDE), BF),
-            pltpu.SemaphoreType.DMA((3,)),
+            pltpu.SemaphoreType.DMA((2,)),
             pltpu.SemaphoreType.DMA((4,)),
             pltpu.SemaphoreType.DMA((8,)),
             pltpu.SemaphoreType.DMA((7,)),
@@ -468,7 +482,7 @@
             flops=10_000_000_000, bytes_accessed=12_000_000, transcendentals=0
         ),
         name="spectra",
-    )(place, rows, to_full, to_half, select, *targets)
+    )(place, rows, to_full, to_half, other, *targets)
 
 
 def gradient_kernel(
@@ -476,7 +490,7 @@
     from_full_hbm, from_half_hbm,
     back_ref, grad_hbm, loss_ref,
     stacked_ref, target_ref, to_mixing_ref, from_full_ref, from_half_ref, grad_ref,
-    held_ref, in_sem, sem,
+    held_ref, member_ref, degree_ref, in_sem, stacked_sem, sem,
 ):
     loads = [
         pltpu.make_async_copy(there, here, in_sem.at[n])
@@ -484,14 +498,31 @@
             (
                 (to_mixing_hbm, to_mixing_ref),
                 (target_hbm, target_ref),
-                (stacked_hbm, stacked_ref),
                 (from_full_hbm, from_full_ref),
                 (from_half_hbm, from_half_ref),
             )
         )
     ]
-    for copy in loads:
+    piece = L // 4
+
+    def load_piece(n):
+        where = pl.ds(piece * n, piece)
+        return pltpu.make_async_copy(
+            stacked_hbm.at[:, where], stacked_ref.at[:, where], stacked_sem.at[n]
+        )
+
+    def keep_piece(n):
+        where = pl.ds(piece * n, piece)
+        return pltpu.make_async_copy(grad_ref.at[:, where], grad_hbm.at[:, where], sem.at[4 + n])
+
+    for copy in loads[:2]:
         copy.start()
+    for n in range(4):
+        load_piece(n).start()
+    for copy in loads[2:]:
+        copy.start()
+    member_ref[...] = block_mask(256, "block")
+    degree_ref[...] = block_mask(256, "inside")
     sums = jnp.sum(sums_ref[...], axis=0)
     sums = sum(sums[10 * n : 10 * n + 10] for n in range(4))
     lane = iota((NBANDS, 128), 1)
@@ -513,18 +544,15 @@
     mix_low = dot(mix_low, widen).astype(BF)
     beside = jnp.concatenate([beside, jnp.zeros((128 - NBANDS, 128), F32)], axis=0)
     beside_high, beside_low = split2(beside)
-    same_member = (iota((size, size), 0) >> 4) == (iota((size, size), 1) >> 4)
-    band_of_column = (iota((size, size), 1) & 15).astype(F32)
-    same_degree = (iota((size, size), 0) & 15) == (iota((size, size), 1) & 15)
     band_of_lane = iota((GROUP, 128), 1).astype(F32)
 
     def mix(g, carry):
         start = pl.multiple_of(g * GROUP, GROUP)
         bands = band_column(target_ref, start, GROUP)
-        column = jnp.concatenate([jnp.broadcast_to(bands, (GROUP, size))] * MEMBERS, axis=0)
-        pick = (same_member & (column == band_of_column)).astype(F32).astype(BF)
-        high = jnp.where(same_degree, dot(pick, mix_high), 0.0).astype(BF)
-        low = jnp.where(same_degree, dot(pick, mix_low), 0.0).astype(BF)
+        pick = pick_bands(bands, member_ref[...])
+        degree = degree_ref[...]
+        high = dot(pick, mix_high).astype(BF) * degree
+        low = dot(pick, mix_low).astype(BF) * degree
         one_hot = (jnp.broadcast_to(bands, (GROUP, 128)) == band_of_lane).astype(F32).astype(BF)
         weights = dot(one_hot, beside_high) + dot(one_hot, beside_low)
         weights = jnp.concatenate(
@@ -540,12 +568,12 @@
         return carry
 
     loads[1].wait()
-    loads[2].wait()
-    lax.fori_loop(0, NGROUPS, mix, 0, unroll=2)
-    kept = pltpu.make_async_copy(grad_ref, grad_hbm, sem.at[4])
-    kept.start()
-    loads[3].wait()
-    loads[4].wait()
+    for n in range(4):
+        load_piece(n).wait()
+        lax.fori_loop(5 * n, 5 * n + 5, mix, 0, unroll=5)
+        keep_piece(n).start()
+    for copy in loads[2:]:
+        copy.wait()
     def inverse(g, carry):
         for slot in range(3):
             grads = [jnp.concatenate(grads_of(grad_ref, g, i, slot), axis=1) for i in range(2)]
@@ -569,7 +597,7 @@
     lax.fori_loop(0, 4, inverse, 0)
     for g in range(4):
         send(g).wait()
-    kept.wait()
+        keep_piece(g).wait()
 
 
 def grads_of(grad_ref, g, i, slot):
@@ -595,8 +623,11 @@
             pltpu.VMEM((2, 2, WIDE, L), BF),
             pltpu.VMEM((MEMBERS, L, WIDE), BF),
             pltpu.VMEM((16, 8, 104, 128), BF),
-            pltpu.SemaphoreType.DMA((5,)),
-            pltpu.SemaphoreType.DMA((5,)),
+            pltpu.VMEM((256, 256), BF),
+            pltpu.VMEM((256, 256), BF),
+            pltpu.SemaphoreType.DMA((4,)),
+            pltpu.SemaphoreType.DMA((4,)),
+            pltpu.SemaphoreType.DMA((8,)),
         ],
         compiler_params=pltpu.CompilerParams(vmem_limit_bytes=63 * MIB),
         cost_estimate=pl.CostEstimate(
@@ -712,20 +743,25 @@
     by_order = jnp.transpose(analysis, (1, 0, 2))
     native = jnp.transpose(fourier[0].reshape(2, 20, 320, 128), (1, 2, 0, 3)).reshape(20, 640, 128)
     packed = pack(native)
-    target_in, partners, full, place, packed = lax.optimization_barrier(
-        (target[0], partners, full, place, packed)
+    target_in, partners, full, cotangent, packed = lax.optimization_barrier(
+        (target[0], partners, full, band_cotangent, packed)
     )
     rows = travel(packed)
     targets = swap(target_blocks(place, target_in, band_ids))
-    to_full, to_half, from_full, from_half, select, to_mixing = prepare(
-        place, by_order, full, half, partners
+    other = jnp.concatenate(
+        [jnp.full((16,), MEMBERS, jnp.int32), partners.T.reshape(64), jnp.zeros((48,), jnp.int32)]
     )
-    cotangent = lax.dynamic_slice_in_dim(band_cotangent, lax.axis_index("dp"), 1, 0)[0]
+    other = jnp.broadcast_to(other[:, None], (128, 128))
+    to_full, to_half, from_full, from_half, to_mixing = prepare(
+        place, by_order, full, half, other
+    )
+    cotangent = lax.dynamic_slice_in_dim(cotangent, lax.axis_index("dp"), 1, 0)[0]
     cotangent = jnp.broadcast_to(cotangent[:, None], (NBANDS, 128))
+    cotangent, rows = lax.optimization_barrier((cotangent, rows))
     share = np.zeros((8, 128), np.float32)
     share[:, :16] = 1.0 / MEMBERS
     share[:, 16:80] = -1.0 / (2.0 * MEMBERS * PARTNERS)
-    stacked, observed, sums = spectra(place, rows, to_full, to_half, select, targets)
+    stacked, observed, sums = spectra(place, rows, to_full, to_half, other, targets)
     sums = exchange(sums.reshape(128, 5, 2, 128), EVERY).reshape(32, 40, 128)
     back, grads, loss = gradient(
         stacked, observed, sums, cotangent, jnp.asarray(share), to_mixing, from_full, from_half
@@ -736,8 +772,9 @@
     weight = weights(place, rows, grads, full, half)
     beside = lax.ppermute(weight[1], "dp", [(0, 1), (1, 0)])
     weight = (weight[0].astype(F32) + beside.astype(F32)).astype(BF)
+    native_grad, place = lax.optimization_barrier((unpack(returned), place))
     grad_analysis = finish(place, swap([weight[k] for k in range(8)]))
-    native_grad = unpack(returned).reshape(20, 320, 2, 128)
+    native_grad = native_grad.reshape(20, 320, 2, 128)
     grad_fourier = jnp.transpose(native_grad, (2, 0, 1, 3)).reshape(1, 2, 20, 40960)
     return (grad_fourier, grad_analysis, loss_bands)
 

time: 286 us -> 278 us (0.972)
  blocking collectives: 0 us -> 31.5 us
  waiting for transfers between devices: 128 us -> 103 us
  starting transfers between devices: 72 us -> 62.2 us
  Pallas kernels: 74.1 us -> 69.2 us
    ppermute x14, waiting for transfers between devices: 103 us -> 47.9 us  [swap(): lax.ppermute(blocks[k], ENS, [(e, e ^ k) for e in range(8)])]
    all_to_all x0 -> x1, blocking collectives: none -> 31.5 us  [exchange(): return lax.all_to_all(x, axes, split_axis=0, concat_axis=0, tiled=True)]
    all_to_all x3 -> x2, waiting for transfers between devices: 23.2 us -> 53.3 us  [exchange(): return lax.all_to_all(x, axes, split_axis=0, concat_axis=0, tiled=True)]
    all_to_all x3 -> x2, starting transfers between devices: 33.3 us -> 23.5 us  [exchange(): return lax.all_to_all(x, axes, split_axis=0, concat_axis=0, tiled=True)]
  transfers between devices with their start and end apart: 19 -> 18, of which waited for: 10 -> 5; matrix products, arithmetic and copies ran while one was open for 2% -> 2% of each run, Pallas kernels for 8% -> 10%
where the time goes in v4:
time: 278 us; the launch traced here: 274 us
  waiting for transfers between devices  103 us (37%)
  Pallas kernels  69.2 us (25%)
  starting transfers between devices  62.2 us (22%)
  blocking collectives  31.5 us (11%)
  local copies, waits for them, and re-layouts  5.26 us (2%)
    all_to_all x2, waiting for transfers between devices, exchange(): return lax.all_to_all(x, axes, split_axis=0, concat_axis=0, tiled=True)  53.3 us
    ppermute x14, waiting for transfers between devices, swap(): lax.ppermute(blocks[k], ENS, [(e, e ^ k) for e in range(8)])  47.9 us
    ppermute x14, starting transfers between devices, swap(): lax.ppermute(blocks[k], ENS, [(e, e ^ k) for e in range(8)])  38.4 us
    all_to_all x1, blocking collectives, exchange(): return lax.all_to_all(x, axes, split_axis=0, concat_axis=0, tiled=True)  31.5 us
    all_to_all x2, starting transfers between devices, exchange(): return lax.all_to_all(x, axes, split_axis=0, concat_axis=0, tiled=True)  23.5 us
    pallas_call x1, Pallas kernels, gradient(): pl.pallas_call(gradient_kernel, out_shape=[jax.ShapeDtypeStruct((16, 8, 1...  16.3 us
    pallas_call x1, Pallas kernels, spectra(): pl.pallas_call(spectra_kernel, out_shape=[jax.ShapeDtypeStruct((JJ, L, WI...  15 us
    pallas_call x1, Pallas kernels, weights(): pl.pallas_call(weight_kernel, out_shape=jax.ShapeDtypeStruct((2, 8, 3, 20...  11.6 us
  transfers between devices with their start and end apart: 18, of which 5 were waited for; matrix products, arithmetic and copies ran while one was open for 2% of the time, Pallas kernels for 10%

profile of v4, /device:TPU:8, one launch (start us, length us, event | category | flops | bytes accessed | tf_op | source)
XLA Modules:
  0.0 274.4 jit_solution(2493037143027958816)
XLA Ops:
  0.6 7.8 %pack.1 = bf16[16,8,104,128]{3,2,1,0:T(8,128)(2,1)} custom-call(bf16[20,640,128]{2,1,0:T(8,128)(2,1)} %bitcast.50, bf16[320,320]{1,0:T(8,128)(2,1)} %constant.45.clone.whole_ref, bf16[2,96,160]{2,1,0:T(8,128)(2,1)} %constant.46.clone.half_ref), custom_call_target="tpu_custom_call" | custom-call | tf_op jit(solution)/shard_map/pack/pallas_call | solution.py:143
  8.5 15.9 %all-to-all-start = ((bf16[128,52,2,128]{3,2,1,0:T(2,128)(2,1)}), bf16[128,52,2,128]{3,2,1,0:T(2,128)(2,1)}, u32[]{:S(2)}, u32[]{:S(2)}) async-start(bf16[128,52,2,128]{3,2,1,0:T(2,128)(2,1)} %bitcast.47), calls=%async_computation | async-start | bytes 6815744 | tf_op jit(solution)/shard_map/all_to_all | solution.py:724
  24.4 0.7 copy.20.band_ref
  25.1 0.7 pad_add_fusion.place_ref
  25.7 1.8 target_blocks.1
  27.6 1.6 collective-permute-start
  29.1 2.7 collective-permute-start.1
  31.8 0.6 collective-permute-start.2
  32.4 5.4 %collective-permute-start.3 = (bf16[40,384]{1,0:T(8,128)(2,1)}, bf16[40,384]{1,0:T(8,128)(2,1)S(1)}, u32[]{:S(2)}, u32[]{:S(2)}) collective-permute-start(bf16[40,384]{1,0:T(8,128)(2,1)} %get-tuple-element.43), channel_id=1, source_target_pairs={{0,4},{1,5},{2,6},{3,7},{4,0},{5,1},{6,2},{7,3},{8,12},{9,13},{10,... | collective-permute-start | bytes 92168 | tf_op jit(solution)/shard_map/ppermute | solution.py:729
  37.7 0.2 collective-permute-start.4
  38.0 0.1 reshape.43
  38.1 8.8 %collective-permute-start.5 = (bf16[40,384]{1,0:T(8,128)(2,1)}, bf16[40,384]{1,0:T(8,128)(2,1)S(1)}, u32[]{:S(2)}, u32[]{:S(2)}) collective-permute-start(bf16[40,384]{1,0:T(8,128)(2,1)} %get-tuple-element.45), channel_id=1, source_target_pairs={{0,6},{1,7},{2,4},{3,5},{4,2},{5,3},{6,0},{7,1},{8,14},{9,15},{10,... | collective-permute-start | bytes 92168 | tf_op jit(solution)/shard_map/ppermute | solution.py:729
  46.9 0.6 collective-permute-start.6
  47.4 0.1 pad_add_fusion.1
  47.5 0.7 broadcast_in_dim.19.other_column_ref.other_ref
  48.2 6.9 %prepare.1 = (bf16[2,2,320,640]{3,2,1,0:T(8,128)(2,1)}, bf16[2,2,320,384]{3,2,1,0:T(8,128)(2,1)}, bf16[2,2,640,320]{3,2,1,0:T(8,128)(2,1)}, bf16[2,2,384,320]{3,2,1,0:T(8,128)(2,1)}, bf16[128,2048]{1,0:T(8,128)(2,1)}) custom-call(s32[3]{0:T(128)} %pad_add_fusion.place_ref, bf16[20,320,320]{2,1,0:T(8,128)(2,1)} %bitcast.48, ...), custom_call_target="tpu_custom_call" | custom-call | tf_op jit(solution)/shard_map/prepare/pallas_call | solution.py:269
  55.1 52.8 %all-to-all-done = bf16[128,52,2,128]{3,2,1,0:T(2,128)(2,1)} async-done(((bf16[128,52,2,128]{3,2,1,0:T(2,128)(2,1)}), bf16[128,52,2,128]{3,2,1,0:T(2,128)(2,1)}, u32[]{:S(2)}, u32[]{:S(2)}) %all-to-all-start) | async-done | bytes 3407904 | tf_op jit(solution)/shard_map/all_to_all | solution.py:724
  108.0 0.7 broadcast_in_dim.17.cotangent_ref
  108.7 0.5 copy-done.13
  109.2 0.0 copy-done.15
  109.3 0.0 copy-done.17
  109.3 15.0 %spectra.1 = (bf16[17,320,384]{2,1,0:T(8,128)(2,1)}, bf16[320,384]{1,0:T(8,128)(2,1)}, f32[32,40,128]{2,1,0:T(8,128)}) custom-call(s32[3]{0:T(128)} %pad_add_fusion.place_ref, bf16[16,8,104,128]{3,2,1,0:T(8,128)(2,1)} %bitcast.9.rows_hbm.rows_ref, bf16[2,2,320,640]{3,2,1,0:T(8,128)(2,1)} %get-tuple-element.36.to_full_hbm, ...), custom_call_target="tpu_custom_call" | custom-call | flops 10000000000 | bytes 12000000 | tf_op jit(solution)/shard_map/spectra/pallas_call | solution.py:457
  124.4 31.5 %all_to_all.15 = f32[128,5,2,128]{3,2,1,0:T(2,128)} all-to-all(f32[128,5,2,128]{3,2,1,0:T(2,128)} %bitcast.52), channel_id=1, replica_groups=mesh['dp'=2,'order_0'=4,'order_1'=4,'ens_0'=2,'ens_1'=4] {'order_0','ord..., dimensions={0} | all-to-all | bytes 1310720 | tf_op jit(solution)/shard_map/all_to_all | solution.py:724
  155.8 16.3 %gradient.1 = (bf16[16,8,104,128]{3,2,1,0:T(8,128)(2,1)}, bf16[16,320,384]{2,1,0:T(8,128)(2,1)}, f32[16,128]{1,0:T(8,128)}) custom-call(bf16[17,320,384]{2,1,0:T(8,128)(2,1)} %get-tuple-element.47.stacked_hbm, bf16[320,384]{1,0:T(8,128)(2,1)} %get-tuple-element.48.target_hbm, f32[32,40,128]{2,1,0:T(8,128)} %bitcast.53, ...), custom_call_target="tpu_custom_call" | custom-call | flops 10000000000 | bytes 12000000 | tf_op jit(solution)/shard_map/gradient/pallas_call | solution.py:609
  172.2 7.7 %all-to-all-start.2 = ((bf16[128,52,2,128]{3,2,1,0:T(2,128)(2,1)}), bf16[128,52,2,128]{3,2,1,0:T(2,128)(2,1)}, u32[]{:S(2)}, u32[]{:S(2)}) async-start(bf16[128,52,2,128]{3,2,1,0:T(2,128)(2,1)} %bitcast.49), calls=%async_computation.2 | async-start | bytes 6815744 | tf_op jit(solution)/shard_map/all_to_all | solution.py:724
  179.8 11.6 %weights.1 = bf16[2,8,3,20,320]{4,3,2,1,0:T(8,128)(2,1)} custom-call(s32[3]{0:T(128)} %pad_add_fusion.place_ref, bf16[16,8,104,128]{3,2,1,0:T(8,128)(2,1)} %bitcast.9.rows_hbm.rows_ref, bf16[16,320,384]{2,1,0:T(8,128)(2,1)} %get-tuple-element.57.grad_ref, bf16[320,640]{1,0:T(8,128)(2,1)} %constant.43.clone.full_ref, bf16[2,320,384]{2,1,0:T(8,128)(2,1)} %constant.44.clone.half_ref), custom_call_target="tpu_custom_call" | custom-call | flops 5000000000 | bytes 8000000 | tf_op jit(solution)/shard_map/weights/pallas_call | solution.py:684
  191.4 1.1 slice_bitcast_fusion
  192.5 0.1 collective-permute-start.7
  192.6 1.8 collective-permute-done.7
  194.4 1.1 fusion
  195.5 0.7 slice_bitcast_fusion.2
  196.2 7.5 %collective-permute-start.14 = (bf16[3,20,320]{2,1,0:T(8,128)(2,1)S(1)}, bf16[3,20,320]{2,1,0:T(8,128)(2,1)S(1)}, u32[]{:S(2)}, u32[]{:S(2)}) collective-permute-start(bf16[3,20,320]{2,1,0:T(8,128)(2,1)S(1)} %get-tuple-element.59), channel_id=1, source_target_pairs={{0,7},{1,6},{2,5},{3,4},{4,3},{5,2},{6,1},{7,0},{8,15},{9,14},{10,... | collective-permute-start | bytes 115208 | tf_op jit(solution)/shard_map/ppermute | solution.py:729
  203.7 0.9 collective-permute-start.13
  204.6 0.1 slice_reduce_fusion
  204.7 0.1 collective-permute-start.15
  204.8 5.5 %collective-permute-start.12 = (bf16[3,20,320]{2,1,0:T(8,128)(2,1)S(1)}, bf16[3,20,320]{2,1,0:T(8,128)(2,1)S(1)}, u32[]{:S(2)}, u32[]{:S(2)}) collective-permute-start(bf16[3,20,320]{2,1,0:T(8,128)(2,1)S(1)} %get-tuple-element.61), channel_id=1, source_target_pairs={{0,5},{1,4},{2,7},{3,6},{4,1},{5,0},{6,3},{7,2},{8,13},{9,12},{10,... | collective-permute-start | bytes 115208 | tf_op jit(solution)/shard_map/ppermute | solution.py:729
  210.2 0.6 collective-permute-start.11
  210.8 2.7 collective-permute-start.10
  213.5 46.6 %collective-permute-done.14.refs_7_ = bf16[3,20,320]{2,1,0:T(8,128)(2,1)S(1)} collective-permute-done((bf16[3,20,320]{2,1,0:T(8,128)(2,1)S(1)}, bf16[3,20,320]{2,1,0:T(8,128)(2,1)S(1)}, u32[]{:S(2)}, u32[]{:S(2)}) %collective-permute-start.14) | collective-permute-done | bytes 38432 | tf_op jit(solution)/shard_map/ppermute | solution.py:729
  260.1 1.4 collective-permute-start.9
  261.5 1.2 collective-permute-done.13.refs_6_
  262.7 0.3 collective-permute-start.8
  263.0 0.5 add.19
  263.5 0.5 all-to-all-done.2
  264.0 7.5 %unpack.1 = bf16[20,640,128]{2,1,0:T(8,128)(2,1)} custom-call(bf16[16,8,104,128]{3,2,1,0:T(8,128)(2,1)} %bitcast.15.y_ref, bf16[320,320]{1,0:T(8,128)(2,1)} %constant.48.clone.whole_ref, bf16[2,160,96]{2,1,0:T(8,128)(2,1)} %constant.49.clone.half_ref), custom_call_target="tpu_custom_call" | custom-call | tf_op jit(solution)/shard_map/unpack/pallas_call | solution.py:154
  271.6 0.5 copy-done.3
  272.2 0.0 copy-done.6
  272.3 2.1 finish.1
  (47 shorter events, 0.2 us)
Async XLA Ops:
  0.6 37.4 %copy-start = (f32[2,16]{1,0:T(2,128)S(1)}, f32[2,16]{1,0:T(2,128)}, u32[]{:S(2)}) copy-start(f32[2,16]{1,0:T(2,128)} %param.18) | copy-start | bytes 388
  8.5 15.9 %copy-start.8 = (s32[40,20]{0,1:T(8,128)S(1)}, s32[40,20]{0,1:T(8,128)}, u32[]{:S(2)}) copy-start(s32[40,20]{0,1:T(8,128)} %param.16) | copy-start | bytes 9604
  8.5 29.5 %copy-start.10 = (s32[16,4]{0,1:T(4,128)S(1)}, s32[16,4]{0,1:T(4,128)}, u32[]{:S(2)}) copy-start(s32[16,4]{0,1:T(4,128)} %param.17) | copy-start | bytes 772
  8.5 99.5 %all-to-all-start = ((bf16[128,52,2,128]{3,2,1,0:T(2,128)(2,1)}), bf16[128,52,2,128]{3,2,1,0:T(2,128)(2,1)}, u32[]{:S(2)}, u32[]{:S(2)}) async-start(bf16[128,52,2,128]{3,2,1,0:T(2,128)(2,1)} %bitcast.47), calls=%async_computation | async-start | bytes 6815744 | tf_op jit(solution)/shard_map/all_to_all | solution.py:724
  27.6 10.5 %collective-permute-start = (bf16[40,384]{1,0:T(8,128)(2,1)}, bf16[40,384]{1,0:T(8,128)(2,1)S(1)}, u32[]{:S(2)}, u32[]{:S(2)}) collective-permute-start(bf16[40,384]{1,0:T(8,128)(2,1)} %get-tuple-element.40), channel_id=1, source_target_pairs={{0,1},{1,0},{2,3},{3,2},{4,5},{5,4},{6,7},{7,6},{8,9},{9,8},{10,11... | collective-permute-start | bytes 92168 | tf_op jit(solution)/shard_map/ppermute | solution.py:729
  29.1 17.7 %collective-permute-start.1 = (bf16[40,384]{1,0:T(8,128)(2,1)}, bf16[40,384]{1,0:T(8,128)(2,1)S(1)}, u32[]{:S(2)}, u32[]{:S(2)}) collective-permute-start(bf16[40,384]{1,0:T(8,128)(2,1)} %get-tuple-element.41), channel_id=1, source_target_pairs={{0,2},{1,3},{2,0},{3,1},{4,6},{5,7},{6,4},{7,5},{8,10},{9,11},{10,... | collective-permute-start | bytes 92168 | tf_op jit(solution)/shard_map/ppermute | solution.py:729
  31.8 76.8 %collective-permute-start.2 = (bf16[40,384]{1,0:T(8,128)(2,1)}, bf16[40,384]{1,0:T(8,128)(2,1)S(1)}, u32[]{:S(2)}, u32[]{:S(2)}) collective-permute-start(bf16[40,384]{1,0:T(8,128)(2,1)} %get-tuple-element.42), channel_id=1, source_target_pairs={{0,3},{1,2},{2,1},{3,0},{4,7},{5,6},{6,5},{7,4},{8,11},{9,10},{10,... | collective-permute-start | bytes 92168 | tf_op jit(solution)/shard_map/ppermute | solution.py:729
  32.4 76.3 %collective-permute-start.3 = (bf16[40,384]{1,0:T(8,128)(2,1)}, bf16[40,384]{1,0:T(8,128)(2,1)S(1)}, u32[]{:S(2)}, u32[]{:S(2)}) collective-permute-start(bf16[40,384]{1,0:T(8,128)(2,1)} %get-tuple-element.43), channel_id=1, source_target_pairs={{0,4},{1,5},{2,6},{3,7},{4,0},{5,1},{6,2},{7,3},{8,12},{9,13},{10,... | collective-permute-start | bytes 92168 | tf_op jit(solution)/shard_map/ppermute | solution.py:729
  37.7 70.9 %collective-permute-start.4 = (bf16[40,384]{1,0:T(8,128)(2,1)}, bf16[40,384]{1,0:T(8,128)(2,1)S(1)}, u32[]{:S(2)}, u32[]{:S(2)}) collective-permute-start(bf16[40,384]{1,0:T(8,128)(2,1)} %get-tuple-element.44), channel_id=1, source_target_pairs={{0,5},{1,4},{2,7},{3,6},{4,1},{5,0},{6,3},{7,2},{8,13},{9,12},{10,... | collective-permute-start | bytes 92168 | tf_op jit(solution)/shard_map/ppermute | solution.py:729
  38.1 70.6 %copy-start.11 = (bf16[40,384]{1,0:T(8,128)(2,1)}, bf16[40,384]{1,0:T(8,128)(2,1)S(1)}, u32[]{:S(2)}) copy-start(bf16[40,384]{1,0:T(8,128)(2,1)S(1)} %collective-permute-done.refs_1_) | copy-start | bytes 92164
  38.1 70.6 %collective-permute-start.5 = (bf16[40,384]{1,0:T(8,128)(2,1)}, bf16[40,384]{1,0:T(8,128)(2,1)S(1)}, u32[]{:S(2)}, u32[]{:S(2)}) collective-permute-start(bf16[40,384]{1,0:T(8,128)(2,1)} %get-tuple-element.45), channel_id=1, source_target_pairs={{0,6},{1,7},{2,4},{3,5},{4,2},{5,3},{6,0},{7,1},{8,14},{9,15},{10,... | collective-permute-start | bytes 92168 | tf_op jit(solution)/shard_map/ppermute | solution.py:729
  46.9 61.9 %copy-start.12 = (bf16[40,384]{1,0:T(8,128)(2,1)}, bf16[40,384]{1,0:T(8,128)(2,1)S(1)}, u32[]{:S(2)}) copy-start(bf16[40,384]{1,0:T(8,128)(2,1)S(1)} %collective-permute-done.1.refs_2_) | copy-start | bytes 92164
  46.9 61.8 %collective-permute-start.6 = (bf16[40,384]{1,0:T(8,128)(2,1)}, bf16[40,384]{1,0:T(8,128)(2,1)S(1)}, u32[]{:S(2)}, u32[]{:S(2)}) collective-permute-start(bf16[40,384]{1,0:T(8,128)(2,1)} %get-tuple-element.46), channel_id=1, source_target_pairs={{0,7},{1,6},{2,5},{3,4},{4,3},{5,2},{6,1},{7,0},{8,15},{9,14},{10,... | collective-permute-start | bytes 92168 | tf_op jit(solution)/shard_map/ppermute | solution.py:729
  108.6 0.6 copy-start.13
  108.6 0.6 copy-start.14
  108.6 0.6 copy-start.15
  108.7 0.6 copy-start.16
  108.7 0.6 copy-start.17
  172.2 91.9 %all-to-all-start.2 = ((bf16[128,52,2,128]{3,2,1,0:T(2,128)(2,1)}), bf16[128,52,2,128]{3,2,1,0:T(2,128)(2,1)}, u32[]{:S(2)}, u32[]{:S(2)}) async-start(bf16[128,52,2,128]{3,2,1,0:T(2,128)(2,1)} %bitcast.49), calls=%async_computation.2 | async-start | bytes 6815744 | tf_op jit(solution)/shard_map/all_to_all | solution.py:724
  179.8 24.7 %copy-start.9 = (f32[16,128]{1,0:T(8,128)S(1)}, f32[16,128]{1,0:T(8,128)}, u32[]{:S(2)}) copy-start(f32[16,128]{1,0:T(8,128)} %get-tuple-element.58) | copy-start | bytes 24580
  192.5 1.9 collective-permute-start.7
  196.2 63.9 %collective-permute-start.14 = (bf16[3,20,320]{2,1,0:T(8,128)(2,1)S(1)}, bf16[3,20,320]{2,1,0:T(8,128)(2,1)S(1)}, u32[]{:S(2)}, u32[]{:S(2)}) collective-permute-start(bf16[3,20,320]{2,1,0:T(8,128)(2,1)S(1)} %get-tuple-element.59), channel_id=1, source_target_pairs={{0,7},{1,6},{2,5},{3,4},{4,3},{5,2},{6,1},{7,0},{8,15},{9,14},{10,... | collective-permute-start | bytes 115208 | tf_op jit(solution)/shard_map/ppermute | solution.py:729
  203.7 59.0 %collective-permute-start.13 = (bf16[3,20,320]{2,1,0:T(8,128)(2,1)S(1)}, bf16[3,20,320]{2,1,0:T(8,128)(2,1)S(1)}, u32[]{:S(2)}, u32[]{:S(2)}) collective-permute-start(bf16[3,20,320]{2,1,0:T(8,128)(2,1)S(1)} %get-tuple-element.60), channel_id=1, source_target_pairs={{0,6},{1,7},{2,4},{3,5},{4,2},{5,3},{6,0},{7,1},{8,14},{9,15},{10,... | collective-permute-start | bytes 115208 | tf_op jit(solution)/shard_map/ppermute | solution.py:729
  204.7 6.1 %collective-permute-start.15 = (f32[16]{0:T(128)S(1)}, f32[16]{0:T(128)S(1)}, u32[]{:S(2)}, u32[]{:S(2)}) collective-permute-start(f32[16]{0:T(128)S(1)} %slice_reduce_fusion), channel_id=1, source_target_pairs={{0,128},{128,0},{1,129},{129,1},{2,130},{130,2},{3,131},{131,3},{4... | collective-permute-start | bytes 200 | tf_op jit(solution)/shard_map/ppermute | solution.py:771
  204.8 66.8 %collective-permute-start.12 = (bf16[3,20,320]{2,1,0:T(8,128)(2,1)S(1)}, bf16[3,20,320]{2,1,0:T(8,128)(2,1)S(1)}, u32[]{:S(2)}, u32[]{:S(2)}) collective-permute-start(bf16[3,20,320]{2,1,0:T(8,128)(2,1)S(1)} %get-tuple-element.61), channel_id=1, source_target_pairs={{0,5},{1,4},{2,7},{3,6},{4,1},{5,0},{6,3},{7,2},{8,13},{9,12},{10,... | collective-permute-start | bytes 115208 | tf_op jit(solution)/shard_map/ppermute | solution.py:729
  210.2 61.3 %collective-permute-start.11 = (bf16[3,20,320]{2,1,0:T(8,128)(2,1)S(1)}, bf16[3,20,320]{2,1,0:T(8,128)(2,1)S(1)}, u32[]{:S(2)}, u32[]{:S(2)}) collective-permute-start(bf16[3,20,320]{2,1,0:T(8,128)(2,1)S(1)} %get-tuple-element.62), channel_id=1, source_target_pairs={{0,4},{1,5},{2,6},{3,7},{4,0},{5,1},{6,2},{7,3},{8,12},{9,13},{10,... | collective-permute-start | bytes 115208 | tf_op jit(solution)/shard_map/ppermute | solution.py:729
  210.8 60.8 %collective-permute-start.10 = (bf16[3,20,320]{2,1,0:T(8,128)(2,1)S(1)}, bf16[3,20,320]{2,1,0:T(8,128)(2,1)S(1)}, u32[]{:S(2)}, u32[]{:S(2)}) collective-permute-start(bf16[3,20,320]{2,1,0:T(8,128)(2,1)S(1)} %get-tuple-element.63), channel_id=1, source_target_pairs={{0,3},{1,2},{2,1},{3,0},{4,7},{5,6},{6,5},{7,4},{8,11},{9,10},{10,... | collective-permute-start | bytes 115208 | tf_op jit(solution)/shard_map/ppermute | solution.py:729
  260.1 11.4 %copy-start.1 = (bf16[3,20,320]{2,1,0:T(8,128)(2,1)}, bf16[3,20,320]{2,1,0:T(8,128)(2,1)S(1)}, u32[]{:S(2)}) copy-start(bf16[3,20,320]{2,1,0:T(8,128)(2,1)S(1)} %collective-permute-done.14.refs_7_) | copy-start | bytes 115204
  260.1 11.5 %collective-permute-start.9 = (bf16[3,20,320]{2,1,0:T(8,128)(2,1)S(1)}, bf16[3,20,320]{2,1,0:T(8,128)(2,1)S(1)}, u32[]{:S(2)}, u32[]{:S(2)}) collective-permute-start(bf16[3,20,320]{2,1,0:T(8,128)(2,1)S(1)} %get-tuple-element.64), channel_id=1, source_target_pairs={{0,2},{1,3},{2,0},{3,1},{4,6},{5,7},{6,4},{7,5},{8,10},{9,11},{10,... | collective-permute-start | bytes 115208 | tf_op jit(solution)/shard_map/ppermute | solution.py:729
  262.7 8.8 %copy-start.2 = (bf16[3,20,320]{2,1,0:T(8,128)(2,1)}, bf16[3,20,320]{2,1,0:T(8,128)(2,1)S(1)}, u32[]{:S(2)}) copy-start(bf16[3,20,320]{2,1,0:T(8,128)(2,1)S(1)} %collective-permute-done.13.refs_6_) | copy-start | bytes 115204
  262.7 8.9 %collective-permute-start.8 = (bf16[3,20,320]{2,1,0:T(8,128)(2,1)S(1)}, bf16[3,20,320]{2,1,0:T(8,128)(2,1)S(1)}, u32[]{:S(2)}, u32[]{:S(2)}) collective-permute-start(bf16[3,20,320]{2,1,0:T(8,128)(2,1)S(1)} %get-tuple-element.65), channel_id=1, source_target_pairs={{0,1},{1,0},{2,3},{3,2},{4,5},{5,4},{6,7},{7,6},{8,9},{9,8},{10,11... | collective-permute-start | bytes 115208 | tf_op jit(solution)/shard_map/ppermute | solution.py:729
  271.5 0.6 copy-start.3
  271.6 0.6 copy-start.4
  271.6 0.6 copy-start.5
  271.6 0.6 copy-start.6
  271.6 0.6 copy-start.7

commit v5 on v4

--- a/solution.py
+++ b/solution.py
@@ -44,13 +44,14 @@
 
 
 def orderings():
-    whole = np.zeros((320, 320), np.float32)
+    whole = np.zeros((64, 64), np.float32)
     half = np.zeros((2, 96, 160), np.float32)
-    for t in range(20):
-        h, s = divmod(t, 10)
-        for i in range(2):
+    for i in range(2):
+        for t in range(4):
             for e in range(8):
-                whole[40 * e + 2 * t + i, 16 * t + 2 * e + i] = 1.0
+                whole[8 * e + 2 * t + i, 16 * t + 2 * e + i] = 1.0
+        for t in range(20):
+            h, s = divmod(t, 10)
             for p in range(4):
                 half[h, 24 * p + 2 * s + i, 8 * t + 2 * p + i] = 1.0
     return whole, half
@@ -84,81 +85,166 @@
     return high, mid, (rest - mid.astype(F32)).astype(BF)
 
 
-def pack_kernel(x_ref, whole_ref, half_ref, o_ref):
-    def columns(start, count):
-        parts = [x_ref[:, 40 * k + start : 40 * k + start + count, :] for k in range(2)]
-        parts = [part.astype(F32).reshape(20 * count, 128).astype(BF) for part in parts]
-        return jnp.concatenate(parts, axis=1)
-
-    for slot in range(2):
-        moved = halves(dot(whole_ref[...], columns(16 * slot, 16)))
-        for k in range(2):
-            o_ref[k, :, 40 * slot : 40 * slot + 40, :] = moved[k].reshape(8, 40, 128).astype(BF)
-    values = columns(32, 8)
-    first = halves(dot(half_ref[0], values))
-    second = halves(dot(half_ref[1], values))
+STEP = 4
+
+
+def pack_step(x_ref, whole_ref, half_ref, o_ref):
+    def block(rows, columns):
+        return x_ref[rows, columns, :].astype(F32).reshape(-1, 128).astype(BF)
+
+    for k in range(STEP):
+        for slot in range(2):
+            start = 40 * k + 16 * slot
+            parts = [block(slice(4 * c, 4 * c + 4), slice(start, start + 16)) for c in range(5)]
+            moved = dot(whole_ref[...], jnp.concatenate(parts, axis=1))
+            moved = [moved[:, 128 * c : 128 * c + 128].reshape(8, 8, 128) for c in range(5)]
+            moved = jnp.concatenate(moved, axis=1).astype(BF)
+            o_ref[k, :, 40 * slot : 40 * slot + 40, :] = moved
+    parts = [block(slice(0, 20), slice(40 * k + 32, 40 * k + 40)) for k in range(STEP)]
+    values = jnp.concatenate(parts, axis=1)
+    firsts = dot(half_ref[0], values)
+    seconds = dot(half_ref[1], values)
     low = iota((96, 128), 1) < 64
-    for k in range(2):
-        real = jnp.where(low, first[k], swap_halves(second[k])).astype(BF)
-        imaginary = jnp.where(low, swap_halves(first[k]), second[k]).astype(BF)
+    for k in range(STEP):
+        first = firsts[:, 128 * k : 128 * k + 128]
+        second = seconds[:, 128 * k : 128 * k + 128]
+        real = jnp.where(low, first, swap_halves(second)).astype(BF)
+        imaginary = jnp.where(low, swap_halves(first), second).astype(BF)
         for p in range(4):
             o_ref[k, 2 * p, 80:104, :] = real[24 * p : 24 * p + 24]
             o_ref[k, 2 * p + 1, 80:104, :] = imaginary[24 * p : 24 * p + 24]
 
 
-def unpack_kernel(y_ref, whole_ref, half_ref, x_ref):
-    for slot in range(2):
-        parts = [y_ref[k, :, 40 * slot : 40 * slot + 40, :].astype(F32) for k in range(2)]
-        parts = [part.reshape(320, 128).astype(BF) for part in parts]
-        moved = halves(dot(whole_ref[...], jnp.concatenate(parts, axis=1)))
-        for k in range(2):
+def unpack_step(y_ref, whole_ref, half_ref, x_ref):
+    for k in range(STEP):
+        for slot in range(2):
+            rows = y_ref[k, :, 40 * slot : 40 * slot + 40, :].astype(F32)
+            parts = [rows[:, 8 * c : 8 * c + 8].reshape(64, 128).astype(BF) for c in range(5)]
+            moved = dot(whole_ref[...], jnp.concatenate(parts, axis=1))
+            moved = [moved[:, 128 * c : 128 * c + 128].reshape(4, 16, 128) for c in range(5)]
             start = 40 * k + 16 * slot
-            x_ref[:, start : start + 16, :] = moved[k].reshape(20, 16, 128).astype(BF)
+            x_ref[:, start : start + 16, :] = jnp.concatenate(moved, axis=0).astype(BF)
     low = iota((96, 128), 1) < 64
     firsts, seconds = [], []
-    for k in range(2):
+    for k in range(STEP):
         real, imaginary = [
             jnp.concatenate([y_ref[k, 2 * p + r, 80:104, :].astype(F32) for p in range(4)], axis=0)
             for r in range(2)
         ]
         firsts.append(jnp.where(low, real, swap_halves(imaginary)).astype(BF))
         seconds.append(jnp.where(low, swap_halves(real), imaginary).astype(BF))
-    moved = halves(
-        dot(half_ref[0], jnp.concatenate(firsts, axis=1))
-        + dot(half_ref[1], jnp.concatenate(seconds, axis=1))
+    moved = dot(half_ref[0], jnp.concatenate(firsts, axis=1))
+    moved = moved + dot(half_ref[1], jnp.concatenate(seconds, axis=1))
+    for k in range(STEP):
+        part = moved[:, 128 * k : 128 * k + 128].reshape(20, 8, 128).astype(BF)
+        x_ref[:, 40 * k + 32 : 40 * k + 40, :] = part
+
+
+def in_steps(step, place_in, place_out, in_hbm, whole_ref, half_ref, out_hbm, *refs, between=None):
+    in_ref, out_ref, in_sem, out_sem = refs
+
+    def load(g):
+        return pltpu.make_async_copy(place_in(in_hbm, g), in_ref.at[g], in_sem.at[g])
+
+    def store(g):
+        return pltpu.make_async_copy(out_ref.at[g], place_out(out_hbm, g), out_sem.at[g])
+
+    for g in range(16 // STEP):
+        load(g).start()
+
+    def one(g, carry):
+        load(g).wait()
+        step(in_ref.at[g], whole_ref, half_ref, out_ref.at[g])
+        store(g).start()
+        return carry
+
+    lax.fori_loop(0, 8 // STEP, one, 0)
+    if between is not None:
+        between()
+    lax.fori_loop(8 // STEP, 16 // STEP, one, 0)
+    for g in range(16 // STEP):
+        store(g).wait()
+
+
+def unpack_kernel(place_ref, in_hbm, whole_ref, half_ref, *refs):
+    r_refs, (out_hbm, weight_hbm), rest = refs[:8], refs[8:10], refs[10:]
+    *step_refs, order_ref, weight_ref, r_sem, weight_sem = rest
+    loads = [
+        pltpu.make_async_copy(
+            r_refs[k], order_ref.at[jnp.bitwise_xor(place_ref[1], k)], r_sem.at[k]
+        )
+        for k in range(8)
+    ]
+    out = pltpu.make_async_copy(weight_ref, weight_hbm, weight_sem)
+
+    def finish():
+        for copy in loads:
+            copy.wait()
+        for e in range(8):
+            weight_ref[:, e, :] = order_ref[e, 0].astype(F32)
+            weight_ref[:, 8 + e, :] = order_ref[e, 1].astype(F32)
+        for p in range(4):
+            both = order_ref[2 * p, 2].astype(F32) + order_ref[2 * p + 1, 2].astype(F32)
+            weight_ref[:, 16 + p, :] = both
+        out.start()
+
+    for copy in loads:
+        copy.start()
+    in_steps(
+        unpack_step, packed_at, native_at, in_hbm, whole_ref, half_ref, out_hbm, *step_refs,
+        between=finish,
     )
-    for k in range(2):
-        x_ref[:, 40 * k + 32 : 40 * k + 40, :] = moved[k].reshape(20, 8, 128).astype(BF)
-
-
-NATIVE = pl.BlockSpec((20, 80, 128), lambda o: (0, o, 0))
-PACKED = pl.BlockSpec((2, 8, 104, 128), lambda o: (o, 0, 0, 0))
-
-
-def constant(shape):
-    return pl.BlockSpec(shape, lambda o: (0,) * len(shape))
+    out.wait()
+
+
+def native_at(ref, g):
+    return ref.at[:, pl.ds(40 * STEP * g, 40 * STEP)]
+
+
+def packed_at(ref, g):
+    return ref.at[pl.ds(STEP * g, STEP)]
+
+
+NATIVE = pltpu.VMEM((16 // STEP, 20, 40 * STEP, 128), BF)
+PACKED = pltpu.VMEM((16 // STEP, STEP, 8, 104, 128), BF)
+SEMS = [pltpu.SemaphoreType.DMA((16 // STEP,))] * 2
 
 
 def pack(x):
     return pl.pallas_call(
-        pack_kernel,
-        grid=(8,),
+        functools.partial(in_steps, pack_step, native_at, packed_at),
         out_shape=jax.ShapeDtypeStruct((16, 8, 104, 128), BF),
-        in_specs=[NATIVE, constant((320, 320)), constant((2, 96, 160))],
-        out_specs=PACKED,
+        in_specs=[HBM, VMEM, VMEM],
+        out_specs=HBM,
+        scratch_shapes=[NATIVE, PACKED] + SEMS,
+        compiler_params=pltpu.CompilerParams(vmem_limit_bytes=63 * MIB),
         name="pack",
     )(x, jnp.asarray(WHOLE_ORDER, BF), jnp.asarray(HALF_ORDER, BF))
 
 
-def unpack(y):
+def unpack(place, y, received):
     return pl.pallas_call(
         unpack_kernel,
-        grid=(8,),
-        out_shape=jax.ShapeDtypeStruct((20, 640, 128), BF),
-        in_specs=[PACKED, constant((320, 320)), constant((2, 160, 96))],
-        out_specs=NATIVE,
+        out_shape=[
+            jax.ShapeDtypeStruct((20, 640, 128), BF),
+            jax.ShapeDtypeStruct((20, 20, L), F32),
+        ],
+        in_specs=[SMEM, HBM, VMEM, VMEM] + [HBM] * 8,
+        out_specs=[HBM, HBM],
+        scratch_shapes=[PACKED, NATIVE]
+        + SEMS
+        + [
+            pltpu.VMEM((8, 3, 20, L), BF),
+            pltpu.VMEM((20, 20, L), F32),
+            pltpu.SemaphoreType.DMA((8,)),
+            pltpu.SemaphoreType.DMA(()),
+        ],
+        compiler_params=pltpu.CompilerParams(vmem_limit_bytes=63 * MIB),
         name="unpack",
-    )(y, jnp.asarray(WHOLE_ORDER.T, BF), jnp.asarray(HALF_ORDER.transpose(0, 2, 1), BF))
+    )(
+        place, y, jnp.asarray(WHOLE_ORDER.T, BF), jnp.asarray(HALF_ORDER.transpose(0, 2, 1), BF),
+        *received,
+    )
 
 
 def target_kernel(place_ref, t_ref, band_ref, *refs):
@@ -343,29 +429,31 @@
         return pltpu.make_async_copy(rows_hbm.at[:, where], rows_ref.at[:, where], rows_sem.at[g])
 
     load_rows(0).start()
-    loads = [pltpu.make_async_copy(to_full_hbm, to_full_ref, in_sem.at[0])]
-    loads.append(pltpu.make_async_copy(to_half_hbm, to_half_ref, in_sem.at[1]))
+    loads = [
+        pltpu.make_async_copy(to_full_hbm.at[n], to_full_ref.at[n], in_sem.at[n]) for n in range(2)
+    ]
+    loads.append(pltpu.make_async_copy(to_half_hbm, to_half_ref, in_sem.at[2]))
     for k in range(8):
         there = order_ref.at[jnp.bitwise_xor(place_ref[1], k)]
         loads.append(pltpu.make_async_copy(target_refs[k], there, target_sem.at[k]))
-    for copy in loads[:2]:
+    for copy in loads[:3]:
         copy.start()
     for g in range(1, 4):
         load_rows(g).start()
-    for copy in loads[2:]:
+    for copy in loads[3:]:
         copy.start()
     mask_ref[...] = block_mask(256, "block")
-    for copy in loads[:2]:
-        copy.wait()
     base = place_ref[0] * 20
     orders = [base + m for m in own_orders(place_ref)]
     degree = iota((L, 128), 0)
     low = iota((L, 128), 1) < 64
     keeps = [degree >= orders[0], degree >= orders[1], (degree >= orders[2]) & low]
 
-    def transform(g, carry):
+    def transform(g, carry, operators=None):
         load_rows(g).wait()
         for slot in range(3):
+            if operators:
+                operators[slot].wait()
             values = two_rows_of(rows_ref, g, slot)
             for i in range(2):
                 if slot < 2:
@@ -385,8 +473,9 @@
         where = pl.ds(4 * g, 4)
         return pltpu.make_async_copy(stacked_ref.at[where], stacked_hbm.at[where], out_sem.at[g])
 
-    lax.fori_loop(0, 4, transform, 0)
-    for copy in loads[2:]:
+    transform(0, 0, loads[:3])
+    lax.fori_loop(1, 4, transform, 0)
+    for copy in loads[3:]:
         copy.wait()
     target_ref[...] = order_ref[...].astype(F32).reshape(L, WIDE).astype(BF)
     stores = [pltpu.make_async_copy(target_ref, target_hbm, out_sem.at[4])]
@@ -472,7 +561,7 @@
             pltpu.VMEM((16, 8, 104, 128), BF),
             pltpu.VMEM((256, 256), BF),
             pltpu.VMEM((8, 40, WIDE), BF),
-            pltpu.SemaphoreType.DMA((2,)),
+            pltpu.SemaphoreType.DMA((3,)),
             pltpu.SemaphoreType.DMA((4,)),
             pltpu.SemaphoreType.DMA((8,)),
             pltpu.SemaphoreType.DMA((7,)),
@@ -534,7 +623,8 @@
     weight = cotangent * (16.0 * MEMBERS * NLAT) * jnp.abs(share) / distance
     beside = jnp.where(lane < MEMBERS, -weight, 0.0)
     loads[0].wait()
-    mixing = sum(dot(part, to_mixing_ref[...]) for part in split3(weight))
+    mixing = dot(jnp.concatenate(split3(weight), axis=0), to_mixing_ref[...])
+    mixing = mixing[:16] + mixing[16:32] + mixing[32:]
     mixing = [mixing[:, 128 * i : 128 * i + 128] for i in range(MEMBERS)]
 
     size = MEMBERS * GROUP
@@ -542,9 +632,10 @@
     mix_high, mix_low = split2(jnp.concatenate(mixing, axis=0))
     mix_high = dot(mix_high, widen).astype(BF)
     mix_low = dot(mix_low, widen).astype(BF)
-    beside = jnp.concatenate([beside, jnp.zeros((128 - NBANDS, 128), F32)], axis=0)
-    beside_high, beside_low = split2(beside)
-    band_of_lane = iota((GROUP, 128), 1).astype(F32)
+    beside_both = jnp.concatenate(
+        [part.astype(F32) for part in split2(beside)] + [jnp.zeros((96, 128), F32)], axis=0
+    ).astype(BF)
+    band_of_lane = (iota((GROUP, 128), 1) & 15).astype(F32)
 
     def mix(g, carry):
         start = pl.multiple_of(g * GROUP, GROUP)
@@ -554,7 +645,7 @@
         high = dot(pick, mix_high).astype(BF) * degree
         low = dot(pick, mix_low).astype(BF) * degree
         one_hot = (jnp.broadcast_to(bands, (GROUP, 128)) == band_of_lane).astype(F32).astype(BF)
-        weights = dot(one_hot, beside_high) + dot(one_hot, beside_low)
+        weights = dot(one_hot, beside_both)
         weights = jnp.concatenate(
             [jnp.broadcast_to(weights[:, i : i + 1], (GROUP, 128)) for i in range(MEMBERS)], axis=0
         )
@@ -696,28 +787,6 @@
         ),
         name="weights",
     )(place, rows, grads, full, half)
-
-
-def finish_kernel(place_ref, *refs):
-    *r_refs, o_ref, order_ref = refs
-    for k in range(8):
-        order_ref[jnp.bitwise_xor(place_ref[1], k)] = r_refs[k][...]
-    for e in range(8):
-        o_ref[:, e, :] = order_ref[e, 0].astype(F32)
-        o_ref[:, 8 + e, :] = order_ref[e, 1].astype(F32)
-    for p in range(4):
-        o_ref[:, 16 + p, :] = order_ref[2 * p, 2].astype(F32) + order_ref[2 * p + 1, 2].astype(F32)
-
-
-def finish(place, received):
-    return pl.pallas_call(
-        finish_kernel,
-        out_shape=jax.ShapeDtypeStruct((20, 20, L), F32),
-        in_specs=[SMEM] + [VMEM] * 8,
-        out_specs=VMEM,
-        scratch_shapes=[pltpu.VMEM((8, 3, 20, L), BF)],
-        name="finish",
-    )(place, *received)
 
 
 def exchange(x, axes):
@@ -772,8 +841,7 @@
     weight = weights(place, rows, grads, full, half)
     beside = lax.ppermute(weight[1], "dp", [(0, 1), (1, 0)])
     weight = (weight[0].astype(F32) + beside.astype(F32)).astype(BF)
-    native_grad, place = lax.optimization_barrier((unpack(returned), place))
-    grad_analysis = finish(place, swap([weight[k] for k in range(8)]))
+    native_grad, grad_analysis = unpack(place, returned, swap([weight[k] for k in range(8)]))
     native_grad = native_grad.reshape(20, 320, 2, 128)
     grad_fourier = jnp.transpose(native_grad, (2, 0, 1, 3)).reshape(1, 2, 20, 40960)
     return (grad_fourier, grad_analysis, loss_bands)

time: 278 us -> 273 us (0.982)
  Pallas kernels: 69.2 us -> 60.8 us
  waiting for transfers between devices: 103 us -> 106 us
    pallas_call x3 -> x2, Pallas kernels: 17.5 us -> 9.83 us  [the longest x1 4.95 us: unpack(): pl.pallas_call(unpack_kernel, out_shape=[jax.ShapeDtypeStruct((20, 640, 1...]
    ppermute x14, waiting for transfers between devices: 47.9 us -> 51 us  [swap(): lax.ppermute(blocks[k], ENS, [(e, e ^ k) for e in range(8)])]
  transfers between devices with their start and end apart: 18 -> 18, of which waited for: 5 -> 6; matrix products, arithmetic and copies ran while one was open for 2% -> 2% of each run, Pallas kernels for 10% -> 8%
where the time goes in v5:
time: 273 us; the launch traced here: 269 us
  waiting for transfers between devices  106 us (39%)
  starting transfers between devices  62.3 us (23%)
  Pallas kernels  60.8 us (22%)
  blocking collectives  31.7 us (12%)
  local copies, waits for them, and re-layouts  5.21 us (2%)
    all_to_all x2, waiting for transfers between devices, exchange(): return lax.all_to_all(x, axes, split_axis=0, concat_axis=0, tiled=True)  52.8 us
    ppermute x14, waiting for transfers between devices, swap(): lax.ppermute(blocks[k], ENS, [(e, e ^ k) for e in range(8)])  51 us
    ppermute x14, starting transfers between devices, swap(): lax.ppermute(blocks[k], ENS, [(e, e ^ k) for e in range(8)])  38.6 us
    all_to_all x1, blocking collectives, exchange(): return lax.all_to_all(x, axes, split_axis=0, concat_axis=0, tiled=True)  31.7 us
    all_to_all x2, starting transfers between devices, exchange(): return lax.all_to_all(x, axes, split_axis=0, concat_axis=0, tiled=True)  23.6 us
    pallas_call x1, Pallas kernels, gradient(): pl.pallas_call(gradient_kernel, out_shape=[jax.ShapeDtypeStruct((16, 8, 1...  16.1 us
    pallas_call x1, Pallas kernels, spectra(): pl.pallas_call(spectra_kernel, out_shape=[jax.ShapeDtypeStruct((JJ, L, WI...  14.4 us
    pallas_call x1, Pallas kernels, weights(): pl.pallas_call(weight_kernel, out_shape=jax.ShapeDtypeStruct((2, 8, 3, 20...  11.6 us
  transfers between devices with their start and end apart: 18, of which 6 were waited for; matrix products, arithmetic and copies ran while one was open for 2% of the time, Pallas kernels for 8%

profile of v5, /device:TPU:8, one launch (start us, length us, event | category | flops | bytes accessed | tf_op | source)
XLA Modules:
  0.0 269.1 jit_solution(12512113252156427674)
XLA Ops:
  0.6 4.9 %pack.1 = bf16[16,8,104,128]{3,2,1,0:T(8,128)(2,1)} custom-call(bf16[20,640,128]{2,1,0:T(8,128)(2,1)} %bitcast.50, bf16[64,64]{1,0:T(8,128)(2,1)} %constant.45.clone.whole_ref, bf16[2,96,160]{2,1,0:T(8,128)(2,1)} %constant.46.clone.half_ref), custom_call_target="tpu_custom_call" | custom-call | tf_op jit(solution)/shard_map/pack/pallas_call | solution.py:214
  5.6 15.9 %all-to-all-start = ((bf16[128,52,2,128]{3,2,1,0:T(2,128)(2,1)}), bf16[128,52,2,128]{3,2,1,0:T(2,128)(2,1)}, u32[]{:S(2)}, u32[]{:S(2)}) async-start(bf16[128,52,2,128]{3,2,1,0:T(2,128)(2,1)} %bitcast.47), calls=%async_computation | async-start | bytes 6815744 | tf_op jit(solution)/shard_map/all_to_all | solution.py:793
  21.5 0.7 copy.20.band_ref
  22.2 0.6 pad_add_fusion.place_ref
  22.8 1.9 target_blocks.1
  24.6 1.6 collective-permute-start
  26.2 2.7 collective-permute-start.1
  28.9 0.6 collective-permute-start.2
  29.4 5.4 %collective-permute-start.3 = (bf16[40,384]{1,0:T(8,128)(2,1)}, bf16[40,384]{1,0:T(8,128)(2,1)S(1)}, u32[]{:S(2)}, u32[]{:S(2)}) collective-permute-start(bf16[40,384]{1,0:T(8,128)(2,1)} %get-tuple-element.43), channel_id=1, source_target_pairs={{0,4},{1,5},{2,6},{3,7},{4,0},{5,1},{6,2},{7,3},{8,12},{9,13},{10,... | collective-permute-start | bytes 92168 | tf_op jit(solution)/shard_map/ppermute | solution.py:798
  34.8 0.2 collective-permute-start.4
  35.1 0.1 reshape.43
  35.1 8.8 %collective-permute-start.5 = (bf16[40,384]{1,0:T(8,128)(2,1)}, bf16[40,384]{1,0:T(8,128)(2,1)S(1)}, u32[]{:S(2)}, u32[]{:S(2)}) collective-permute-start(bf16[40,384]{1,0:T(8,128)(2,1)} %get-tuple-element.45), channel_id=1, source_target_pairs={{0,6},{1,7},{2,4},{3,5},{4,2},{5,3},{6,0},{7,1},{8,14},{9,15},{10,... | collective-permute-start | bytes 92168 | tf_op jit(solution)/shard_map/ppermute | solution.py:798
  43.9 0.6 collective-permute-start.6
  44.5 0.1 pad_add_fusion.1
  44.5 0.7 broadcast_in_dim.19.other_column_ref.other_ref
  45.3 6.9 %prepare.1 = (bf16[2,2,320,640]{3,2,1,0:T(8,128)(2,1)}, bf16[2,2,320,384]{3,2,1,0:T(8,128)(2,1)}, bf16[2,2,640,320]{3,2,1,0:T(8,128)(2,1)}, bf16[2,2,384,320]{3,2,1,0:T(8,128)(2,1)}, bf16[128,2048]{1,0:T(8,128)(2,1)}) custom-call(s32[3]{0:T(128)} %pad_add_fusion.place_ref, bf16[20,320,320]{2,1,0:T(8,128)(2,1)} %bitcast.48, ...), custom_call_target="tpu_custom_call" | custom-call | tf_op jit(solution)/shard_map/prepare/pallas_call | solution.py:355
  52.2 52.8 %all-to-all-done = bf16[128,52,2,128]{3,2,1,0:T(2,128)(2,1)} async-done(((bf16[128,52,2,128]{3,2,1,0:T(2,128)(2,1)}), bf16[128,52,2,128]{3,2,1,0:T(2,128)(2,1)}, u32[]{:S(2)}, u32[]{:S(2)}) %all-to-all-start) | async-done | bytes 3407904 | tf_op jit(solution)/shard_map/all_to_all | solution.py:793
  105.0 0.7 broadcast_in_dim.17.cotangent_ref
  105.8 0.5 copy-done.13
  106.3 0.0 copy-done.15
  106.3 0.0 copy-done.16
  106.3 0.0 copy-done.17
  106.4 14.4 %spectra.1 = (bf16[17,320,384]{2,1,0:T(8,128)(2,1)}, bf16[320,384]{1,0:T(8,128)(2,1)}, f32[32,40,128]{2,1,0:T(8,128)}) custom-call(s32[3]{0:T(128)} %pad_add_fusion.place_ref, bf16[16,8,104,128]{3,2,1,0:T(8,128)(2,1)} %bitcast.9.rows_hbm.rows_ref, bf16[2,2,320,640]{3,2,1,0:T(8,128)(2,1)} %get-tuple-element.36.to_full_hbm, ...), custom_call_target="tpu_custom_call" | custom-call | flops 10000000000 | bytes 12000000 | tf_op jit(solution)/shard_map/spectra/pallas_call | solution.py:546
  120.8 31.7 %all_to_all.15 = f32[128,5,2,128]{3,2,1,0:T(2,128)} all-to-all(f32[128,5,2,128]{3,2,1,0:T(2,128)} %bitcast.51), channel_id=1, replica_groups=mesh['dp'=2,'order_0'=4,'order_1'=4,'ens_0'=2,'ens_1'=4] {'order_0','ord..., dimensions={0} | all-to-all | bytes 1310720 | tf_op jit(solution)/shard_map/all_to_all | solution.py:793
  152.5 16.1 %gradient.1 = (bf16[16,8,104,128]{3,2,1,0:T(8,128)(2,1)}, bf16[16,320,384]{2,1,0:T(8,128)(2,1)}, f32[16,128]{1,0:T(8,128)}) custom-call(bf16[17,320,384]{2,1,0:T(8,128)(2,1)} %get-tuple-element.47.stacked_hbm, bf16[320,384]{1,0:T(8,128)(2,1)} %get-tuple-element.48.target_hbm, f32[32,40,128]{2,1,0:T(8,128)} %bitcast.52, ...), custom_call_target="tpu_custom_call" | custom-call | flops 10000000000 | bytes 12000000 | tf_op jit(solution)/shard_map/gradient/pallas_call | solution.py:700
  168.7 7.7 %all-to-all-start.2 = ((bf16[128,52,2,128]{3,2,1,0:T(2,128)(2,1)}), bf16[128,52,2,128]{3,2,1,0:T(2,128)(2,1)}, u32[]{:S(2)}, u32[]{:S(2)}) async-start(bf16[128,52,2,128]{3,2,1,0:T(2,128)(2,1)} %bitcast.49), calls=%async_computation.2 | async-start | bytes 6815744 | tf_op jit(solution)/shard_map/all_to_all | solution.py:793
  176.4 11.6 %weights.1 = bf16[2,8,3,20,320]{4,3,2,1,0:T(8,128)(2,1)} custom-call(s32[3]{0:T(128)} %pad_add_fusion.place_ref, bf16[16,8,104,128]{3,2,1,0:T(8,128)(2,1)} %bitcast.9.rows_hbm.rows_ref, bf16[16,320,384]{2,1,0:T(8,128)(2,1)} %get-tuple-element.55.grad_ref, bf16[320,640]{1,0:T(8,128)(2,1)} %constant.43.clone.full_ref, bf16[2,320,384]{2,1,0:T(8,128)(2,1)} %constant.44.clone.half_ref), custom_call_target="tpu_custom_call" | custom-call | flops 5000000000 | bytes 8000000 | tf_op jit(solution)/shard_map/weights/pallas_call | solution.py:775
  188.0 1.1 slice_bitcast_fusion
  189.1 0.1 collective-permute-start.7
  189.2 1.8 collective-permute-done.7
  190.9 1.1 fusion
  192.1 0.7 slice_bitcast_fusion.2
  192.8 7.5 %collective-permute-start.14 = (bf16[3,20,320]{2,1,0:T(8,128)(2,1)S(1)}, bf16[3,20,320]{2,1,0:T(8,128)(2,1)S(1)}, u32[]{:S(2)}, u32[]{:S(2)}) collective-permute-start(bf16[3,20,320]{2,1,0:T(8,128)(2,1)S(1)} %get-tuple-element.59), channel_id=1, source_target_pairs={{0,7},{1,6},{2,5},{3,4},{4,3},{5,2},{6,1},{7,0},{8,15},{9,14},{10,... | collective-permute-start | bytes 115208 | tf_op jit(solution)/shard_map/ppermute | solution.py:798
  200.2 0.9 collective-permute-start.13
  201.1 0.1 slice_reduce_fusion
  201.2 0.1 collective-permute-start.15
  201.3 5.5 %collective-permute-start.12 = (bf16[3,20,320]{2,1,0:T(8,128)(2,1)S(1)}, bf16[3,20,320]{2,1,0:T(8,128)(2,1)S(1)}, u32[]{:S(2)}, u32[]{:S(2)}) collective-permute-start(bf16[3,20,320]{2,1,0:T(8,128)(2,1)S(1)} %get-tuple-element.61), channel_id=1, source_target_pairs={{0,5},{1,4},{2,7},{3,6},{4,1},{5,0},{6,3},{7,2},{8,13},{9,12},{10,... | collective-permute-start | bytes 115208 | tf_op jit(solution)/shard_map/ppermute | solution.py:798
  206.8 0.6 collective-permute-start.11
  207.3 2.7 collective-permute-start.10
  210.0 46.6 %collective-permute-done.14.refs_7_ = bf16[3,20,320]{2,1,0:T(8,128)(2,1)S(1)} collective-permute-done((bf16[3,20,320]{2,1,0:T(8,128)(2,1)S(1)}, bf16[3,20,320]{2,1,0:T(8,128)(2,1)S(1)}, u32[]{:S(2)}, u32[]{:S(2)}) %collective-permute-start.14) | collective-permute-done | bytes 38432 | tf_op jit(solution)/shard_map/ppermute | solution.py:798
  256.7 1.5 collective-permute-start.9
  258.1 1.1 collective-permute-done.13.refs_6_
  259.2 0.3 collective-permute-start.8
  259.6 0.5 add.19
  260.1 2.2 collective-permute-done.9.refs_2_
  262.3 1.1 collective-permute-done.8.refs_1_
  263.4 0.5 copy-done.7
  264.0 5.0 %unpack.1 = (bf16[20,640,128]{2,1,0:T(8,128)(2,1)}, f32[20,20,320]{2,1,0:T(8,128)}) custom-call(s32[3]{0:T(128)} %pad_add_fusion.place_ref, bf16[16,8,104,128]{3,2,1,0:T(8,128)(2,1)} %bitcast.15.in_hbm, bf16[64,64]{1,0:T(8,128)(2,1)} %constant.48.clone.whole_ref, bf16[2,160,96]{2,1,0:T(8,128)(2,1)} %constant.49.clone.half_ref, ...), custom_call_target="tpu_custom_call" | custom-call | tf_op jit(solution)/shard_map/unpack/pallas_call | solution.py:226
  (46 shorter events, 0.1 us)
Async XLA Ops:
  0.6 34.4 %copy-start = (f32[2,16]{1,0:T(2,128)S(1)}, f32[2,16]{1,0:T(2,128)}, u32[]{:S(2)}) copy-start(f32[2,16]{1,0:T(2,128)} %param.18) | copy-start | bytes 388
  5.5 15.9 %copy-start.8 = (s32[40,20]{0,1:T(8,128)S(1)}, s32[40,20]{0,1:T(8,128)}, u32[]{:S(2)}) copy-start(s32[40,20]{0,1:T(8,128)} %param.16) | copy-start | bytes 9604
  5.5 29.5 %copy-start.10 = (s32[16,4]{0,1:T(4,128)S(1)}, s32[16,4]{0,1:T(4,128)}, u32[]{:S(2)}) copy-start(s32[16,4]{0,1:T(4,128)} %param.17) | copy-start | bytes 772
  5.6 99.4 %all-to-all-start = ((bf16[128,52,2,128]{3,2,1,0:T(2,128)(2,1)}), bf16[128,52,2,128]{3,2,1,0:T(2,128)(2,1)}, u32[]{:S(2)}, u32[]{:S(2)}) async-start(bf16[128,52,2,128]{3,2,1,0:T(2,128)(2,1)} %bitcast.47), calls=%async_computation | async-start | bytes 6815744 | tf_op jit(solution)/shard_map/all_to_all | solution.py:793
  24.6 10.5 %collective-permute-start = (bf16[40,384]{1,0:T(8,128)(2,1)}, bf16[40,384]{1,0:T(8,128)(2,1)S(1)}, u32[]{:S(2)}, u32[]{:S(2)}) collective-permute-start(bf16[40,384]{1,0:T(8,128)(2,1)} %get-tuple-element.40), channel_id=1, source_target_pairs={{0,1},{1,0},{2,3},{3,2},{4,5},{5,4},{6,7},{7,6},{8,9},{9,8},{10,11... | collective-permute-start | bytes 92168 | tf_op jit(solution)/shard_map/ppermute | solution.py:798
  26.2 17.7 %collective-permute-start.1 = (bf16[40,384]{1,0:T(8,128)(2,1)}, bf16[40,384]{1,0:T(8,128)(2,1)S(1)}, u32[]{:S(2)}, u32[]{:S(2)}) collective-permute-start(bf16[40,384]{1,0:T(8,128)(2,1)} %get-tuple-element.41), channel_id=1, source_target_pairs={{0,2},{1,3},{2,0},{3,1},{4,6},{5,7},{6,4},{7,5},{8,10},{9,11},{10,... | collective-permute-start | bytes 92168 | tf_op jit(solution)/shard_map/ppermute | solution.py:798
  28.9 76.8 %collective-permute-start.2 = (bf16[40,384]{1,0:T(8,128)(2,1)}, bf16[40,384]{1,0:T(8,128)(2,1)S(1)}, u32[]{:S(2)}, u32[]{:S(2)}) collective-permute-start(bf16[40,384]{1,0:T(8,128)(2,1)} %get-tuple-element.42), channel_id=1, source_target_pairs={{0,3},{1,2},{2,1},{3,0},{4,7},{5,6},{6,5},{7,4},{8,11},{9,10},{10,... | collective-permute-start | bytes 92168 | tf_op jit(solution)/shard_map/ppermute | solution.py:798
  29.4 76.3 %collective-permute-start.3 = (bf16[40,384]{1,0:T(8,128)(2,1)}, bf16[40,384]{1,0:T(8,128)(2,1)S(1)}, u32[]{:S(2)}, u32[]{:S(2)}) collective-permute-start(bf16[40,384]{1,0:T(8,128)(2,1)} %get-tuple-element.43), channel_id=1, source_target_pairs={{0,4},{1,5},{2,6},{3,7},{4,0},{5,1},{6,2},{7,3},{8,12},{9,13},{10,... | collective-permute-start | bytes 92168 | tf_op jit(solution)/shard_map/ppermute | solution.py:798
  34.8 70.9 %collective-permute-start.4 = (bf16[40,384]{1,0:T(8,128)(2,1)}, bf16[40,384]{1,0:T(8,128)(2,1)S(1)}, u32[]{:S(2)}, u32[]{:S(2)}) collective-permute-start(bf16[40,384]{1,0:T(8,128)(2,1)} %get-tuple-element.44), channel_id=1, source_target_pairs={{0,5},{1,4},{2,7},{3,6},{4,1},{5,0},{6,3},{7,2},{8,13},{9,12},{10,... | collective-permute-start | bytes 92168 | tf_op jit(solution)/shard_map/ppermute | solution.py:798
  35.1 70.6 %copy-start.11 = (bf16[40,384]{1,0:T(8,128)(2,1)}, bf16[40,384]{1,0:T(8,128)(2,1)S(1)}, u32[]{:S(2)}) copy-start(bf16[40,384]{1,0:T(8,128)(2,1)S(1)} %collective-permute-done.refs_1_) | copy-start | bytes 92164
  35.1 70.6 %collective-permute-start.5 = (bf16[40,384]{1,0:T(8,128)(2,1)}, bf16[40,384]{1,0:T(8,128)(2,1)S(1)}, u32[]{:S(2)}, u32[]{:S(2)}) collective-permute-start(bf16[40,384]{1,0:T(8,128)(2,1)} %get-tuple-element.45), channel_id=1, source_target_pairs={{0,6},{1,7},{2,4},{3,5},{4,2},{5,3},{6,0},{7,1},{8,14},{9,15},{10,... | collective-permute-start | bytes 92168 | tf_op jit(solution)/shard_map/ppermute | solution.py:798
  43.9 61.9 %copy-start.12 = (bf16[40,384]{1,0:T(8,128)(2,1)}, bf16[40,384]{1,0:T(8,128)(2,1)S(1)}, u32[]{:S(2)}) copy-start(bf16[40,384]{1,0:T(8,128)(2,1)S(1)} %collective-permute-done.1.refs_2_) | copy-start | bytes 92164
  43.9 61.8 %collective-permute-start.6 = (bf16[40,384]{1,0:T(8,128)(2,1)}, bf16[40,384]{1,0:T(8,128)(2,1)S(1)}, u32[]{:S(2)}, u32[]{:S(2)}) collective-permute-start(bf16[40,384]{1,0:T(8,128)(2,1)} %get-tuple-element.46), channel_id=1, source_target_pairs={{0,7},{1,6},{2,5},{3,4},{4,3},{5,2},{6,1},{7,0},{8,15},{9,14},{10,... | collective-permute-start | bytes 92168 | tf_op jit(solution)/shard_map/ppermute | solution.py:798
  105.7 0.6 copy-start.13
  105.7 0.6 copy-start.14
  105.7 0.6 copy-start.15
  105.7 0.6 copy-start.16
  105.7 0.6 copy-start.17
  168.7 94.7 %all-to-all-start.2 = ((bf16[128,52,2,128]{3,2,1,0:T(2,128)(2,1)}), bf16[128,52,2,128]{3,2,1,0:T(2,128)(2,1)}, u32[]{:S(2)}, u32[]{:S(2)}) async-start(bf16[128,52,2,128]{3,2,1,0:T(2,128)(2,1)} %bitcast.49), calls=%async_computation.2 | async-start | bytes 6815744 | tf_op jit(solution)/shard_map/all_to_all | solution.py:793
  176.4 24.7 %copy-start.9 = (f32[16,128]{1,0:T(8,128)S(1)}, f32[16,128]{1,0:T(8,128)}, u32[]{:S(2)}) copy-start(f32[16,128]{1,0:T(8,128)} %get-tuple-element.58) | copy-start | bytes 24580
  189.1 1.9 collective-permute-start.7
  192.8 63.9 %collective-permute-start.14 = (bf16[3,20,320]{2,1,0:T(8,128)(2,1)S(1)}, bf16[3,20,320]{2,1,0:T(8,128)(2,1)S(1)}, u32[]{:S(2)}, u32[]{:S(2)}) collective-permute-start(bf16[3,20,320]{2,1,0:T(8,128)(2,1)S(1)} %get-tuple-element.59), channel_id=1, source_target_pairs={{0,7},{1,6},{2,5},{3,4},{4,3},{5,2},{6,1},{7,0},{8,15},{9,14},{10,... | collective-permute-start | bytes 115208 | tf_op jit(solution)/shard_map/ppermute | solution.py:798
  200.2 59.0 %collective-permute-start.13 = (bf16[3,20,320]{2,1,0:T(8,128)(2,1)S(1)}, bf16[3,20,320]{2,1,0:T(8,128)(2,1)S(1)}, u32[]{:S(2)}, u32[]{:S(2)}) collective-permute-start(bf16[3,20,320]{2,1,0:T(8,128)(2,1)S(1)} %get-tuple-element.60), channel_id=1, source_target_pairs={{0,6},{1,7},{2,4},{3,5},{4,2},{5,3},{6,0},{7,1},{8,14},{9,15},{10,... | collective-permute-start | bytes 115208 | tf_op jit(solution)/shard_map/ppermute | solution.py:798
  201.2 6.1 %collective-permute-start.15 = (f32[16]{0:T(128)S(1)}, f32[16]{0:T(128)S(1)}, u32[]{:S(2)}, u32[]{:S(2)}) collective-permute-start(f32[16]{0:T(128)S(1)} %slice_reduce_fusion), channel_id=1, source_target_pairs={{0,128},{128,0},{1,129},{129,1},{2,130},{130,2},{3,131},{131,3},{4... | collective-permute-start | bytes 200 | tf_op jit(solution)/shard_map/ppermute | solution.py:840
  201.3 58.8 %collective-permute-start.12 = (bf16[3,20,320]{2,1,0:T(8,128)(2,1)S(1)}, bf16[3,20,320]{2,1,0:T(8,128)(2,1)S(1)}, u32[]{:S(2)}, u32[]{:S(2)}) collective-permute-start(bf16[3,20,320]{2,1,0:T(8,128)(2,1)S(1)} %get-tuple-element.61), channel_id=1, source_target_pairs={{0,5},{1,4},{2,7},{3,6},{4,1},{5,0},{6,3},{7,2},{8,13},{9,12},{10,... | collective-permute-start | bytes 115208 | tf_op jit(solution)/shard_map/ppermute | solution.py:798
  206.8 53.3 %collective-permute-start.11 = (bf16[3,20,320]{2,1,0:T(8,128)(2,1)S(1)}, bf16[3,20,320]{2,1,0:T(8,128)(2,1)S(1)}, u32[]{:S(2)}, u32[]{:S(2)}) collective-permute-start(bf16[3,20,320]{2,1,0:T(8,128)(2,1)S(1)} %get-tuple-element.62), channel_id=1, source_target_pairs={{0,4},{1,5},{2,6},{3,7},{4,0},{5,1},{6,2},{7,3},{8,12},{9,13},{10,... | collective-permute-start | bytes 115208 | tf_op jit(solution)/shard_map/ppermute | solution.py:798
  207.3 52.8 %collective-permute-start.10 = (bf16[3,20,320]{2,1,0:T(8,128)(2,1)S(1)}, bf16[3,20,320]{2,1,0:T(8,128)(2,1)S(1)}, u32[]{:S(2)}, u32[]{:S(2)}) collective-permute-start(bf16[3,20,320]{2,1,0:T(8,128)(2,1)S(1)} %get-tuple-element.63), channel_id=1, source_target_pairs={{0,3},{1,2},{2,1},{3,0},{4,7},{5,6},{6,5},{7,4},{8,11},{9,10},{10,... | collective-permute-start | bytes 115208 | tf_op jit(solution)/shard_map/ppermute | solution.py:798
  256.7 6.7 %copy-start.1 = (bf16[3,20,320]{2,1,0:T(8,128)(2,1)}, bf16[3,20,320]{2,1,0:T(8,128)(2,1)S(1)}, u32[]{:S(2)}) copy-start(bf16[3,20,320]{2,1,0:T(8,128)(2,1)S(1)} %collective-permute-done.14.refs_7_) | copy-start | bytes 115204
  256.7 5.7 %collective-permute-start.9 = (bf16[3,20,320]{2,1,0:T(8,128)(2,1)S(1)}, bf16[3,20,320]{2,1,0:T(8,128)(2,1)S(1)}, u32[]{:S(2)}, u32[]{:S(2)}) collective-permute-start(bf16[3,20,320]{2,1,0:T(8,128)(2,1)S(1)} %get-tuple-element.64), channel_id=1, source_target_pairs={{0,2},{1,3},{2,0},{3,1},{4,6},{5,7},{6,4},{7,5},{8,10},{9,11},{10,... | collective-permute-start | bytes 115208 | tf_op jit(solution)/shard_map/ppermute | solution.py:798
  259.2 4.2 %copy-start.2 = (bf16[3,20,320]{2,1,0:T(8,128)(2,1)}, bf16[3,20,320]{2,1,0:T(8,128)(2,1)S(1)}, u32[]{:S(2)}) copy-start(bf16[3,20,320]{2,1,0:T(8,128)(2,1)S(1)} %collective-permute-done.13.refs_6_) | copy-start | bytes 115204
  259.2 4.2 %collective-permute-start.8 = (bf16[3,20,320]{2,1,0:T(8,128)(2,1)S(1)}, bf16[3,20,320]{2,1,0:T(8,128)(2,1)S(1)}, u32[]{:S(2)}, u32[]{:S(2)}) collective-permute-start(bf16[3,20,320]{2,1,0:T(8,128)(2,1)S(1)} %get-tuple-element.65), channel_id=1, source_target_pairs={{0,1},{1,0},{2,3},{3,2},{4,5},{5,4},{6,7},{7,6},{8,9},{9,8},{10,11... | collective-permute-start | bytes 115208 | tf_op jit(solution)/shard_map/ppermute | solution.py:798
  260.1 3.3 %copy-start.3 = (bf16[3,20,320]{2,1,0:T(8,128)(2,1)}, bf16[3,20,320]{2,1,0:T(8,128)(2,1)S(1)}, u32[]{:S(2)}) copy-start(bf16[3,20,320]{2,1,0:T(8,128)(2,1)S(1)} %collective-permute-done.12.refs_5_) | copy-start | bytes 115204
  260.1 3.3 %copy-start.4 = (bf16[3,20,320]{2,1,0:T(8,128)(2,1)}, bf16[3,20,320]{2,1,0:T(8,128)(2,1)S(1)}, u32[]{:S(2)}) copy-start(bf16[3,20,320]{2,1,0:T(8,128)(2,1)S(1)} %collective-permute-done.11.refs_4_) | copy-start | bytes 115204
  260.1 3.3 %copy-start.5 = (bf16[3,20,320]{2,1,0:T(8,128)(2,1)}, bf16[3,20,320]{2,1,0:T(8,128)(2,1)S(1)}, u32[]{:S(2)}) copy-start(bf16[3,20,320]{2,1,0:T(8,128)(2,1)S(1)} %collective-permute-done.10.refs_3_) | copy-start | bytes 115204
  262.3 1.1 copy-start.6
  263.4 0.6 copy-start.7

commit v6 on v5

--- a/solution.py
+++ b/solution.py
@@ -341,6 +341,7 @@
         own = own_ref[min(n, 2)]
         to_ref = to_full_ref.at[n] if n < 2 else to_half_ref.at[n - 2]
         from_ref = from_full_ref.at[n] if n < 2 else from_half_ref.at[n - 2]
+        from_ref[...] = jnp.zeros_like(from_ref)
         spread = dot(own, choose, 0, 0)
         member = iota(spread.shape, 1) % 2
         for i in range(2):
@@ -348,7 +349,7 @@
         spread = dot(choose, own, 0, 0)
         member = iota(spread.shape, 0) % 2
         for i in range(2):
-            from_ref[i] = jnp.where(member == i, spread, 0.0).astype(BF)
+            from_ref[:, WIDE * i : WIDE * i + L] = jnp.where(member == i, spread, 0.0).astype(BF)
 
 
 def prepare(place, analysis, full, half, other):
@@ -357,8 +358,8 @@
         out_shape=[
             jax.ShapeDtypeStruct((2, 2, L, 640), BF),
             jax.ShapeDtypeStruct((2, 2, L, WIDE), BF),
-            jax.ShapeDtypeStruct((2, 2, 640, L), BF),
-            jax.ShapeDtypeStruct((2, 2, WIDE, L), BF),
+            jax.ShapeDtypeStruct((2, 640, WIDE + L), BF),
+            jax.ShapeDtypeStruct((2, WIDE, WIDE + L), BF),
             jax.ShapeDtypeStruct((128, MEMBERS * 128), BF),
         ],
         in_specs=[SMEM, HBM, VMEM, VMEM, VMEM],
@@ -668,11 +669,10 @@
     def inverse(g, carry):
         for slot in range(3):
             grads = [jnp.concatenate(grads_of(grad_ref, g, i, slot), axis=1) for i in range(2)]
-            from_ref = from_full_ref.at[slot] if slot < 2 else from_half_ref.at[0]
-            parts = halves(dot(from_ref[0], grads[0]) + dot(from_ref[1], grads[1]))
+            grads = jnp.concatenate([grads[0], jnp.zeros((WIDE - L, 256), BF), grads[1]], axis=0)
+            parts = halves(dot(from_full_ref[slot] if slot < 2 else from_half_ref[0], grads))
             if slot == 2:
-                from_ref = from_half_ref.at[1]
-                other = halves(dot(from_ref[0], grads[0]) + dot(from_ref[1], grads[1]))
+                other = halves(dot(from_half_ref[1], grads))
                 parts = [parts[k] + swap_halves(other[k]) for k in range(2)]
             start, count = STARTS[slot], COUNTS[slot]
             for k in range(2):
@@ -710,8 +710,8 @@
             pltpu.VMEM((JJ, L, WIDE), BF),
             pltpu.VMEM((L, WIDE), BF),
             pltpu.VMEM((128, MEMBERS * 128), BF),
-            pltpu.VMEM((2, 2, 640, L), BF),
-            pltpu.VMEM((2, 2, WIDE, L), BF),
+            pltpu.VMEM((2, 640, WIDE + L), BF),
+            pltpu.VMEM((2, WIDE, WIDE + L), BF),
             pltpu.VMEM((MEMBERS, L, WIDE), BF),
             pltpu.VMEM((16, 8, 104, 128), BF),
             pltpu.VMEM((256, 256), BF),
@@ -793,10 +793,8 @@
     return lax.all_to_all(x, axes, split_axis=0, concat_axis=0, tiled=True)
 
 
-def swap(blocks):
-    return [blocks[0]] + [
-        lax.ppermute(blocks[k], ENS, [(e, e ^ k) for e in range(8)]) for k in range(1, 8)
-    ]
+def swap(blocks, kinds):
+    return [lax.ppermute(blocks[k], ENS, [(e, e ^ k) for e in range(8)]) for k in kinds]
 
 
 def travel(x):
@@ -816,17 +814,18 @@
         (target[0], partners, full, band_cotangent, packed)
     )
     rows = travel(packed)
-    targets = swap(target_blocks(place, target_in, band_ids))
+    blocks = target_blocks(place, target_in, band_ids)
+    targets = [blocks[0]] + swap(blocks, range(1, 8))
     other = jnp.concatenate(
         [jnp.full((16,), MEMBERS, jnp.int32), partners.T.reshape(64), jnp.zeros((48,), jnp.int32)]
     )
     other = jnp.broadcast_to(other[:, None], (128, 128))
+    cotangent = lax.dynamic_slice_in_dim(cotangent, lax.axis_index("dp"), 1, 0)[0]
+    cotangent = jnp.broadcast_to(cotangent[:, None], (NBANDS, 128))
+    cotangent, other = lax.optimization_barrier((cotangent, other))
     to_full, to_half, from_full, from_half, to_mixing = prepare(
         place, by_order, full, half, other
     )
-    cotangent = lax.dynamic_slice_in_dim(cotangent, lax.axis_index("dp"), 1, 0)[0]
-    cotangent = jnp.broadcast_to(cotangent[:, None], (NBANDS, 128))
-    cotangent, rows = lax.optimization_barrier((cotangent, rows))
     share = np.zeros((8, 128), np.float32)
     share[:, :16] = 1.0 / MEMBERS
     share[:, 16:80] = -1.0 / (2.0 * MEMBERS * PARTNERS)
@@ -841,7 +840,10 @@
     weight = weights(place, rows, grads, full, half)
     beside = lax.ppermute(weight[1], "dp", [(0, 1), (1, 0)])
     weight = (weight[0].astype(F32) + beside.astype(F32)).astype(BF)
-    native_grad, grad_analysis = unpack(place, returned, swap([weight[k] for k in range(8)]))
+    near = swap([weight[k] for k in range(8)], (1, 2))
+    *far, near[0], near[1] = lax.optimization_barrier((*[weight[k] for k in range(3, 8)], *near))
+    far = swap([weight[0]] * 3 + far, range(3, 8))
+    native_grad, grad_analysis = unpack(place, returned, [weight[0]] + near + far)
     native_grad = native_grad.reshape(20, 320, 2, 128)
     grad_fourier = jnp.transpose(native_grad, (2, 0, 1, 3)).reshape(1, 2, 20, 40960)
     return (grad_fourier, grad_analysis, loss_bands)

time: 273 us -> 267 us (0.978)
  waiting for transfers between devices: 106 us -> 100 us
    all_to_all x2, waiting for transfers between devices: 52.8 us -> 1.53 us  [exchange(): return lax.all_to_all(x, axes, split_axis=0, concat_axis=0, tiled=True)]
    ppermute x14, waiting for transfers between devices: 51 us -> 96.9 us  [swap(): lax.ppermute(blocks[k], ENS, [(e, e ^ k) for e in range(8)])]
  transfers between devices with their start and end apart: 18 -> 18, of which waited for: 6 -> 12; matrix products, arithmetic and copies ran while one was open for 2% -> 2% of each run, Pallas kernels for 8% -> 8%
where the time goes in v6:
time: 267 us; the launch traced here: 264 us
  waiting for transfers between devices  100 us (37%)
  starting transfers between devices  64.2 us (24%)
  Pallas kernels  59.8 us (22%)
  blocking collectives  31.7 us (12%)
  local copies, waits for them, and re-layouts  4.49 us (2%)
    ppermute x14, waiting for transfers between devices, swap(): lax.ppermute(blocks[k], ENS, [(e, e ^ k) for e in range(8)])  96.9 us
    ppermute x14, starting transfers between devices, swap(): lax.ppermute(blocks[k], ENS, [(e, e ^ k) for e in range(8)])  40.4 us
    all_to_all x1, blocking collectives, exchange(): return lax.all_to_all(x, axes, split_axis=0, concat_axis=0, tiled=True)  31.7 us
    all_to_all x2, starting transfers between devices, exchange(): return lax.all_to_all(x, axes, split_axis=0, concat_axis=0, tiled=True)  23.6 us
    pallas_call x1, Pallas kernels, gradient(): pl.pallas_call(gradient_kernel, out_shape=[jax.ShapeDtypeStruct((16, 8, 1...  15.1 us
    pallas_call x1, Pallas kernels, spectra(): pl.pallas_call(spectra_kernel, out_shape=[jax.ShapeDtypeStruct((JJ, L, WI...  14.5 us
    pallas_call x1, Pallas kernels, weights(): pl.pallas_call(weight_kernel, out_shape=jax.ShapeDtypeStruct((2, 8, 3, 20...  11.6 us
    pallas_call x1, Pallas kernels, prepare(): pl.pallas_call(prepare_kernel, out_shape=[jax.ShapeDtypeStruct((2, 2, L,...  6.93 us
  transfers between devices with their start and end apart: 18, of which 12 were waited for; matrix products, arithmetic and copies ran while one was open for 2% of the time, Pallas kernels for 8%

profile of v6, /device:TPU:8, one launch (start us, length us, event | category | flops | bytes accessed | tf_op | source)
XLA Modules:
  0.0 263.8 jit_solution(12965947227847161099)
XLA Ops:
  0.6 4.9 %pack.1 = bf16[16,8,104,128]{3,2,1,0:T(8,128)(2,1)} custom-call(bf16[20,640,128]{2,1,0:T(8,128)(2,1)} %bitcast.50, bf16[64,64]{1,0:T(8,128)(2,1)} %constant.45.clone.whole_ref, bf16[2,96,160]{2,1,0:T(8,128)(2,1)} %constant.46.clone.half_ref), custom_call_target="tpu_custom_call" | custom-call | tf_op jit(solution)/shard_map/pack/pallas_call | solution.py:214
  5.6 15.9 %all-to-all-start = ((bf16[128,52,2,128]{3,2,1,0:T(2,128)(2,1)}), bf16[128,52,2,128]{3,2,1,0:T(2,128)(2,1)}, u32[]{:S(2)}, u32[]{:S(2)}) async-start(bf16[128,52,2,128]{3,2,1,0:T(2,128)(2,1)} %bitcast.47), calls=%async_computation | async-start | bytes 6815744 | tf_op jit(solution)/shard_map/all_to_all | solution.py:793
  21.5 0.7 copy.20.band_ref
  22.2 0.6 pad_add_fusion.place_ref
  22.8 1.9 target_blocks.1
  24.6 1.6 collective-permute-start
  26.2 2.7 %collective-permute-start.1 = (bf16[40,384]{1,0:T(8,128)(2,1)}, bf16[40,384]{1,0:T(8,128)(2,1)S(1)}, u32[]{:S(2)}, u32[]{:S(2)}) collective-permute-start(bf16[40,384]{1,0:T(8,128)(2,1)} %get-tuple-element.48), channel_id=1, source_target_pairs={{0,2},{1,3},{2,0},{3,1},{4,6},{5,7},{6,4},{7,5},{8,10},{9,11},{10,... | collective-permute-start | bytes 92168 | tf_op jit(solution)/shard_map/ppermute | solution.py:797
  28.9 0.6 collective-permute-start.2
  29.4 5.4 %collective-permute-start.3 = (bf16[40,384]{1,0:T(8,128)(2,1)}, bf16[40,384]{1,0:T(8,128)(2,1)S(1)}, u32[]{:S(2)}, u32[]{:S(2)}) collective-permute-start(bf16[40,384]{1,0:T(8,128)(2,1)} %get-tuple-element.50), channel_id=1, source_target_pairs={{0,4},{1,5},{2,6},{3,7},{4,0},{5,1},{6,2},{7,3},{8,12},{9,13},{10,... | collective-permute-start | bytes 92168 | tf_op jit(solution)/shard_map/ppermute | solution.py:797
  34.8 0.2 collective-permute-start.4
  35.1 0.1 reshape.43
  35.1 8.8 %collective-permute-start.5 = (bf16[40,384]{1,0:T(8,128)(2,1)}, bf16[40,384]{1,0:T(8,128)(2,1)S(1)}, u32[]{:S(2)}, u32[]{:S(2)}) collective-permute-start(bf16[40,384]{1,0:T(8,128)(2,1)} %get-tuple-element.52), channel_id=1, source_target_pairs={{0,6},{1,7},{2,4},{3,5},{4,2},{5,3},{6,0},{7,1},{8,14},{9,15},{10,... | collective-permute-start | bytes 92168 | tf_op jit(solution)/shard_map/ppermute | solution.py:797
  43.9 0.6 collective-permute-start.6
  44.5 0.7 broadcast_in_dim.17.cotangent_ref
  45.2 0.7 broadcast_in_dim.19.other_column_ref.other_ref
  45.9 6.9 %prepare.1 = (bf16[2,2,320,640]{3,2,1,0:T(8,128)(2,1)}, bf16[2,2,320,384]{3,2,1,0:T(8,128)(2,1)}, bf16[2,640,704]{2,1,0:T(8,128)(2,1)}, bf16[2,384,704]{2,1,0:T(8,128)(2,1)}, bf16[128,2048]{1,0:T(8,128)(2,1)}) custom-call(s32[3]{0:T(128)} %pad_add_fusion.place_ref, bf16[20,320,320]{2,1,0:T(8,128)(2,1)} %bitcast.48, ...), custom_call_target="tpu_custom_call" | custom-call | tf_op jit(solution)/shard_map/prepare/pallas_call | solution.py:356
  52.9 46.8 %collective-permute-done.3.refs_4_ = bf16[40,384]{1,0:T(8,128)(2,1)S(1)} collective-permute-done((bf16[40,384]{1,0:T(8,128)(2,1)}, bf16[40,384]{1,0:T(8,128)(2,1)S(1)}, u32[]{:S(2)}, u32[]{:S(2)}) %collective-permute-start.3) | collective-permute-done | bytes 30752 | tf_op jit(solution)/shard_map/ppermute | solution.py:797
  99.7 0.9 collective-permute-done.4.refs_5_
  100.5 3.1 %collective-permute-done.5.refs_6_ = bf16[40,384]{1,0:T(8,128)(2,1)S(1)} collective-permute-done((bf16[40,384]{1,0:T(8,128)(2,1)}, bf16[40,384]{1,0:T(8,128)(2,1)S(1)}, u32[]{:S(2)}, u32[]{:S(2)}) %collective-permute-start.5) | collective-permute-done | bytes 30752 | tf_op jit(solution)/shard_map/ppermute | solution.py:797
  103.6 1.4 all-to-all-done
  105.0 14.5 %spectra.1 = (bf16[17,320,384]{2,1,0:T(8,128)(2,1)}, bf16[320,384]{1,0:T(8,128)(2,1)}, f32[32,40,128]{2,1,0:T(8,128)}) custom-call(s32[3]{0:T(128)} %pad_add_fusion.place_ref, bf16[16,8,104,128]{3,2,1,0:T(8,128)(2,1)} %bitcast.8.rows_hbm.rows_ref, bf16[2,2,320,640]{3,2,1,0:T(8,128)(2,1)} %get-tuple-element.43.to_full_hbm, ...), custom_call_target="tpu_custom_call" | custom-call | flops 10000000000 | bytes 12000000 | tf_op jit(solution)/shard_map/spectra/pallas_call | solution.py:547
  119.5 31.7 %all_to_all.15 = f32[128,5,2,128]{3,2,1,0:T(2,128)} all-to-all(f32[128,5,2,128]{3,2,1,0:T(2,128)} %bitcast.51), channel_id=1, replica_groups=mesh['dp'=2,'order_0'=4,'order_1'=4,'ens_0'=2,'ens_1'=4] {'order_0','ord..., dimensions={0} | all-to-all | bytes 1310720 | tf_op jit(solution)/shard_map/all_to_all | solution.py:793
  151.2 15.1 %gradient.1 = (bf16[16,8,104,128]{3,2,1,0:T(8,128)(2,1)}, bf16[16,320,384]{2,1,0:T(8,128)(2,1)}, f32[16,128]{1,0:T(8,128)}) custom-call(bf16[17,320,384]{2,1,0:T(8,128)(2,1)} %get-tuple-element.54.stacked_hbm, bf16[320,384]{1,0:T(8,128)(2,1)} %get-tuple-element.55.target_hbm, f32[32,40,128]{2,1,0:T(8,128)} %bitcast.52, ...), custom_call_target="tpu_custom_call" | custom-call | flops 10000000000 | bytes 12000000 | tf_op jit(solution)/shard_map/gradient/pallas_call | solution.py:700
  166.3 7.7 %all-to-all-start.2 = ((bf16[128,52,2,128]{3,2,1,0:T(2,128)(2,1)}), bf16[128,52,2,128]{3,2,1,0:T(2,128)(2,1)}, u32[]{:S(2)}, u32[]{:S(2)}) async-start(bf16[128,52,2,128]{3,2,1,0:T(2,128)(2,1)} %bitcast.49), calls=%async_computation.2 | async-start | bytes 6815744 | tf_op jit(solution)/shard_map/all_to_all | solution.py:793
  174.0 11.6 %weights.1 = bf16[2,8,3,20,320]{4,3,2,1,0:T(8,128)(2,1)} custom-call(s32[3]{0:T(128)} %pad_add_fusion.place_ref, bf16[16,8,104,128]{3,2,1,0:T(8,128)(2,1)} %bitcast.8.rows_hbm.rows_ref, bf16[16,320,384]{2,1,0:T(8,128)(2,1)} %get-tuple-element.62.grad_ref, bf16[320,640]{1,0:T(8,128)(2,1)} %constant.43.clone.full_ref, bf16[2,320,384]{2,1,0:T(8,128)(2,1)} %constant.44.clone.half_ref), custom_call_target="tpu_custom_call" | custom-call | flops 5000000000 | bytes 8000000 | tf_op jit(solution)/shard_map/weights/pallas_call | solution.py:775
  185.6 1.1 slice_bitcast_fusion
  186.7 0.1 collective-permute-start.7
  186.8 1.8 collective-permute-done.7
  188.6 1.1 fusion
  189.7 0.7 slice_bitcast_fusion.2
  190.4 3.0 %collective-permute-start.9 = (bf16[3,20,320]{2,1,0:T(8,128)(2,1)S(1)}, bf16[3,20,320]{2,1,0:T(8,128)(2,1)S(1)}, u32[]{:S(2)}, u32[]{:S(2)}) collective-permute-start(bf16[3,20,320]{2,1,0:T(8,128)(2,1)S(1)} %get-tuple-element.73), channel_id=1, source_target_pairs={{0,2},{1,3},{2,0},{3,1},{4,6},{5,7},{6,4},{7,5},{8,10},{9,11},{10,... | collective-permute-start | bytes 115208 | tf_op jit(solution)/shard_map/ppermute | solution.py:797
  193.3 0.6 collective-permute-start.8
  193.9 0.1 slice_reduce_fusion
  194.0 0.1 collective-permute-start.15
  194.1 2.2 collective-permute-done.9.refs_2_
  196.4 3.4 %collective-permute-done.8.refs_1_ = bf16[3,20,320]{2,1,0:T(8,128)(2,1)S(1)} collective-permute-done((bf16[3,20,320]{2,1,0:T(8,128)(2,1)S(1)}, bf16[3,20,320]{2,1,0:T(8,128)(2,1)S(1)}, u32[]{:S(2)}, u32[]{:S(2)}) %collective-permute-start.8) | collective-permute-done | bytes 38432 | tf_op jit(solution)/shard_map/ppermute | solution.py:797
  199.7 1.8 collective-permute-start.10
  201.5 6.4 %collective-permute-start.11 = (bf16[3,20,320]{2,1,0:T(8,128)(2,1)S(1)}, bf16[3,20,320]{2,1,0:T(8,128)(2,1)S(1)}, u32[]{:S(2)}, u32[]{:S(2)}) collective-permute-start(bf16[3,20,320]{2,1,0:T(8,128)(2,1)S(1)} %get-tuple-element.66), channel_id=1, source_target_pairs={{0,4},{1,5},{2,6},{3,7},{4,0},{5,1},{6,2},{7,3},{8,12},{9,13},{10,... | collective-permute-start | bytes 115208 | tf_op jit(solution)/shard_map/ppermute | solution.py:797
  207.9 8.0 %collective-permute-start.13 = (bf16[3,20,320]{2,1,0:T(8,128)(2,1)S(1)}, bf16[3,20,320]{2,1,0:T(8,128)(2,1)S(1)}, u32[]{:S(2)}, u32[]{:S(2)}) collective-permute-start(bf16[3,20,320]{2,1,0:T(8,128)(2,1)S(1)} %get-tuple-element.68), channel_id=1, source_target_pairs={{0,6},{1,7},{2,4},{3,5},{4,2},{5,3},{6,0},{7,1},{8,14},{9,15},{10,... | collective-permute-start | bytes 115208 | tf_op jit(solution)/shard_map/ppermute | solution.py:797
  215.9 0.9 collective-permute-start.14
  216.9 0.5 add.19
  217.4 35.1 %collective-permute-done.11.refs_4_ = bf16[3,20,320]{2,1,0:T(8,128)(2,1)S(1)} collective-permute-done((bf16[3,20,320]{2,1,0:T(8,128)(2,1)S(1)}, bf16[3,20,320]{2,1,0:T(8,128)(2,1)S(1)}, u32[]{:S(2)}, u32[]{:S(2)}) %collective-permute-start.11) | collective-permute-done | bytes 38432 | tf_op jit(solution)/shard_map/ppermute | solution.py:797
  252.5 1.8 collective-permute-done.12.refs_5_
  254.3 3.4 %collective-permute-done.13.refs_6_ = bf16[3,20,320]{2,1,0:T(8,128)(2,1)S(1)} collective-permute-done((bf16[3,20,320]{2,1,0:T(8,128)(2,1)S(1)}, bf16[3,20,320]{2,1,0:T(8,128)(2,1)S(1)}, u32[]{:S(2)}, u32[]{:S(2)}) %collective-permute-start.13) | collective-permute-done | bytes 38432 | tf_op jit(solution)/shard_map/ppermute | solution.py:797
  257.7 0.3 collective-permute-done.14.refs_7_
  258.0 0.2 all-to-all-done.2
  258.3 0.3 copy-done.7
  258.6 5.0 %unpack.1 = (bf16[20,640,128]{2,1,0:T(8,128)(2,1)}, f32[20,20,320]{2,1,0:T(8,128)}) custom-call(s32[3]{0:T(128)} %pad_add_fusion.place_ref, bf16[16,8,104,128]{3,2,1,0:T(8,128)(2,1)} %bitcast.15.in_hbm, bf16[64,64]{1,0:T(8,128)(2,1)} %constant.48.clone.whole_ref, bf16[2,160,96]{2,1,0:T(8,128)(2,1)} %constant.49.clone.half_ref, ...), custom_call_target="tpu_custom_call" | custom-call | tf_op jit(solution)/shard_map/unpack/pallas_call | solution.py:226
  (46 shorter events, 0.3 us)
Async XLA Ops:
  0.6 34.4 %copy-start = (f32[2,16]{1,0:T(2,128)S(1)}, f32[2,16]{1,0:T(2,128)}, u32[]{:S(2)}) copy-start(f32[2,16]{1,0:T(2,128)} %param.18) | copy-start | bytes 388
  5.5 15.9 %copy-start.8 = (s32[40,20]{0,1:T(8,128)S(1)}, s32[40,20]{0,1:T(8,128)}, u32[]{:S(2)}) copy-start(s32[40,20]{0,1:T(8,128)} %param.16) | copy-start | bytes 9604
  5.5 29.5 %copy-start.10 = (s32[16,4]{0,1:T(4,128)S(1)}, s32[16,4]{0,1:T(4,128)}, u32[]{:S(2)}) copy-start(s32[16,4]{0,1:T(4,128)} %param.17) | copy-start | bytes 772
  5.6 99.4 %all-to-all-start = ((bf16[128,52,2,128]{3,2,1,0:T(2,128)(2,1)}), bf16[128,52,2,128]{3,2,1,0:T(2,128)(2,1)}, u32[]{:S(2)}, u32[]{:S(2)}) async-start(bf16[128,52,2,128]{3,2,1,0:T(2,128)(2,1)} %bitcast.47), calls=%async_computation | async-start | bytes 6815744 | tf_op jit(solution)/shard_map/all_to_all | solution.py:793
  24.6 10.5 %collective-permute-start = (bf16[40,384]{1,0:T(8,128)(2,1)}, bf16[40,384]{1,0:T(8,128)(2,1)S(1)}, u32[]{:S(2)}, u32[]{:S(2)}) collective-permute-start(bf16[40,384]{1,0:T(8,128)(2,1)} %get-tuple-element.47), channel_id=1, source_target_pairs={{0,1},{1,0},{2,3},{3,2},{4,5},{5,4},{6,7},{7,6},{8,9},{9,8},{10,11... | collective-permute-start | bytes 92168 | tf_op jit(solution)/shard_map/ppermute | solution.py:797
  26.2 17.7 %collective-permute-start.1 = (bf16[40,384]{1,0:T(8,128)(2,1)}, bf16[40,384]{1,0:T(8,128)(2,1)S(1)}, u32[]{:S(2)}, u32[]{:S(2)}) collective-permute-start(bf16[40,384]{1,0:T(8,128)(2,1)} %get-tuple-element.48), channel_id=1, source_target_pairs={{0,2},{1,3},{2,0},{3,1},{4,6},{5,7},{6,4},{7,5},{8,10},{9,11},{10,... | collective-permute-start | bytes 92168 | tf_op jit(solution)/shard_map/ppermute | solution.py:797
  28.9 24.0 %collective-permute-start.2 = (bf16[40,384]{1,0:T(8,128)(2,1)}, bf16[40,384]{1,0:T(8,128)(2,1)S(1)}, u32[]{:S(2)}, u32[]{:S(2)}) collective-permute-start(bf16[40,384]{1,0:T(8,128)(2,1)} %get-tuple-element.49), channel_id=1, source_target_pairs={{0,3},{1,2},{2,1},{3,0},{4,7},{5,6},{6,5},{7,4},{8,11},{9,10},{10,... | collective-permute-start | bytes 92168 | tf_op jit(solution)/shard_map/ppermute | solution.py:797
  29.4 70.2 %collective-permute-start.3 = (bf16[40,384]{1,0:T(8,128)(2,1)}, bf16[40,384]{1,0:T(8,128)(2,1)S(1)}, u32[]{:S(2)}, u32[]{:S(2)}) collective-permute-start(bf16[40,384]{1,0:T(8,128)(2,1)} %get-tuple-element.50), channel_id=1, source_target_pairs={{0,4},{1,5},{2,6},{3,7},{4,0},{5,1},{6,2},{7,3},{8,12},{9,13},{10,... | collective-permute-start | bytes 92168 | tf_op jit(solution)/shard_map/ppermute | solution.py:797
  34.8 65.7 %collective-permute-start.4 = (bf16[40,384]{1,0:T(8,128)(2,1)}, bf16[40,384]{1,0:T(8,128)(2,1)S(1)}, u32[]{:S(2)}, u32[]{:S(2)}) collective-permute-start(bf16[40,384]{1,0:T(8,128)(2,1)} %get-tuple-element.51), channel_id=1, source_target_pairs={{0,5},{1,4},{2,7},{3,6},{4,1},{5,0},{6,3},{7,2},{8,13},{9,12},{10,... | collective-permute-start | bytes 92168 | tf_op jit(solution)/shard_map/ppermute | solution.py:797
  35.1 69.9 %copy-start.11 = (bf16[40,384]{1,0:T(8,128)(2,1)}, bf16[40,384]{1,0:T(8,128)(2,1)S(1)}, u32[]{:S(2)}) copy-start(bf16[40,384]{1,0:T(8,128)(2,1)S(1)} %collective-permute-done.refs_1_) | copy-start | bytes 92164
  35.1 68.5 %collective-permute-start.5 = (bf16[40,384]{1,0:T(8,128)(2,1)}, bf16[40,384]{1,0:T(8,128)(2,1)S(1)}, u32[]{:S(2)}, u32[]{:S(2)}) collective-permute-start(bf16[40,384]{1,0:T(8,128)(2,1)} %get-tuple-element.52), channel_id=1, source_target_pairs={{0,6},{1,7},{2,4},{3,5},{4,2},{5,3},{6,0},{7,1},{8,14},{9,15},{10,... | collective-permute-start | bytes 92168 | tf_op jit(solution)/shard_map/ppermute | solution.py:797
  43.9 61.1 %copy-start.12 = (bf16[40,384]{1,0:T(8,128)(2,1)}, bf16[40,384]{1,0:T(8,128)(2,1)S(1)}, u32[]{:S(2)}) copy-start(bf16[40,384]{1,0:T(8,128)(2,1)S(1)} %collective-permute-done.1.refs_2_) | copy-start | bytes 92164
  43.9 59.7 %collective-permute-start.6 = (bf16[40,384]{1,0:T(8,128)(2,1)}, bf16[40,384]{1,0:T(8,128)(2,1)S(1)}, u32[]{:S(2)}, u32[]{:S(2)}) collective-permute-start(bf16[40,384]{1,0:T(8,128)(2,1)} %get-tuple-element.53), channel_id=1, source_target_pairs={{0,7},{1,6},{2,5},{3,4},{4,3},{5,2},{6,1},{7,0},{8,15},{9,14},{10,... | collective-permute-start | bytes 92168 | tf_op jit(solution)/shard_map/ppermute | solution.py:797
  52.9 52.1 %copy-start.13 = (bf16[40,384]{1,0:T(8,128)(2,1)}, bf16[40,384]{1,0:T(8,128)(2,1)S(1)}, u32[]{:S(2)}) copy-start(bf16[40,384]{1,0:T(8,128)(2,1)S(1)} %collective-permute-done.2.refs_3_) | copy-start | bytes 92164
  99.7 5.3 %copy-start.14 = (bf16[40,384]{1,0:T(8,128)(2,1)}, bf16[40,384]{1,0:T(8,128)(2,1)S(1)}, u32[]{:S(2)}) copy-start(bf16[40,384]{1,0:T(8,128)(2,1)S(1)} %collective-permute-done.3.refs_4_) | copy-start | bytes 92164
  100.5 4.5 %copy-start.15 = (bf16[40,384]{1,0:T(8,128)(2,1)}, bf16[40,384]{1,0:T(8,128)(2,1)S(1)}, u32[]{:S(2)}) copy-start(bf16[40,384]{1,0:T(8,128)(2,1)S(1)} %collective-permute-done.4.refs_5_) | copy-start | bytes 92164
  103.6 1.4 copy-start.16
  103.6 1.4 copy-start.17
  166.3 91.9 %all-to-all-start.2 = ((bf16[128,52,2,128]{3,2,1,0:T(2,128)(2,1)}), bf16[128,52,2,128]{3,2,1,0:T(2,128)(2,1)}, u32[]{:S(2)}, u32[]{:S(2)}) async-start(bf16[128,52,2,128]{3,2,1,0:T(2,128)(2,1)} %bitcast.49), calls=%async_computation.2 | async-start | bytes 6815744 | tf_op jit(solution)/shard_map/all_to_all | solution.py:793
  174.0 19.9 %copy-start.9 = (f32[16,128]{1,0:T(8,128)S(1)}, f32[16,128]{1,0:T(8,128)}, u32[]{:S(2)}) copy-start(f32[16,128]{1,0:T(8,128)} %get-tuple-element.72) | copy-start | bytes 24580
  186.7 1.9 collective-permute-start.7
  190.4 6.0 %collective-permute-start.9 = (bf16[3,20,320]{2,1,0:T(8,128)(2,1)S(1)}, bf16[3,20,320]{2,1,0:T(8,128)(2,1)S(1)}, u32[]{:S(2)}, u32[]{:S(2)}) collective-permute-start(bf16[3,20,320]{2,1,0:T(8,128)(2,1)S(1)} %get-tuple-element.73), channel_id=1, source_target_pairs={{0,2},{1,3},{2,0},{3,1},{4,6},{5,7},{6,4},{7,5},{8,10},{9,11},{10,... | collective-permute-start | bytes 115208 | tf_op jit(solution)/shard_map/ppermute | solution.py:797
  193.3 6.4 %collective-permute-start.8 = (bf16[3,20,320]{2,1,0:T(8,128)(2,1)S(1)}, bf16[3,20,320]{2,1,0:T(8,128)(2,1)S(1)}, u32[]{:S(2)}, u32[]{:S(2)}) collective-permute-start(bf16[3,20,320]{2,1,0:T(8,128)(2,1)S(1)} %get-tuple-element.74), channel_id=1, source_target_pairs={{0,1},{1,0},{2,3},{3,2},{4,5},{5,4},{6,7},{7,6},{8,9},{9,8},{10,11... | collective-permute-start | bytes 115208 | tf_op jit(solution)/shard_map/ppermute | solution.py:797
  194.0 21.9 %collective-permute-start.15 = (f32[16]{0:T(128)S(1)}, f32[16]{0:T(128)S(1)}, u32[]{:S(2)}, u32[]{:S(2)}) collective-permute-start(f32[16]{0:T(128)S(1)} %slice_reduce_fusion), channel_id=1, source_target_pairs={{0,128},{128,0},{1,129},{129,1},{2,130},{130,2},{3,131},{131,3},{4... | collective-permute-start | bytes 200 | tf_op jit(solution)/shard_map/ppermute | solution.py:839
  196.4 61.8 %copy-start.1 = (bf16[3,20,320]{2,1,0:T(8,128)(2,1)}, bf16[3,20,320]{2,1,0:T(8,128)(2,1)S(1)}, u32[]{:S(2)}) copy-start(bf16[3,20,320]{2,1,0:T(8,128)(2,1)S(1)} %collective-permute-done.9.refs_2_) | copy-start | bytes 115204
  199.7 58.4 %copy-start.2 = (bf16[3,20,320]{2,1,0:T(8,128)(2,1)}, bf16[3,20,320]{2,1,0:T(8,128)(2,1)S(1)}, u32[]{:S(2)}) copy-start(bf16[3,20,320]{2,1,0:T(8,128)(2,1)S(1)} %collective-permute-done.8.refs_1_) | copy-start | bytes 115204
  199.7 17.7 %collective-permute-start.10 = (bf16[3,20,320]{2,1,0:T(8,128)(2,1)S(1)}, bf16[3,20,320]{2,1,0:T(8,128)(2,1)S(1)}, u32[]{:S(2)}, u32[]{:S(2)}) collective-permute-start(bf16[3,20,320]{2,1,0:T(8,128)(2,1)S(1)} %get-tuple-element.65), channel_id=1, source_target_pairs={{0,3},{1,2},{2,1},{3,0},{4,7},{5,6},{6,5},{7,4},{8,11},{9,10},{10,... | collective-permute-start | bytes 115208 | tf_op jit(solution)/shard_map/ppermute | solution.py:797
  201.5 50.9 %collective-permute-start.11 = (bf16[3,20,320]{2,1,0:T(8,128)(2,1)S(1)}, bf16[3,20,320]{2,1,0:T(8,128)(2,1)S(1)}, u32[]{:S(2)}, u32[]{:S(2)}) collective-permute-start(bf16[3,20,320]{2,1,0:T(8,128)(2,1)S(1)} %get-tuple-element.66), channel_id=1, source_target_pairs={{0,4},{1,5},{2,6},{3,7},{4,0},{5,1},{6,2},{7,3},{8,12},{9,13},{10,... | collective-permute-start | bytes 115208 | tf_op jit(solution)/shard_map/ppermute | solution.py:797
  207.9 46.3 %collective-permute-start.12 = (bf16[3,20,320]{2,1,0:T(8,128)(2,1)S(1)}, bf16[3,20,320]{2,1,0:T(8,128)(2,1)S(1)}, u32[]{:S(2)}, u32[]{:S(2)}) collective-permute-start(bf16[3,20,320]{2,1,0:T(8,128)(2,1)S(1)} %get-tuple-element.67), channel_id=1, source_target_pairs={{0,5},{1,4},{2,7},{3,6},{4,1},{5,0},{6,3},{7,2},{8,13},{9,12},{10,... | collective-permute-start | bytes 115208 | tf_op jit(solution)/shard_map/ppermute | solution.py:797
  207.9 49.7 %collective-permute-start.13 = (bf16[3,20,320]{2,1,0:T(8,128)(2,1)S(1)}, bf16[3,20,320]{2,1,0:T(8,128)(2,1)S(1)}, u32[]{:S(2)}, u32[]{:S(2)}) collective-permute-start(bf16[3,20,320]{2,1,0:T(8,128)(2,1)S(1)} %get-tuple-element.68), channel_id=1, source_target_pairs={{0,6},{1,7},{2,4},{3,5},{4,2},{5,3},{6,0},{7,1},{8,14},{9,15},{10,... | collective-permute-start | bytes 115208 | tf_op jit(solution)/shard_map/ppermute | solution.py:797
  215.9 42.1 %collective-permute-start.14 = (bf16[3,20,320]{2,1,0:T(8,128)(2,1)S(1)}, bf16[3,20,320]{2,1,0:T(8,128)(2,1)S(1)}, u32[]{:S(2)}, u32[]{:S(2)}) collective-permute-start(bf16[3,20,320]{2,1,0:T(8,128)(2,1)S(1)} %get-tuple-element.69), channel_id=1, source_target_pairs={{0,7},{1,6},{2,5},{3,4},{4,3},{5,2},{6,1},{7,0},{8,15},{9,14},{10,... | collective-permute-start | bytes 115208 | tf_op jit(solution)/shard_map/ppermute | solution.py:797
  217.4 40.8 %copy-start.3 = (bf16[3,20,320]{2,1,0:T(8,128)(2,1)}, bf16[3,20,320]{2,1,0:T(8,128)(2,1)S(1)}, u32[]{:S(2)}) copy-start(bf16[3,20,320]{2,1,0:T(8,128)(2,1)S(1)} %collective-permute-done.10.refs_3_) | copy-start | bytes 115204
  252.5 5.7 %copy-start.4 = (bf16[3,20,320]{2,1,0:T(8,128)(2,1)}, bf16[3,20,320]{2,1,0:T(8,128)(2,1)S(1)}, u32[]{:S(2)}) copy-start(bf16[3,20,320]{2,1,0:T(8,128)(2,1)S(1)} %collective-permute-done.11.refs_4_) | copy-start | bytes 115204
  254.3 3.9 %copy-start.5 = (bf16[3,20,320]{2,1,0:T(8,128)(2,1)}, bf16[3,20,320]{2,1,0:T(8,128)(2,1)S(1)}, u32[]{:S(2)}) copy-start(bf16[3,20,320]{2,1,0:T(8,128)(2,1)S(1)} %collective-permute-done.12.refs_5_) | copy-start | bytes 115204
  257.7 0.6 copy-start.6
  258.0 0.6 copy-start.7

commit v7 on v6

--- a/solution.py
+++ b/solution.py
@@ -576,11 +576,11 @@
 
 
 def gradient_kernel(
-    stacked_hbm, target_hbm, sums_ref, cotangent_ref, share_ref, to_mixing_hbm,
+    stacked_hbm, target_hbm, sums_hbm, cotangent_ref, share_ref, to_mixing_hbm,
     from_full_hbm, from_half_hbm,
     back_ref, grad_hbm, loss_ref,
     stacked_ref, target_ref, to_mixing_ref, from_full_ref, from_half_ref, grad_ref,
-    held_ref, member_ref, degree_ref, in_sem, stacked_sem, sem,
+    held_ref, member_ref, degree_ref, sums_ref, in_sem, stacked_sem, sem,
 ):
     loads = [
         pltpu.make_async_copy(there, here, in_sem.at[n])
@@ -590,9 +590,11 @@
                 (target_hbm, target_ref),
                 (from_full_hbm, from_full_ref),
                 (from_half_hbm, from_half_ref),
+                (sums_hbm, sums_ref),
             )
         )
     ]
+    loads[4].start()
     piece = L // 4
 
     def load_piece(n):
@@ -609,10 +611,11 @@
         copy.start()
     for n in range(4):
         load_piece(n).start()
-    for copy in loads[2:]:
+    for copy in loads[2:4]:
         copy.start()
     member_ref[...] = block_mask(256, "block")
     degree_ref[...] = block_mask(256, "inside")
+    loads[4].wait()
     sums = jnp.sum(sums_ref[...], axis=0)
     sums = sum(sums[10 * n : 10 * n + 10] for n in range(4))
     lane = iota((NBANDS, 128), 1)
@@ -664,7 +667,7 @@
         load_piece(n).wait()
         lax.fori_loop(5 * n, 5 * n + 5, mix, 0, unroll=5)
         keep_piece(n).start()
-    for copy in loads[2:]:
+    for copy in loads[2:4]:
         copy.wait()
     def inverse(g, carry):
         for slot in range(3):
@@ -704,7 +707,7 @@
             jax.ShapeDtypeStruct((MEMBERS, L, WIDE), BF),
             jax.ShapeDtypeStruct((NBANDS, 128), F32),
         ],
-        in_specs=[HBM, HBM, VMEM, VMEM, VMEM, HBM, HBM, HBM],
+        in_specs=[HBM, HBM, HBM, VMEM, VMEM, HBM, HBM, HBM],
         out_specs=[HBM, HBM, VMEM],
         scratch_shapes=[
             pltpu.VMEM((JJ, L, WIDE), BF),
@@ -716,7 +719,8 @@
             pltpu.VMEM((16, 8, 104, 128), BF),
             pltpu.VMEM((256, 256), BF),
             pltpu.VMEM((256, 256), BF),
-            pltpu.SemaphoreType.DMA((4,)),
+            pltpu.VMEM((32, 40, 128), F32),
+            pltpu.SemaphoreType.DMA((5,)),
             pltpu.SemaphoreType.DMA((4,)),
             pltpu.SemaphoreType.DMA((8,)),
         ],
@@ -814,8 +818,13 @@
         (target[0], partners, full, band_cotangent, packed)
     )
     rows = travel(packed)
-    blocks = target_blocks(place, target_in, band_ids)
-    targets = [blocks[0]] + swap(blocks, range(1, 8))
+    blocks = list(target_blocks(place, target_in, band_ids))
+    far = swap(blocks, range(4, 8))
+    near = swap(blocks, (3,))
+    for k in (2, 1):
+        blocks[k], near[0] = lax.optimization_barrier((blocks[k], near[0]))
+        near = swap(blocks, (k,)) + near
+    targets = [blocks[0]] + near + far
     other = jnp.concatenate(
         [jnp.full((16,), MEMBERS, jnp.int32), partners.T.reshape(64), jnp.zeros((48,), jnp.int32)]
     )
@@ -840,10 +849,13 @@
     weight = weights(place, rows, grads, full, half)
     beside = lax.ppermute(weight[1], "dp", [(0, 1), (1, 0)])
     weight = (weight[0].astype(F32) + beside.astype(F32)).astype(BF)
-    near = swap([weight[k] for k in range(8)], (1, 2))
-    *far, near[0], near[1] = lax.optimization_barrier((*[weight[k] for k in range(3, 8)], *near))
-    far = swap([weight[0]] * 3 + far, range(3, 8))
-    native_grad, grad_analysis = unpack(place, returned, [weight[0]] + near + far)
+    pieces = [weight[k] for k in range(8)]
+    far = swap(pieces, range(4, 8))
+    near = swap(pieces, (3,))
+    for k in (2, 1):
+        pieces[k], near[0] = lax.optimization_barrier((pieces[k], near[0]))
+        near = swap(pieces, (k,)) + near
+    native_grad, grad_analysis = unpack(place, returned, [pieces[0]] + near + far)
     native_grad = native_grad.reshape(20, 320, 2, 128)
     grad_fourier = jnp.transpose(native_grad, (2, 0, 1, 3)).reshape(1, 2, 20, 40960)
     return (grad_fourier, grad_analysis, loss_bands)

time: 267 us -> 266 us (level)
  transfers between devices with their start and end apart: 18 -> 18, of which waited for: 12 -> 10; matrix products, arithmetic and copies ran while one was open for 2% -> 2% of each run, Pallas kernels for 8% -> 8%
where the time goes in v7:
time: 266 us; the launch traced here: 263 us
  waiting for transfers between devices  102 us (38%)
  starting transfers between devices  62.2 us (23%)
  Pallas kernels  59.6 us (22%)
  blocking collectives  31.7 us (12%)
  local copies, waits for them, and re-layouts  4.08 us (2%)
    ppermute x14, waiting for transfers between devices, swap(): lax.ppermute(blocks[k], ENS, [(e, e ^ k) for e in range(8)])  97.7 us
    ppermute x14, starting transfers between devices, swap(): lax.ppermute(blocks[k], ENS, [(e, e ^ k) for e in range(8)])  38.4 us
    all_to_all x1, blocking collectives, exchange(): return lax.all_to_all(x, axes, split_axis=0, concat_axis=0, tiled=True)  31.7 us
    all_to_all x2, starting transfers between devices, exchange(): return lax.all_to_all(x, axes, split_axis=0, concat_axis=0, tiled=True)  23.6 us
    pallas_call x1, Pallas kernels, gradient(): pl.pallas_call(gradient_kernel, out_shape=[jax.ShapeDtypeStruct((16, 8, 1...  14.9 us
    pallas_call x1, Pallas kernels, spectra(): pl.pallas_call(spectra_kernel, out_shape=[jax.ShapeDtypeStruct((JJ, L, WI...  14.5 us
    pallas_call x1, Pallas kernels, weights(): pl.pallas_call(weight_kernel, out_shape=jax.ShapeDtypeStruct((2, 8, 3, 20...  11.6 us
    pallas_call x1, Pallas kernels, prepare(): pl.pallas_call(prepare_kernel, out_shape=[jax.ShapeDtypeStruct((2, 2, L,...  6.92 us
  transfers between devices with their start and end apart: 18, of which 10 were waited for; matrix products, arithmetic and copies ran while one was open for 2% of the time, Pallas kernels for 8%

profile of v7, /device:TPU:8, one launch (start us, length us, event | category | flops | bytes accessed | tf_op | source)
XLA Modules:
  0.0 263.2 jit_solution(11782650383234349722)
XLA Ops:
  0.6 0.0 copy-start
  0.6 4.9 %pack.1 = bf16[16,8,104,128]{3,2,1,0:T(8,128)(2,1)} custom-call(bf16[20,640,128]{2,1,0:T(8,128)(2,1)} %bitcast.50, bf16[64,64]{1,0:T(8,128)(2,1)} %constant.45.clone.whole_ref, bf16[2,96,160]{2,1,0:T(8,128)(2,1)} %constant.46.clone.half_ref), custom_call_target="tpu_custom_call" | custom-call | tf_op jit(solution)/shard_map/pack/pallas_call | solution.py:214
  5.5 0.0 copy-start.8
  5.5 0.0 copy-start.10
  5.6 15.9 %all-to-all-start = ((bf16[128,52,2,128]{3,2,1,0:T(2,128)(2,1)}), bf16[128,52,2,128]{3,2,1,0:T(2,128)(2,1)}, u32[]{:S(2)}, u32[]{:S(2)}) async-start(bf16[128,52,2,128]{3,2,1,0:T(2,128)(2,1)} %bitcast.47), calls=%async_computation | async-start | bytes 6815744 | tf_op jit(solution)/shard_map/all_to_all | solution.py:797
  21.5 0.7 copy.20.band_ref
  22.1 0.6 pad_add_fusion.place_ref
  22.8 1.9 target_blocks.1
  24.6 2.8 %collective-permute-start = (bf16[40,384]{1,0:T(8,128)(2,1)}, bf16[40,384]{1,0:T(8,128)(2,1)S(1)}, u32[]{:S(2)}, u32[]{:S(2)}) collective-permute-start(bf16[40,384]{1,0:T(8,128)(2,1)} %get-tuple-element.50), channel_id=1, source_target_pairs={{0,3},{1,2},{2,1},{3,0},{4,7},{5,6},{6,5},{7,4},{8,11},{9,10},{10,... | collective-permute-start | bytes 92168 | tf_op jit(solution)/shard_map/ppermute | solution.py:801
  27.4 5.4 %collective-permute-start.3 = (bf16[40,384]{1,0:T(8,128)(2,1)}, bf16[40,384]{1,0:T(8,128)(2,1)S(1)}, u32[]{:S(2)}, u32[]{:S(2)}) collective-permute-start(bf16[40,384]{1,0:T(8,128)(2,1)} %get-tuple-element.55), channel_id=1, source_target_pairs={{0,4},{1,5},{2,6},{3,7},{4,0},{5,1},{6,2},{7,3},{8,12},{9,13},{10,... | collective-permute-start | bytes 92168 | tf_op jit(solution)/shard_map/ppermute | solution.py:801
  32.8 0.2 collective-permute-start.4
  33.0 6.6 %collective-permute-start.5 = (bf16[40,384]{1,0:T(8,128)(2,1)}, bf16[40,384]{1,0:T(8,128)(2,1)S(1)}, u32[]{:S(2)}, u32[]{:S(2)}) collective-permute-start(bf16[40,384]{1,0:T(8,128)(2,1)} %get-tuple-element.57), channel_id=1, source_target_pairs={{0,6},{1,7},{2,4},{3,5},{4,2},{5,3},{6,0},{7,1},{8,14},{9,15},{10,... | collective-permute-start | bytes 92168 | tf_op jit(solution)/shard_map/ppermute | solution.py:801
  39.6 2.7 %collective-permute-start.6 = (bf16[40,384]{1,0:T(8,128)(2,1)}, bf16[40,384]{1,0:T(8,128)(2,1)S(1)}, u32[]{:S(2)}, u32[]{:S(2)}) collective-permute-start(bf16[40,384]{1,0:T(8,128)(2,1)} %get-tuple-element.58), channel_id=1, source_target_pairs={{0,7},{1,6},{2,5},{3,4},{4,3},{5,2},{6,1},{7,0},{8,15},{9,14},{10,... | collective-permute-start | bytes 92168 | tf_op jit(solution)/shard_map/ppermute | solution.py:801
  42.3 0.1 reshape.43
  42.4 5.7 %collective-permute-done.1.refs_2_ = bf16[40,384]{1,0:T(8,128)(2,1)S(1)} collective-permute-done((bf16[40,384]{1,0:T(8,128)(2,1)}, bf16[40,384]{1,0:T(8,128)(2,1)S(1)}, u32[]{:S(2)}, u32[]{:S(2)}) %collective-permute-start.1) | collective-permute-done | bytes 30752 | tf_op jit(solution)/shard_map/ppermute | solution.py:801
  48.1 0.1 pad_add_fusion.1
  48.2 0.7 broadcast_in_dim.17.cotangent_ref
  48.9 0.7 broadcast_in_dim.19.other_column_ref.other_ref
  49.6 6.9 %prepare.1 = (bf16[2,2,320,640]{3,2,1,0:T(8,128)(2,1)}, bf16[2,2,320,384]{3,2,1,0:T(8,128)(2,1)}, bf16[2,640,704]{2,1,0:T(8,128)(2,1)}, bf16[2,384,704]{2,1,0:T(8,128)(2,1)}, bf16[128,2048]{1,0:T(8,128)(2,1)}) custom-call(s32[3]{0:T(128)} %pad_add_fusion.place_ref, bf16[20,320,320]{2,1,0:T(8,128)(2,1)} %bitcast.48, ...), custom_call_target="tpu_custom_call" | custom-call | tf_op jit(solution)/shard_map/prepare/pallas_call | solution.py:356
  56.5 43.1 %collective-permute-done.3.refs_4_ = bf16[40,384]{1,0:T(8,128)(2,1)S(1)} collective-permute-done((bf16[40,384]{1,0:T(8,128)(2,1)}, bf16[40,384]{1,0:T(8,128)(2,1)S(1)}, u32[]{:S(2)}, u32[]{:S(2)}) %collective-permute-start.3) | collective-permute-done | bytes 30752 | tf_op jit(solution)/shard_map/ppermute | solution.py:801
  99.7 0.9 collective-permute-done.4.refs_5_
  100.5 3.1 %collective-permute-done.5.refs_6_ = bf16[40,384]{1,0:T(8,128)(2,1)S(1)} collective-permute-done((bf16[40,384]{1,0:T(8,128)(2,1)}, bf16[40,384]{1,0:T(8,128)(2,1)S(1)}, u32[]{:S(2)}, u32[]{:S(2)}) %collective-permute-start.5) | collective-permute-done | bytes 30752 | tf_op jit(solution)/shard_map/ppermute | solution.py:801
  103.6 1.4 all-to-all-done
  105.0 14.5 %spectra.1 = (bf16[17,320,384]{2,1,0:T(8,128)(2,1)}, bf16[320,384]{1,0:T(8,128)(2,1)}, f32[32,40,128]{2,1,0:T(8,128)}) custom-call(s32[3]{0:T(128)} %pad_add_fusion.place_ref, bf16[16,8,104,128]{3,2,1,0:T(8,128)(2,1)} %bitcast.8.rows_hbm.rows_ref, bf16[2,2,320,640]{3,2,1,0:T(8,128)(2,1)} %get-tuple-element.44.to_full_hbm, ...), custom_call_target="tpu_custom_call" | custom-call | flops 10000000000 | bytes 12000000 | tf_op jit(solution)/shard_map/spectra/pallas_call | solution.py:547
  119.5 31.7 %all_to_all.15 = f32[128,5,2,128]{3,2,1,0:T(2,128)} all-to-all(f32[128,5,2,128]{3,2,1,0:T(2,128)} %bitcast.51), channel_id=1, replica_groups=mesh['dp'=2,'order_0'=4,'order_1'=4,'ens_0'=2,'ens_1'=4] {'order_0','ord..., dimensions={0} | all-to-all | bytes 1310720 | tf_op jit(solution)/shard_map/all_to_all | solution.py:797
  151.2 14.9 %gradient.1 = (bf16[16,8,104,128]{3,2,1,0:T(8,128)(2,1)}, bf16[16,320,384]{2,1,0:T(8,128)(2,1)}, f32[16,128]{1,0:T(8,128)}) custom-call(bf16[17,320,384]{2,1,0:T(8,128)(2,1)} %get-tuple-element.59.stacked_hbm, bf16[320,384]{1,0:T(8,128)(2,1)} %get-tuple-element.60.target_hbm, f32[32,40,128]{2,1,0:T(8,128)} %bitcast.52, ...), custom_call_target="tpu_custom_call" | custom-call | flops 10000000000 | bytes 12000000 | tf_op jit(solution)/shard_map/gradient/pallas_call | solution.py:703
  166.1 7.7 %all-to-all-start.2 = ((bf16[128,52,2,128]{3,2,1,0:T(2,128)(2,1)}), bf16[128,52,2,128]{3,2,1,0:T(2,128)(2,1)}, u32[]{:S(2)}, u32[]{:S(2)}) async-start(bf16[128,52,2,128]{3,2,1,0:T(2,128)(2,1)} %bitcast.49), calls=%async_computation.2 | async-start | bytes 6815744 | tf_op jit(solution)/shard_map/all_to_all | solution.py:797
  173.9 11.6 %weights.1 = bf16[2,8,3,20,320]{4,3,2,1,0:T(8,128)(2,1)} custom-call(s32[3]{0:T(128)} %pad_add_fusion.place_ref, bf16[16,8,104,128]{3,2,1,0:T(8,128)(2,1)} %bitcast.8.rows_hbm.rows_ref, bf16[16,320,384]{2,1,0:T(8,128)(2,1)} %get-tuple-element.67.grad_ref, bf16[320,640]{1,0:T(8,128)(2,1)} %constant.43.clone.full_ref, bf16[2,320,384]{2,1,0:T(8,128)(2,1)} %constant.44.clone.half_ref), custom_call_target="tpu_custom_call" | custom-call | flops 5000000000 | bytes 8000000 | tf_op jit(solution)/shard_map/weights/pallas_call | solution.py:779
  185.5 1.1 slice_bitcast_fusion
  186.5 0.1 collective-permute-start.7
  186.6 1.8 collective-permute-done.7
  188.4 1.1 fusion
  189.6 0.7 slice_bitcast_fusion.2
  190.2 2.7 %collective-permute-start.8 = (bf16[3,20,320]{2,1,0:T(8,128)(2,1)S(1)}, bf16[3,20,320]{2,1,0:T(8,128)(2,1)S(1)}, u32[]{:S(2)}, u32[]{:S(2)}) collective-permute-start(bf16[3,20,320]{2,1,0:T(8,128)(2,1)S(1)} %get-tuple-element.79), channel_id=1, source_target_pairs={{0,3},{1,2},{2,1},{3,0},{4,7},{5,6},{6,5},{7,4},{8,11},{9,10},{10,... | collective-permute-start | bytes 115208 | tf_op jit(solution)/shard_map/ppermute | solution.py:801
  192.9 3.3 %collective-permute-done.8.refs_3_ = bf16[3,20,320]{2,1,0:T(8,128)(2,1)S(1)} collective-permute-done((bf16[3,20,320]{2,1,0:T(8,128)(2,1)S(1)}, bf16[3,20,320]{2,1,0:T(8,128)(2,1)S(1)}, u32[]{:S(2)}, u32[]{:S(2)}) %collective-permute-start.8) | collective-permute-done | bytes 38432 | tf_op jit(solution)/shard_map/ppermute | solution.py:801
  196.2 1.2 collective-permute-start.9
  197.4 0.1 slice_reduce_fusion
  197.5 0.1 collective-permute-start.15
  197.6 6.3 %collective-permute-start.14 = (bf16[3,20,320]{2,1,0:T(8,128)(2,1)S(1)}, bf16[3,20,320]{2,1,0:T(8,128)(2,1)S(1)}, u32[]{:S(2)}, u32[]{:S(2)}) collective-permute-start(bf16[3,20,320]{2,1,0:T(8,128)(2,1)S(1)} %get-tuple-element.75), channel_id=1, source_target_pairs={{0,7},{1,6},{2,5},{3,4},{4,3},{5,2},{6,1},{7,0},{8,15},{9,14},{10,... | collective-permute-start | bytes 115208 | tf_op jit(solution)/shard_map/ppermute | solution.py:801
  204.0 3.1 %collective-permute-start.13 = (bf16[3,20,320]{2,1,0:T(8,128)(2,1)S(1)}, bf16[3,20,320]{2,1,0:T(8,128)(2,1)S(1)}, u32[]{:S(2)}, u32[]{:S(2)}) collective-permute-start(bf16[3,20,320]{2,1,0:T(8,128)(2,1)S(1)} %get-tuple-element.76), channel_id=1, source_target_pairs={{0,6},{1,7},{2,4},{3,5},{4,2},{5,3},{6,0},{7,1},{8,14},{9,15},{10,... | collective-permute-start | bytes 115208 | tf_op jit(solution)/shard_map/ppermute | solution.py:801
  207.1 4.9 %collective-permute-start.12 = (bf16[3,20,320]{2,1,0:T(8,128)(2,1)S(1)}, bf16[3,20,320]{2,1,0:T(8,128)(2,1)S(1)}, u32[]{:S(2)}, u32[]{:S(2)}) collective-permute-start(bf16[3,20,320]{2,1,0:T(8,128)(2,1)S(1)} %get-tuple-element.77), channel_id=1, source_target_pairs={{0,5},{1,4},{2,7},{3,6},{4,1},{5,0},{6,3},{7,2},{8,13},{9,12},{10,... | collective-permute-start | bytes 115208 | tf_op jit(solution)/shard_map/ppermute | solution.py:801
  212.0 0.2 collective-permute-start.11
  212.2 2.4 collective-permute-start.10
  214.5 0.5 add.19
  215.0 39.1 %collective-permute-done.14.refs_7_ = bf16[3,20,320]{2,1,0:T(8,128)(2,1)S(1)} collective-permute-done((bf16[3,20,320]{2,1,0:T(8,128)(2,1)S(1)}, bf16[3,20,320]{2,1,0:T(8,128)(2,1)S(1)}, u32[]{:S(2)}, u32[]{:S(2)}) %collective-permute-start.14) | collective-permute-done | bytes 38432 | tf_op jit(solution)/shard_map/ppermute | solution.py:801
  254.1 2.5 collective-permute-done.13.refs_6_
  256.6 1.4 all-to-all-done.2
  258.1 5.0 %unpack.1 = (bf16[20,640,128]{2,1,0:T(8,128)(2,1)}, f32[20,20,320]{2,1,0:T(8,128)}) custom-call(s32[3]{0:T(128)} %pad_add_fusion.place_ref, bf16[16,8,104,128]{3,2,1,0:T(8,128)(2,1)} %bitcast.15.in_hbm, bf16[64,64]{1,0:T(8,128)(2,1)} %constant.48.clone.whole_ref, bf16[2,160,96]{2,1,0:T(8,128)(2,1)} %constant.49.clone.half_ref, ...), custom_call_target="tpu_custom_call" | custom-call | tf_op jit(solution)/shard_map/unpack/pallas_call | solution.py:226
  (46 shorter events, 0.1 us)
Async XLA Ops:
  0.6 41.6 %copy-start = (f32[2,16]{1,0:T(2,128)S(1)}, f32[2,16]{1,0:T(2,128)}, u32[]{:S(2)}) copy-start(f32[2,16]{1,0:T(2,128)} %param.18) | copy-start | bytes 388
  5.5 15.9 %copy-start.8 = (s32[40,20]{0,1:T(8,128)S(1)}, s32[40,20]{0,1:T(8,128)}, u32[]{:S(2)}) copy-start(s32[40,20]{0,1:T(8,128)} %param.16) | copy-start | bytes 9604
  5.5 36.8 %copy-start.10 = (s32[16,4]{0,1:T(4,128)S(1)}, s32[16,4]{0,1:T(4,128)}, u32[]{:S(2)}) copy-start(s32[16,4]{0,1:T(4,128)} %param.17) | copy-start | bytes 772
  5.6 99.4 %all-to-all-start = ((bf16[128,52,2,128]{3,2,1,0:T(2,128)(2,1)}), bf16[128,52,2,128]{3,2,1,0:T(2,128)(2,1)}, u32[]{:S(2)}, u32[]{:S(2)}) async-start(bf16[128,52,2,128]{3,2,1,0:T(2,128)(2,1)} %bitcast.47), calls=%async_computation | async-start | bytes 6815744 | tf_op jit(solution)/shard_map/all_to_all | solution.py:797
  24.6 17.6 %collective-permute-start = (bf16[40,384]{1,0:T(8,128)(2,1)}, bf16[40,384]{1,0:T(8,128)(2,1)S(1)}, u32[]{:S(2)}, u32[]{:S(2)}) collective-permute-start(bf16[40,384]{1,0:T(8,128)(2,1)} %get-tuple-element.50), channel_id=1, source_target_pairs={{0,3},{1,2},{2,1},{3,0},{4,7},{5,6},{6,5},{7,4},{8,11},{9,10},{10,... | collective-permute-start | bytes 92168 | tf_op jit(solution)/shard_map/ppermute | solution.py:801
  27.4 72.3 %collective-permute-start.3 = (bf16[40,384]{1,0:T(8,128)(2,1)}, bf16[40,384]{1,0:T(8,128)(2,1)S(1)}, u32[]{:S(2)}, u32[]{:S(2)}) collective-permute-start(bf16[40,384]{1,0:T(8,128)(2,1)} %get-tuple-element.55), channel_id=1, source_target_pairs={{0,4},{1,5},{2,6},{3,7},{4,0},{5,1},{6,2},{7,3},{8,12},{9,13},{10,... | collective-permute-start | bytes 92168 | tf_op jit(solution)/shard_map/ppermute | solution.py:801
  32.8 67.8 %collective-permute-start.4 = (bf16[40,384]{1,0:T(8,128)(2,1)}, bf16[40,384]{1,0:T(8,128)(2,1)S(1)}, u32[]{:S(2)}, u32[]{:S(2)}) collective-permute-start(bf16[40,384]{1,0:T(8,128)(2,1)} %get-tuple-element.56), channel_id=1, source_target_pairs={{0,5},{1,4},{2,7},{3,6},{4,1},{5,0},{6,3},{7,2},{8,13},{9,12},{10,... | collective-permute-start | bytes 92168 | tf_op jit(solution)/shard_map/ppermute | solution.py:801
  33.0 70.6 %collective-permute-start.5 = (bf16[40,384]{1,0:T(8,128)(2,1)}, bf16[40,384]{1,0:T(8,128)(2,1)S(1)}, u32[]{:S(2)}, u32[]{:S(2)}) collective-permute-start(bf16[40,384]{1,0:T(8,128)(2,1)} %get-tuple-element.57), channel_id=1, source_target_pairs={{0,6},{1,7},{2,4},{3,5},{4,2},{5,3},{6,0},{7,1},{8,14},{9,15},{10,... | collective-permute-start | bytes 92168 | tf_op jit(solution)/shard_map/ppermute | solution.py:801
  39.6 64.0 %collective-permute-start.6 = (bf16[40,384]{1,0:T(8,128)(2,1)}, bf16[40,384]{1,0:T(8,128)(2,1)S(1)}, u32[]{:S(2)}, u32[]{:S(2)}) collective-permute-start(bf16[40,384]{1,0:T(8,128)(2,1)} %get-tuple-element.58), channel_id=1, source_target_pairs={{0,7},{1,6},{2,5},{3,4},{4,3},{5,2},{6,1},{7,0},{8,15},{9,14},{10,... | collective-permute-start | bytes 92168 | tf_op jit(solution)/shard_map/ppermute | solution.py:801
  42.3 62.7 %copy-start.11 = (bf16[40,384]{1,0:T(8,128)(2,1)}, bf16[40,384]{1,0:T(8,128)(2,1)S(1)}, u32[]{:S(2)}) copy-start(bf16[40,384]{1,0:T(8,128)(2,1)S(1)} %collective-permute-done.refs_3_) | copy-start | bytes 92164
  42.3 5.8 %collective-permute-start.1 = (bf16[40,384]{1,0:T(8,128)(2,1)}, bf16[40,384]{1,0:T(8,128)(2,1)S(1)}, u32[]{:S(2)}, u32[]{:S(2)}) collective-permute-start(bf16[40,384]{1,0:T(8,128)(2,1)} %get-tuple-element.51), channel_id=1, source_target_pairs={{0,2},{1,3},{2,0},{3,1},{4,6},{5,7},{6,4},{7,5},{8,10},{9,11},{10,... | collective-permute-start | bytes 92168 | tf_op jit(solution)/shard_map/ppermute | solution.py:801
  48.1 56.9 %copy-start.16 = (bf16[40,384]{1,0:T(8,128)(2,1)}, bf16[40,384]{1,0:T(8,128)(2,1)S(1)}, u32[]{:S(2)}) copy-start(bf16[40,384]{1,0:T(8,128)(2,1)S(1)} %collective-permute-done.1.refs_2_) | copy-start | bytes 92164
  48.1 55.5 %collective-permute-start.2 = (bf16[40,384]{1,0:T(8,128)(2,1)}, bf16[40,384]{1,0:T(8,128)(2,1)S(1)}, u32[]{:S(2)}, u32[]{:S(2)}) collective-permute-start(bf16[40,384]{1,0:T(8,128)(2,1)} %get-tuple-element.52), channel_id=1, source_target_pairs={{0,1},{1,0},{2,3},{3,2},{4,5},{5,4},{6,7},{7,6},{8,9},{9,8},{10,11... | collective-permute-start | bytes 92168 | tf_op jit(solution)/shard_map/ppermute | solution.py:801
  99.7 5.3 %copy-start.12 = (bf16[40,384]{1,0:T(8,128)(2,1)}, bf16[40,384]{1,0:T(8,128)(2,1)S(1)}, u32[]{:S(2)}) copy-start(bf16[40,384]{1,0:T(8,128)(2,1)S(1)} %collective-permute-done.3.refs_4_) | copy-start | bytes 92164
  100.5 4.5 %copy-start.13 = (bf16[40,384]{1,0:T(8,128)(2,1)}, bf16[40,384]{1,0:T(8,128)(2,1)S(1)}, u32[]{:S(2)}) copy-start(bf16[40,384]{1,0:T(8,128)(2,1)S(1)} %collective-permute-done.4.refs_5_) | copy-start | bytes 92164
  103.6 1.4 copy-start.14
  103.6 1.4 copy-start.15
  103.6 1.4 copy-start.17
  166.1 91.9 %all-to-all-start.2 = ((bf16[128,52,2,128]{3,2,1,0:T(2,128)(2,1)}), bf16[128,52,2,128]{3,2,1,0:T(2,128)(2,1)}, u32[]{:S(2)}, u32[]{:S(2)}) async-start(bf16[128,52,2,128]{3,2,1,0:T(2,128)(2,1)} %bitcast.49), calls=%async_computation.2 | async-start | bytes 6815744 | tf_op jit(solution)/shard_map/all_to_all | solution.py:797
  173.9 23.6 %copy-start.9 = (f32[16,128]{1,0:T(8,128)S(1)}, f32[16,128]{1,0:T(8,128)}, u32[]{:S(2)}) copy-start(f32[16,128]{1,0:T(8,128)} %get-tuple-element.74) | copy-start | bytes 24580
  186.5 1.9 collective-permute-start.7
  190.2 6.0 %collective-permute-start.8 = (bf16[3,20,320]{2,1,0:T(8,128)(2,1)S(1)}, bf16[3,20,320]{2,1,0:T(8,128)(2,1)S(1)}, u32[]{:S(2)}, u32[]{:S(2)}) collective-permute-start(bf16[3,20,320]{2,1,0:T(8,128)(2,1)S(1)} %get-tuple-element.79), channel_id=1, source_target_pairs={{0,3},{1,2},{2,1},{3,0},{4,7},{5,6},{6,5},{7,4},{8,11},{9,10},{10,... | collective-permute-start | bytes 115208 | tf_op jit(solution)/shard_map/ppermute | solution.py:801
  196.2 61.8 %copy-start.1 = (bf16[3,20,320]{2,1,0:T(8,128)(2,1)}, bf16[3,20,320]{2,1,0:T(8,128)(2,1)S(1)}, u32[]{:S(2)}) copy-start(bf16[3,20,320]{2,1,0:T(8,128)(2,1)S(1)} %collective-permute-done.8.refs_3_) | copy-start | bytes 115204
  196.2 15.8 %collective-permute-start.9 = (bf16[3,20,320]{2,1,0:T(8,128)(2,1)S(1)}, bf16[3,20,320]{2,1,0:T(8,128)(2,1)S(1)}, u32[]{:S(2)}, u32[]{:S(2)}) collective-permute-start(bf16[3,20,320]{2,1,0:T(8,128)(2,1)S(1)} %get-tuple-element.68), channel_id=1, source_target_pairs={{0,2},{1,3},{2,0},{3,1},{4,6},{5,7},{6,4},{7,5},{8,10},{9,11},{10,... | collective-permute-start | bytes 115208 | tf_op jit(solution)/shard_map/ppermute | solution.py:801
  197.5 14.6 %collective-permute-start.15 = (f32[16]{0:T(128)S(1)}, f32[16]{0:T(128)S(1)}, u32[]{:S(2)}, u32[]{:S(2)}) collective-permute-start(f32[16]{0:T(128)S(1)} %slice_reduce_fusion), channel_id=1, source_target_pairs={{0,128},{128,0},{1,129},{129,1},{2,130},{130,2},{3,131},{131,3},{4... | collective-permute-start | bytes 200 | tf_op jit(solution)/shard_map/ppermute | solution.py:848
  197.6 56.5 %collective-permute-start.14 = (bf16[3,20,320]{2,1,0:T(8,128)(2,1)S(1)}, bf16[3,20,320]{2,1,0:T(8,128)(2,1)S(1)}, u32[]{:S(2)}, u32[]{:S(2)}) collective-permute-start(bf16[3,20,320]{2,1,0:T(8,128)(2,1)S(1)} %get-tuple-element.75), channel_id=1, source_target_pairs={{0,7},{1,6},{2,5},{3,4},{4,3},{5,2},{6,1},{7,0},{8,15},{9,14},{10,... | collective-permute-start | bytes 115208 | tf_op jit(solution)/shard_map/ppermute | solution.py:801
  204.0 52.6 %collective-permute-start.13 = (bf16[3,20,320]{2,1,0:T(8,128)(2,1)S(1)}, bf16[3,20,320]{2,1,0:T(8,128)(2,1)S(1)}, u32[]{:S(2)}, u32[]{:S(2)}) collective-permute-start(bf16[3,20,320]{2,1,0:T(8,128)(2,1)S(1)} %get-tuple-element.76), channel_id=1, source_target_pairs={{0,6},{1,7},{2,4},{3,5},{4,2},{5,3},{6,0},{7,1},{8,14},{9,15},{10,... | collective-permute-start | bytes 115208 | tf_op jit(solution)/shard_map/ppermute | solution.py:801
  207.1 49.5 %collective-permute-start.12 = (bf16[3,20,320]{2,1,0:T(8,128)(2,1)S(1)}, bf16[3,20,320]{2,1,0:T(8,128)(2,1)S(1)}, u32[]{:S(2)}, u32[]{:S(2)}) collective-permute-start(bf16[3,20,320]{2,1,0:T(8,128)(2,1)S(1)} %get-tuple-element.77), channel_id=1, source_target_pairs={{0,5},{1,4},{2,7},{3,6},{4,1},{5,0},{6,3},{7,2},{8,13},{9,12},{10,... | collective-permute-start | bytes 115208 | tf_op jit(solution)/shard_map/ppermute | solution.py:801
  212.0 46.1 %copy-start.2 = (bf16[3,20,320]{2,1,0:T(8,128)(2,1)}, bf16[3,20,320]{2,1,0:T(8,128)(2,1)S(1)}, u32[]{:S(2)}) copy-start(bf16[3,20,320]{2,1,0:T(8,128)(2,1)S(1)} %collective-permute-done.9.refs_2_) | copy-start | bytes 115204
  212.0 44.6 %collective-permute-start.11 = (bf16[3,20,320]{2,1,0:T(8,128)(2,1)S(1)}, bf16[3,20,320]{2,1,0:T(8,128)(2,1)S(1)}, u32[]{:S(2)}, u32[]{:S(2)}) collective-permute-start(bf16[3,20,320]{2,1,0:T(8,128)(2,1)S(1)} %get-tuple-element.78), channel_id=1, source_target_pairs={{0,4},{1,5},{2,6},{3,7},{4,0},{5,1},{6,2},{7,3},{8,12},{9,13},{10,... | collective-permute-start | bytes 115208 | tf_op jit(solution)/shard_map/ppermute | solution.py:801
  212.2 44.5 %collective-permute-start.10 = (bf16[3,20,320]{2,1,0:T(8,128)(2,1)S(1)}, bf16[3,20,320]{2,1,0:T(8,128)(2,1)S(1)}, u32[]{:S(2)}, u32[]{:S(2)}) collective-permute-start(bf16[3,20,320]{2,1,0:T(8,128)(2,1)S(1)} %get-tuple-element.69), channel_id=1, source_target_pairs={{0,1},{1,0},{2,3},{3,2},{4,5},{5,4},{6,7},{7,6},{8,9},{9,8},{10,11... | collective-permute-start | bytes 115208 | tf_op jit(solution)/shard_map/ppermute | solution.py:801
  254.1 3.9 %copy-start.3 = (bf16[3,20,320]{2,1,0:T(8,128)(2,1)}, bf16[3,20,320]{2,1,0:T(8,128)(2,1)S(1)}, u32[]{:S(2)}) copy-start(bf16[3,20,320]{2,1,0:T(8,128)(2,1)S(1)} %collective-permute-done.14.refs_7_) | copy-start | bytes 115204
  256.6 1.4 copy-start.4
  256.6 1.4 copy-start.5
  256.6 1.4 copy-start.6
  256.6 1.4 copy-start.7

commit v8 on v7

--- a/solution.py
+++ b/solution.py
@@ -688,7 +688,7 @@
         where = pl.ds(2 * g, 2)
         return pltpu.make_async_copy(held_ref.at[:, where], back_ref.at[:, where], sem.at[g])
 
-    lax.fori_loop(0, 4, inverse, 0)
+    lax.fori_loop(0, 4, inverse, 0, unroll=2)
     for g in range(4):
         send(g).wait()
         keep_piece(g).wait()

time: 266 us -> 265 us (level)
  no operation moved by 1% of the time
where the time goes in v8:
time: 265 us; the launch traced here: 263 us
  waiting for transfers between devices  102 us (38%)
  starting transfers between devices  62.2 us (23%)
  Pallas kernels  59.1 us (22%)
  blocking collectives  31.7 us (12%)
  local copies, waits for them, and re-layouts  4.08 us (2%)
    ppermute x14, waiting for transfers between devices, swap(): lax.ppermute(blocks[k], ENS, [(e, e ^ k) for e in range(8)])  97.7 us
    ppermute x14, starting transfers between devices, swap(): lax.ppermute(blocks[k], ENS, [(e, e ^ k) for e in range(8)])  38.4 us
    all_to_all x1, blocking collectives, exchange(): return lax.all_to_all(x, axes, split_axis=0, concat_axis=0, tiled=True)  31.7 us
    all_to_all x2, starting transfers between devices, exchange(): return lax.all_to_all(x, axes, split_axis=0, concat_axis=0, tiled=True)  23.6 us
    pallas_call x1, Pallas kernels, spectra(): pl.pallas_call(spectra_kernel, out_shape=[jax.ShapeDtypeStruct((JJ, L, WI...  14.5 us
    pallas_call x1, Pallas kernels, gradient(): pl.pallas_call(gradient_kernel, out_shape=[jax.ShapeDtypeStruct((16, 8, 1...  14.4 us
    pallas_call x1, Pallas kernels, weights(): pl.pallas_call(weight_kernel, out_shape=jax.ShapeDtypeStruct((2, 8, 3, 20...  11.6 us
    pallas_call x1, Pallas kernels, prepare(): pl.pallas_call(prepare_kernel, out_shape=[jax.ShapeDtypeStruct((2, 2, L,...  6.92 us
  transfers between devices with their start and end apart: 18, of which 10 were waited for; matrix products, arithmetic and copies ran while one was open for 2% of the time, Pallas kernels for 8%

profile of v8, /device:TPU:8, one launch (start us, length us, event | category | flops | bytes accessed | tf_op | source)
XLA Modules:
  0.0 262.8 jit_solution(15707454678997599327)
XLA Ops:
  0.6 0.0 copy-start
  0.6 4.9 %pack.1 = bf16[16,8,104,128]{3,2,1,0:T(8,128)(2,1)} custom-call(bf16[20,640,128]{2,1,0:T(8,128)(2,1)} %bitcast.50, bf16[64,64]{1,0:T(8,128)(2,1)} %constant.45.clone.whole_ref, bf16[2,96,160]{2,1,0:T(8,128)(2,1)} %constant.46.clone.half_ref), custom_call_target="tpu_custom_call" | custom-call | tf_op jit(solution)/shard_map/pack/pallas_call | solution.py:214
  5.5 0.0 copy-start.8
  5.6 15.9 %all-to-all-start = ((bf16[128,52,2,128]{3,2,1,0:T(2,128)(2,1)}), bf16[128,52,2,128]{3,2,1,0:T(2,128)(2,1)}, u32[]{:S(2)}, u32[]{:S(2)}) async-start(bf16[128,52,2,128]{3,2,1,0:T(2,128)(2,1)} %bitcast.47), calls=%async_computation | async-start | bytes 6815744 | tf_op jit(solution)/shard_map/all_to_all | solution.py:797
  21.5 0.7 copy.20.band_ref
  22.1 0.6 pad_add_fusion.place_ref
  22.8 1.9 target_blocks.1
  24.6 2.8 %collective-permute-start = (bf16[40,384]{1,0:T(8,128)(2,1)}, bf16[40,384]{1,0:T(8,128)(2,1)S(1)}, u32[]{:S(2)}, u32[]{:S(2)}) collective-permute-start(bf16[40,384]{1,0:T(8,128)(2,1)} %get-tuple-element.50), channel_id=1, source_target_pairs={{0,3},{1,2},{2,1},{3,0},{4,7},{5,6},{6,5},{7,4},{8,11},{9,10},{10,... | collective-permute-start | bytes 92168 | tf_op jit(solution)/shard_map/ppermute | solution.py:801
  27.4 5.4 %collective-permute-start.3 = (bf16[40,384]{1,0:T(8,128)(2,1)}, bf16[40,384]{1,0:T(8,128)(2,1)S(1)}, u32[]{:S(2)}, u32[]{:S(2)}) collective-permute-start(bf16[40,384]{1,0:T(8,128)(2,1)} %get-tuple-element.55), channel_id=1, source_target_pairs={{0,4},{1,5},{2,6},{3,7},{4,0},{5,1},{6,2},{7,3},{8,12},{9,13},{10,... | collective-permute-start | bytes 92168 | tf_op jit(solution)/shard_map/ppermute | solution.py:801
  32.8 0.2 collective-permute-start.4
  33.0 6.6 %collective-permute-start.5 = (bf16[40,384]{1,0:T(8,128)(2,1)}, bf16[40,384]{1,0:T(8,128)(2,1)S(1)}, u32[]{:S(2)}, u32[]{:S(2)}) collective-permute-start(bf16[40,384]{1,0:T(8,128)(2,1)} %get-tuple-element.57), channel_id=1, source_target_pairs={{0,6},{1,7},{2,4},{3,5},{4,2},{5,3},{6,0},{7,1},{8,14},{9,15},{10,... | collective-permute-start | bytes 92168 | tf_op jit(solution)/shard_map/ppermute | solution.py:801
  39.6 2.7 %collective-permute-start.6 = (bf16[40,384]{1,0:T(8,128)(2,1)}, bf16[40,384]{1,0:T(8,128)(2,1)S(1)}, u32[]{:S(2)}, u32[]{:S(2)}) collective-permute-start(bf16[40,384]{1,0:T(8,128)(2,1)} %get-tuple-element.58), channel_id=1, source_target_pairs={{0,7},{1,6},{2,5},{3,4},{4,3},{5,2},{6,1},{7,0},{8,15},{9,14},{10,... | collective-permute-start | bytes 92168 | tf_op jit(solution)/shard_map/ppermute | solution.py:801
  42.3 0.1 reshape.43
  42.4 5.7 %collective-permute-done.1.refs_2_ = bf16[40,384]{1,0:T(8,128)(2,1)S(1)} collective-permute-done((bf16[40,384]{1,0:T(8,128)(2,1)}, bf16[40,384]{1,0:T(8,128)(2,1)S(1)}, u32[]{:S(2)}, u32[]{:S(2)}) %collective-permute-start.1) | collective-permute-done | bytes 30752 | tf_op jit(solution)/shard_map/ppermute | solution.py:801
  48.1 0.1 pad_add_fusion.1
  48.2 0.7 broadcast_in_dim.17.cotangent_ref
  48.9 0.7 broadcast_in_dim.19.other_column_ref.other_ref
  49.6 6.9 %prepare.1 = (bf16[2,2,320,640]{3,2,1,0:T(8,128)(2,1)}, bf16[2,2,320,384]{3,2,1,0:T(8,128)(2,1)}, bf16[2,640,704]{2,1,0:T(8,128)(2,1)}, bf16[2,384,704]{2,1,0:T(8,128)(2,1)}, bf16[128,2048]{1,0:T(8,128)(2,1)}) custom-call(s32[3]{0:T(128)} %pad_add_fusion.place_ref, bf16[20,320,320]{2,1,0:T(8,128)(2,1)} %bitcast.48, ...), custom_call_target="tpu_custom_call" | custom-call | tf_op jit(solution)/shard_map/prepare/pallas_call | solution.py:356
  56.5 43.1 %collective-permute-done.3.refs_4_ = bf16[40,384]{1,0:T(8,128)(2,1)S(1)} collective-permute-done((bf16[40,384]{1,0:T(8,128)(2,1)}, bf16[40,384]{1,0:T(8,128)(2,1)S(1)}, u32[]{:S(2)}, u32[]{:S(2)}) %collective-permute-start.3) | collective-permute-done | bytes 30752 | tf_op jit(solution)/shard_map/ppermute | solution.py:801
  99.7 0.9 collective-permute-done.4.refs_5_
  100.5 3.1 %collective-permute-done.5.refs_6_ = bf16[40,384]{1,0:T(8,128)(2,1)S(1)} collective-permute-done((bf16[40,384]{1,0:T(8,128)(2,1)}, bf16[40,384]{1,0:T(8,128)(2,1)S(1)}, u32[]{:S(2)}, u32[]{:S(2)}) %collective-permute-start.5) | collective-permute-done | bytes 30752 | tf_op jit(solution)/shard_map/ppermute | solution.py:801
  103.6 1.4 all-to-all-done
  105.0 14.5 %spectra.1 = (bf16[17,320,384]{2,1,0:T(8,128)(2,1)}, bf16[320,384]{1,0:T(8,128)(2,1)}, f32[32,40,128]{2,1,0:T(8,128)}) custom-call(s32[3]{0:T(128)} %pad_add_fusion.place_ref, bf16[16,8,104,128]{3,2,1,0:T(8,128)(2,1)} %bitcast.8.rows_hbm.rows_ref, bf16[2,2,320,640]{3,2,1,0:T(8,128)(2,1)} %get-tuple-element.44.to_full_hbm, ...), custom_call_target="tpu_custom_call" | custom-call | flops 10000000000 | bytes 12000000 | tf_op jit(solution)/shard_map/spectra/pallas_call | solution.py:547
  119.5 31.7 %all_to_all.15 = f32[128,5,2,128]{3,2,1,0:T(2,128)} all-to-all(f32[128,5,2,128]{3,2,1,0:T(2,128)} %bitcast.51), channel_id=1, replica_groups=mesh['dp'=2,'order_0'=4,'order_1'=4,'ens_0'=2,'ens_1'=4] {'order_0','ord..., dimensions={0} | all-to-all | bytes 1310720 | tf_op jit(solution)/shard_map/all_to_all | solution.py:797
  151.2 14.4 %gradient.1 = (bf16[16,8,104,128]{3,2,1,0:T(8,128)(2,1)}, bf16[16,320,384]{2,1,0:T(8,128)(2,1)}, f32[16,128]{1,0:T(8,128)}) custom-call(bf16[17,320,384]{2,1,0:T(8,128)(2,1)} %get-tuple-element.59.stacked_hbm, bf16[320,384]{1,0:T(8,128)(2,1)} %get-tuple-element.60.target_hbm, f32[32,40,128]{2,1,0:T(8,128)} %bitcast.52, ...), custom_call_target="tpu_custom_call" | custom-call | flops 10000000000 | bytes 12000000 | tf_op jit(solution)/shard_map/gradient/pallas_call | solution.py:703
  165.7 7.7 %all-to-all-start.2 = ((bf16[128,52,2,128]{3,2,1,0:T(2,128)(2,1)}), bf16[128,52,2,128]{3,2,1,0:T(2,128)(2,1)}, u32[]{:S(2)}, u32[]{:S(2)}) async-start(bf16[128,52,2,128]{3,2,1,0:T(2,128)(2,1)} %bitcast.49), calls=%async_computation.2 | async-start | bytes 6815744 | tf_op jit(solution)/shard_map/all_to_all | solution.py:797
  173.4 0.0 copy-start.9
  173.4 11.6 %weights.1 = bf16[2,8,3,20,320]{4,3,2,1,0:T(8,128)(2,1)} custom-call(s32[3]{0:T(128)} %pad_add_fusion.place_ref, bf16[16,8,104,128]{3,2,1,0:T(8,128)(2,1)} %bitcast.8.rows_hbm.rows_ref, bf16[16,320,384]{2,1,0:T(8,128)(2,1)} %get-tuple-element.67.grad_ref, bf16[320,640]{1,0:T(8,128)(2,1)} %constant.43.clone.full_ref, bf16[2,320,384]{2,1,0:T(8,128)(2,1)} %constant.44.clone.half_ref), custom_call_target="tpu_custom_call" | custom-call | flops 5000000000 | bytes 8000000 | tf_op jit(solution)/shard_map/weights/pallas_call | solution.py:779
  185.0 1.1 slice_bitcast_fusion
  186.1 0.1 collective-permute-start.7
  186.2 1.8 collective-permute-done.7
  187.9 1.1 fusion
  189.1 0.7 slice_bitcast_fusion.2
  189.8 2.7 %collective-permute-start.8 = (bf16[3,20,320]{2,1,0:T(8,128)(2,1)S(1)}, bf16[3,20,320]{2,1,0:T(8,128)(2,1)S(1)}, u32[]{:S(2)}, u32[]{:S(2)}) collective-permute-start(bf16[3,20,320]{2,1,0:T(8,128)(2,1)S(1)} %get-tuple-element.79), channel_id=1, source_target_pairs={{0,3},{1,2},{2,1},{3,0},{4,7},{5,6},{6,5},{7,4},{8,11},{9,10},{10,... | collective-permute-start | bytes 115208 | tf_op jit(solution)/shard_map/ppermute | solution.py:801
  192.4 3.3 %collective-permute-done.8.refs_3_ = bf16[3,20,320]{2,1,0:T(8,128)(2,1)S(1)} collective-permute-done((bf16[3,20,320]{2,1,0:T(8,128)(2,1)S(1)}, bf16[3,20,320]{2,1,0:T(8,128)(2,1)S(1)}, u32[]{:S(2)}, u32[]{:S(2)}) %collective-permute-start.8) | collective-permute-done | bytes 38432 | tf_op jit(solution)/shard_map/ppermute | solution.py:801
  195.7 1.2 collective-permute-start.9
  196.9 0.1 slice_reduce_fusion
  197.0 0.1 collective-permute-start.15
  197.1 6.3 %collective-permute-start.14 = (bf16[3,20,320]{2,1,0:T(8,128)(2,1)S(1)}, bf16[3,20,320]{2,1,0:T(8,128)(2,1)S(1)}, u32[]{:S(2)}, u32[]{:S(2)}) collective-permute-start(bf16[3,20,320]{2,1,0:T(8,128)(2,1)S(1)} %get-tuple-element.75), channel_id=1, source_target_pairs={{0,7},{1,6},{2,5},{3,4},{4,3},{5,2},{6,1},{7,0},{8,15},{9,14},{10,... | collective-permute-start | bytes 115208 | tf_op jit(solution)/shard_map/ppermute | solution.py:801
  203.5 3.1 %collective-permute-start.13 = (bf16[3,20,320]{2,1,0:T(8,128)(2,1)S(1)}, bf16[3,20,320]{2,1,0:T(8,128)(2,1)S(1)}, u32[]{:S(2)}, u32[]{:S(2)}) collective-permute-start(bf16[3,20,320]{2,1,0:T(8,128)(2,1)S(1)} %get-tuple-element.76), channel_id=1, source_target_pairs={{0,6},{1,7},{2,4},{3,5},{4,2},{5,3},{6,0},{7,1},{8,14},{9,15},{10,... | collective-permute-start | bytes 115208 | tf_op jit(solution)/shard_map/ppermute | solution.py:801
  206.6 4.9 %collective-permute-start.12 = (bf16[3,20,320]{2,1,0:T(8,128)(2,1)S(1)}, bf16[3,20,320]{2,1,0:T(8,128)(2,1)S(1)}, u32[]{:S(2)}, u32[]{:S(2)}) collective-permute-start(bf16[3,20,320]{2,1,0:T(8,128)(2,1)S(1)} %get-tuple-element.77), channel_id=1, source_target_pairs={{0,5},{1,4},{2,7},{3,6},{4,1},{5,0},{6,3},{7,2},{8,13},{9,12},{10,... | collective-permute-start | bytes 115208 | tf_op jit(solution)/shard_map/ppermute | solution.py:801
  211.5 0.2 collective-permute-start.11
  211.7 2.4 collective-permute-start.10
  214.0 0.5 add.19
  214.5 39.1 %collective-permute-done.14.refs_7_ = bf16[3,20,320]{2,1,0:T(8,128)(2,1)S(1)} collective-permute-done((bf16[3,20,320]{2,1,0:T(8,128)(2,1)S(1)}, bf16[3,20,320]{2,1,0:T(8,128)(2,1)S(1)}, u32[]{:S(2)}, u32[]{:S(2)}) %collective-permute-start.14) | collective-permute-done | bytes 38432 | tf_op jit(solution)/shard_map/ppermute | solution.py:801
  253.6 2.5 collective-permute-done.13.refs_6_
  256.2 1.4 all-to-all-done.2
  257.6 5.0 %unpack.1 = (bf16[20,640,128]{2,1,0:T(8,128)(2,1)}, f32[20,20,320]{2,1,0:T(8,128)}) custom-call(s32[3]{0:T(128)} %pad_add_fusion.place_ref, bf16[16,8,104,128]{3,2,1,0:T(8,128)(2,1)} %bitcast.15.in_hbm, bf16[64,64]{1,0:T(8,128)(2,1)} %constant.48.clone.whole_ref, bf16[2,160,96]{2,1,0:T(8,128)(2,1)} %constant.49.clone.half_ref, ...), custom_call_target="tpu_custom_call" | custom-call | tf_op jit(solution)/shard_map/unpack/pallas_call | solution.py:226
  (46 shorter events, 0.1 us)
Async XLA Ops:
  0.6 41.6 %copy-start = (f32[2,16]{1,0:T(2,128)S(1)}, f32[2,16]{1,0:T(2,128)}, u32[]{:S(2)}) copy-start(f32[2,16]{1,0:T(2,128)} %param.18) | copy-start | bytes 388
  5.5 15.9 %copy-start.8 = (s32[40,20]{0,1:T(8,128)S(1)}, s32[40,20]{0,1:T(8,128)}, u32[]{:S(2)}) copy-start(s32[40,20]{0,1:T(8,128)} %param.16) | copy-start | bytes 9604
  5.5 36.8 %copy-start.10 = (s32[16,4]{0,1:T(4,128)S(1)}, s32[16,4]{0,1:T(4,128)}, u32[]{:S(2)}) copy-start(s32[16,4]{0,1:T(4,128)} %param.17) | copy-start | bytes 772
  5.6 99.4 %all-to-all-start = ((bf16[128,52,2,128]{3,2,1,0:T(2,128)(2,1)}), bf16[128,52,2,128]{3,2,1,0:T(2,128)(2,1)}, u32[]{:S(2)}, u32[]{:S(2)}) async-start(bf16[128,52,2,128]{3,2,1,0:T(2,128)(2,1)} %bitcast.47), calls=%async_computation | async-start | bytes 6815744 | tf_op jit(solution)/shard_map/all_to_all | solution.py:797
  24.6 17.6 %collective-permute-start = (bf16[40,384]{1,0:T(8,128)(2,1)}, bf16[40,384]{1,0:T(8,128)(2,1)S(1)}, u32[]{:S(2)}, u32[]{:S(2)}) collective-permute-start(bf16[40,384]{1,0:T(8,128)(2,1)} %get-tuple-element.50), channel_id=1, source_target_pairs={{0,3},{1,2},{2,1},{3,0},{4,7},{5,6},{6,5},{7,4},{8,11},{9,10},{10,... | collective-permute-start | bytes 92168 | tf_op jit(solution)/shard_map/ppermute | solution.py:801
  27.4 72.3 %collective-permute-start.3 = (bf16[40,384]{1,0:T(8,128)(2,1)}, bf16[40,384]{1,0:T(8,128)(2,1)S(1)}, u32[]{:S(2)}, u32[]{:S(2)}) collective-permute-start(bf16[40,384]{1,0:T(8,128)(2,1)} %get-tuple-element.55), channel_id=1, source_target_pairs={{0,4},{1,5},{2,6},{3,7},{4,0},{5,1},{6,2},{7,3},{8,12},{9,13},{10,... | collective-permute-start | bytes 92168 | tf_op jit(solution)/shard_map/ppermute | solution.py:801
  32.8 67.8 %collective-permute-start.4 = (bf16[40,384]{1,0:T(8,128)(2,1)}, bf16[40,384]{1,0:T(8,128)(2,1)S(1)}, u32[]{:S(2)}, u32[]{:S(2)}) collective-permute-start(bf16[40,384]{1,0:T(8,128)(2,1)} %get-tuple-element.56), channel_id=1, source_target_pairs={{0,5},{1,4},{2,7},{3,6},{4,1},{5,0},{6,3},{7,2},{8,13},{9,12},{10,... | collective-permute-start | bytes 92168 | tf_op jit(solution)/shard_map/ppermute | solution.py:801
  33.0 70.6 %collective-permute-start.5 = (bf16[40,384]{1,0:T(8,128)(2,1)}, bf16[40,384]{1,0:T(8,128)(2,1)S(1)}, u32[]{:S(2)}, u32[]{:S(2)}) collective-permute-start(bf16[40,384]{1,0:T(8,128)(2,1)} %get-tuple-element.57), channel_id=1, source_target_pairs={{0,6},{1,7},{2,4},{3,5},{4,2},{5,3},{6,0},{7,1},{8,14},{9,15},{10,... | collective-permute-start | bytes 92168 | tf_op jit(solution)/shard_map/ppermute | solution.py:801
  39.6 64.0 %collective-permute-start.6 = (bf16[40,384]{1,0:T(8,128)(2,1)}, bf16[40,384]{1,0:T(8,128)(2,1)S(1)}, u32[]{:S(2)}, u32[]{:S(2)}) collective-permute-start(bf16[40,384]{1,0:T(8,128)(2,1)} %get-tuple-element.58), channel_id=1, source_target_pairs={{0,7},{1,6},{2,5},{3,4},{4,3},{5,2},{6,1},{7,0},{8,15},{9,14},{10,... | collective-permute-start | bytes 92168 | tf_op jit(solution)/shard_map/ppermute | solution.py:801
  42.3 62.7 %copy-start.11 = (bf16[40,384]{1,0:T(8,128)(2,1)}, bf16[40,384]{1,0:T(8,128)(2,1)S(1)}, u32[]{:S(2)}) copy-start(bf16[40,384]{1,0:T(8,128)(2,1)S(1)} %collective-permute-done.refs_3_) | copy-start | bytes 92164
  42.3 5.8 %collective-permute-start.1 = (bf16[40,384]{1,0:T(8,128)(2,1)}, bf16[40,384]{1,0:T(8,128)(2,1)S(1)}, u32[]{:S(2)}, u32[]{:S(2)}) collective-permute-start(bf16[40,384]{1,0:T(8,128)(2,1)} %get-tuple-element.51), channel_id=1, source_target_pairs={{0,2},{1,3},{2,0},{3,1},{4,6},{5,7},{6,4},{7,5},{8,10},{9,11},{10,... | collective-permute-start | bytes 92168 | tf_op jit(solution)/shard_map/ppermute | solution.py:801
  48.1 56.9 %copy-start.16 = (bf16[40,384]{1,0:T(8,128)(2,1)}, bf16[40,384]{1,0:T(8,128)(2,1)S(1)}, u32[]{:S(2)}) copy-start(bf16[40,384]{1,0:T(8,128)(2,1)S(1)} %collective-permute-done.1.refs_2_) | copy-start | bytes 92164
  48.1 55.5 %collective-permute-start.2 = (bf16[40,384]{1,0:T(8,128)(2,1)}, bf16[40,384]{1,0:T(8,128)(2,1)S(1)}, u32[]{:S(2)}, u32[]{:S(2)}) collective-permute-start(bf16[40,384]{1,0:T(8,128)(2,1)} %get-tuple-element.52), channel_id=1, source_target_pairs={{0,1},{1,0},{2,3},{3,2},{4,5},{5,4},{6,7},{7,6},{8,9},{9,8},{10,11... | collective-permute-start | bytes 92168 | tf_op jit(solution)/shard_map/ppermute | solution.py:801
  99.7 5.3 %copy-start.12 = (bf16[40,384]{1,0:T(8,128)(2,1)}, bf16[40,384]{1,0:T(8,128)(2,1)S(1)}, u32[]{:S(2)}) copy-start(bf16[40,384]{1,0:T(8,128)(2,1)S(1)} %collective-permute-done.3.refs_4_) | copy-start | bytes 92164
  100.5 4.5 %copy-start.13 = (bf16[40,384]{1,0:T(8,128)(2,1)}, bf16[40,384]{1,0:T(8,128)(2,1)S(1)}, u32[]{:S(2)}) copy-start(bf16[40,384]{1,0:T(8,128)(2,1)S(1)} %collective-permute-done.4.refs_5_) | copy-start | bytes 92164
  103.6 1.4 copy-start.14
  103.6 1.4 copy-start.15
  103.6 1.4 copy-start.17
  165.7 91.9 %all-to-all-start.2 = ((bf16[128,52,2,128]{3,2,1,0:T(2,128)(2,1)}), bf16[128,52,2,128]{3,2,1,0:T(2,128)(2,1)}, u32[]{:S(2)}, u32[]{:S(2)}) async-start(bf16[128,52,2,128]{3,2,1,0:T(2,128)(2,1)} %bitcast.49), calls=%async_computation.2 | async-start | bytes 6815744 | tf_op jit(solution)/shard_map/all_to_all | solution.py:797
  173.4 23.6 %copy-start.9 = (f32[16,128]{1,0:T(8,128)S(1)}, f32[16,128]{1,0:T(8,128)}, u32[]{:S(2)}) copy-start(f32[16,128]{1,0:T(8,128)} %get-tuple-element.74) | copy-start | bytes 24580
  186.1 1.9 collective-permute-start.7
  189.8 6.0 %collective-permute-start.8 = (bf16[3,20,320]{2,1,0:T(8,128)(2,1)S(1)}, bf16[3,20,320]{2,1,0:T(8,128)(2,1)S(1)}, u32[]{:S(2)}, u32[]{:S(2)}) collective-permute-start(bf16[3,20,320]{2,1,0:T(8,128)(2,1)S(1)} %get-tuple-element.79), channel_id=1, source_target_pairs={{0,3},{1,2},{2,1},{3,0},{4,7},{5,6},{6,5},{7,4},{8,11},{9,10},{10,... | collective-permute-start | bytes 115208 | tf_op jit(solution)/shard_map/ppermute | solution.py:801
  195.7 61.8 %copy-start.1 = (bf16[3,20,320]{2,1,0:T(8,128)(2,1)}, bf16[3,20,320]{2,1,0:T(8,128)(2,1)S(1)}, u32[]{:S(2)}) copy-start(bf16[3,20,320]{2,1,0:T(8,128)(2,1)S(1)} %collective-permute-done.8.refs_3_) | copy-start | bytes 115204
  195.7 15.8 %collective-permute-start.9 = (bf16[3,20,320]{2,1,0:T(8,128)(2,1)S(1)}, bf16[3,20,320]{2,1,0:T(8,128)(2,1)S(1)}, u32[]{:S(2)}, u32[]{:S(2)}) collective-permute-start(bf16[3,20,320]{2,1,0:T(8,128)(2,1)S(1)} %get-tuple-element.68), channel_id=1, source_target_pairs={{0,2},{1,3},{2,0},{3,1},{4,6},{5,7},{6,4},{7,5},{8,10},{9,11},{10,... | collective-permute-start | bytes 115208 | tf_op jit(solution)/shard_map/ppermute | solution.py:801
  197.0 14.6 %collective-permute-start.15 = (f32[16]{0:T(128)S(1)}, f32[16]{0:T(128)S(1)}, u32[]{:S(2)}, u32[]{:S(2)}) collective-permute-start(f32[16]{0:T(128)S(1)} %slice_reduce_fusion), channel_id=1, source_target_pairs={{0,128},{128,0},{1,129},{129,1},{2,130},{130,2},{3,131},{131,3},{4... | collective-permute-start | bytes 200 | tf_op jit(solution)/shard_map/ppermute | solution.py:848
  197.1 56.5 %collective-permute-start.14 = (bf16[3,20,320]{2,1,0:T(8,128)(2,1)S(1)}, bf16[3,20,320]{2,1,0:T(8,128)(2,1)S(1)}, u32[]{:S(2)}, u32[]{:S(2)}) collective-permute-start(bf16[3,20,320]{2,1,0:T(8,128)(2,1)S(1)} %get-tuple-element.75), channel_id=1, source_target_pairs={{0,7},{1,6},{2,5},{3,4},{4,3},{5,2},{6,1},{7,0},{8,15},{9,14},{10,... | collective-permute-start | bytes 115208 | tf_op jit(solution)/shard_map/ppermute | solution.py:801
  203.5 52.6 %collective-permute-start.13 = (bf16[3,20,320]{2,1,0:T(8,128)(2,1)S(1)}, bf16[3,20,320]{2,1,0:T(8,128)(2,1)S(1)}, u32[]{:S(2)}, u32[]{:S(2)}) collective-permute-start(bf16[3,20,320]{2,1,0:T(8,128)(2,1)S(1)} %get-tuple-element.76), channel_id=1, source_target_pairs={{0,6},{1,7},{2,4},{3,5},{4,2},{5,3},{6,0},{7,1},{8,14},{9,15},{10,... | collective-permute-start | bytes 115208 | tf_op jit(solution)/shard_map/ppermute | solution.py:801
  206.6 49.5 %collective-permute-start.12 = (bf16[3,20,320]{2,1,0:T(8,128)(2,1)S(1)}, bf16[3,20,320]{2,1,0:T(8,128)(2,1)S(1)}, u32[]{:S(2)}, u32[]{:S(2)}) collective-permute-start(bf16[3,20,320]{2,1,0:T(8,128)(2,1)S(1)} %get-tuple-element.77), channel_id=1, source_target_pairs={{0,5},{1,4},{2,7},{3,6},{4,1},{5,0},{6,3},{7,2},{8,13},{9,12},{10,... | collective-permute-start | bytes 115208 | tf_op jit(solution)/shard_map/ppermute | solution.py:801
  211.5 46.1 %copy-start.2 = (bf16[3,20,320]{2,1,0:T(8,128)(2,1)}, bf16[3,20,320]{2,1,0:T(8,128)(2,1)S(1)}, u32[]{:S(2)}) copy-start(bf16[3,20,320]{2,1,0:T(8,128)(2,1)S(1)} %collective-permute-done.9.refs_2_) | copy-start | bytes 115204
  211.5 44.6 %collective-permute-start.11 = (bf16[3,20,320]{2,1,0:T(8,128)(2,1)S(1)}, bf16[3,20,320]{2,1,0:T(8,128)(2,1)S(1)}, u32[]{:S(2)}, u32[]{:S(2)}) collective-permute-start(bf16[3,20,320]{2,1,0:T(8,128)(2,1)S(1)} %get-tuple-element.78), channel_id=1, source_target_pairs={{0,4},{1,5},{2,6},{3,7},{4,0},{5,1},{6,2},{7,3},{8,12},{9,13},{10,... | collective-permute-start | bytes 115208 | tf_op jit(solution)/shard_map/ppermute | solution.py:801
  211.7 44.5 %collective-permute-start.10 = (bf16[3,20,320]{2,1,0:T(8,128)(2,1)S(1)}, bf16[3,20,320]{2,1,0:T(8,128)(2,1)S(1)}, u32[]{:S(2)}, u32[]{:S(2)}) collective-permute-start(bf16[3,20,320]{2,1,0:T(8,128)(2,1)S(1)} %get-tuple-element.69), channel_id=1, source_target_pairs={{0,1},{1,0},{2,3},{3,2},{4,5},{5,4},{6,7},{7,6},{8,9},{9,8},{10,11... | collective-permute-start | bytes 115208 | tf_op jit(solution)/shard_map/ppermute | solution.py:801
  253.6 3.9 %copy-start.3 = (bf16[3,20,320]{2,1,0:T(8,128)(2,1)}, bf16[3,20,320]{2,1,0:T(8,128)(2,1)S(1)}, u32[]{:S(2)}) copy-start(bf16[3,20,320]{2,1,0:T(8,128)(2,1)S(1)} %collective-permute-done.14.refs_7_) | copy-start | bytes 115204
  256.1 1.4 copy-start.4
  256.1 1.4 copy-start.5
  256.1 1.4 copy-start.6
  256.2 1.4 copy-start.7
